TPU v7x, 128 devices: a whole 4x4x4 slice. The times are simulated.
128 devices in a mesh: row: 8 (over x, z_hi), col: 16 (over y, z_lo, core).
Axes of the slice: x: 4, y: 4, z: 4 (z_hi: 2, z_lo: 2; z = z_hi * 2 + z_lo), core: 2. Of those that a mesh axis runs over, the one named last changes fastest.
Arguments:
- points: float32 [8, 131072], P(None, ('row', 'col')), may hold values from -4 to 4
- point_order: int32 [128, 1024], P(('row', 'col')), may hold values from 0 to 1023, each once within a row
- noise_var: float32 [131072], P(('row', 'col')), may hold values from 0.1 to 3
- inv_scale: float32 [8], replicated, may hold values from 0.2 to 0.6
- basis_vectors: float32 [16, 64, 131072], P(None, None, ('row', 'col')), may hold values from -4 to 4
- current: float32 [64, 131072], P(None, ('row', 'col')), may hold values from -22 to 22
- tile_rows: int32 [8, 16, 64], P('row', 'col'), may hold values from 0 to 63, as said below
- tile_cols: int32 [8, 16, 64], P('row', 'col'), may hold values from 0 to 31
Outputs:
- lanczos_next: float32 [64, 131072], P(None, ('row', 'col'))
- coefficients: float32 [4, 64], replicated
- gradient_product: float32 [64, 131072], P(None, ('row', 'col'))
Inputs may be any that keep to these rules, and one draw needn't show every extreme that they name: In each grid cell the 64 pairs (tile_rows, tile_cols) are distinct; each cell lists its 4 pairs with I = J; over all cells no unordered pair of distinct blocks is listed twice: it is listed as (I, J) with I < J when I + J is odd and with I > J when I + J is even.
All inputs are finite; a program needn't handle non-finite values.
Results may differ from a plain program's by a relative error of at most 0.00019.
Values sent between devices are 32-bit elements; how exact they have to be, the bound alone decides.
No kernel may reach another device: no remote copies, remote signals or barrier semaphores. Data moves between devices by JAX's collectives and lax.ppermute only.
A program may use at most 128 MiB of HBM per device.

v0:
```python
import functools
import math

import jax
import jax.numpy as jnp
from jax import lax
from jax.experimental import pallas as pl
from jax.experimental.pallas import tpu as pltpu
from jax.sharding import PartitionSpec as P


BLOCK = 256
GROUP = 4

ROOT_THREE = math.sqrt(3.0)
SUPPORT = 3.0
EPSILON = 1e-06
F32 = jnp.float32
BF16 = jnp.bfloat16


def shift_y(v, s):
    return lax.ppermute(v, "col", [(i, (i + 4 * s) % 16) for i in range(16)])


def shift_x(v, s):
    return lax.ppermute(v, "row", [(i, (i + 2 * s) % 8) for i in range(8)])


def flip_core(v):
    return lax.ppermute(v, "col", [(i, i ^ 1) for i in range(16)])


def flip_z_lo(v):
    return lax.ppermute(v, "col", [(i, i ^ 2) for i in range(16)])


def flip_z_hi(v):
    return lax.ppermute(v, "row", [(i, i ^ 1) for i in range(8)])


def sum_everywhere(v):
    for axis, size, bits in (("col", 16, (1, 2, 4, 8)), ("row", 8, (1, 2, 4))):
        for bit in bits:
            v = v + lax.ppermute(v, axis, [(i, i ^ bit) for i in range(size)])
    return v


def gather_points(v):
    rows, cols = v[None], v[None]
    for row_bit, col_bit in ((2, 1), (4, 2), (8, 4), (1, None)):
        more = lax.ppermute(rows, "col", [(i, i ^ row_bit) for i in range(16)])
        rows = jnp.concatenate([rows, more])
        if col_bit is not None:
            more = lax.ppermute(cols, "row", [(i, i ^ col_bit) for i in range(8)])
            cols = jnp.concatenate([cols, more])
    return rows, cols


def gather_row_group(v):
    pair = jnp.stack([v, flip_z_hi(v)])
    return [pair] + [shift_x(pair, s) for s in (1, 2, 3)]


def gather_col_group(v):
    pair = jnp.stack([v, flip_z_lo(v)])
    own = [pair] + [shift_y(pair, s) for s in (1, 2, 3)]
    return own + [flip_core(v) for v in own]


def split_three(v):
    high = v.astype(BF16).astype(F32)
    rest = v - high
    middle = rest.astype(BF16).astype(F32)
    return high, middle, rest - middle


def split_two(v):
    scaled = v * 65537.0
    high = scaled - (scaled - v)
    return high, v - high


def tile_kernel(row_at, col_at, row_points, col_points, scale, kern, slope, left, right):
    @pl.when(pl.program_id(0) == 0)
    def _():
        def features(points, is_left):
            scaled = points * scale[...]
            size = scaled.shape[1]
            norm = split_three(jnp.sum(scaled * scaled, axis=0, keepdims=True))
            one = jnp.ones((1, size), F32)
            none = jnp.zeros((2, size), F32)
            if is_left:
                high, middle, low = split_three(scaled)
                parts = [high, high, middle, middle, high, low, *norm, one, one, one]
            else:
                high, middle, low = split_three(-2.0 * scaled)
                parts = [high, middle, high, middle, low, high, one, one, one, *norm]
            parts += [none, jnp.zeros((8, size), F32)]
            return jnp.concatenate(parts, axis=0).astype(BF16)

        width = row_points.shape[2]
        for held, points in ((left, row_points), (right, col_points)):
            for k in range(points.shape[0]):
                held[:, pl.ds(k * width, width)] = features(points[k], held is left)

    base = pl.program_id(0) * GROUP
    for g in range(GROUP):
        row_lane = pl.multiple_of(row_at[base + g], BLOCK)
        col_lane = pl.multiple_of(col_at[base + g], BLOCK)
        dist_sq = lax.dot_general(
            left[:, pl.ds(row_lane, BLOCK)],
            right[:, pl.ds(col_lane, BLOCK)],
            (((0,), (0,)), ((), ())),
            preferred_element_type=F32,
        )
        shifted = jnp.maximum(dist_sq, 0.0) + EPSILON
        radius = shifted * lax.rsqrt(shifted)
        decaying = jnp.exp2(radius * (-ROOT_THREE / math.log(2.0)))
        tapered = jnp.maximum(1.0 - radius * (1.0 / SUPPORT), 0.0)
        common = decaying * (tapered * tapered * tapered)
        weight = tapered * (3.0 + (12.0 / SUPPORT) * radius)
        growing = (1.0 / 3.0) + (ROOT_THREE / 3.0) * radius
        kernel_tile = common * weight * growing
        slope_tile = shifted * common * (weight + (60.0 / (SUPPORT * SUPPORT)) * growing)
        for out, tile in ((kern, kernel_tile), (slope, slope_tile)):
            high, low = split_two(tile)
            out[g, 0] = high.astype(BF16)
            out[g, 1] = low.astype(BF16)


def make_tiles(row_at, col_at, row_points, col_points, scale):
    tiles = row_at.shape[0]
    whole = lambda v: pl.BlockSpec(v.shape, lambda i, *_: (0,) * v.ndim)
    out_spec = pl.BlockSpec((GROUP, 2, BLOCK, BLOCK), lambda i, *_: (i, 0, 0, 0))
    out = jax.ShapeDtypeStruct((tiles, 2, BLOCK, BLOCK), BF16)
    return pl.pallas_call(
        tile_kernel,
        out_shape=(out, out),
        grid_spec=pltpu.PrefetchScalarGridSpec(
            num_scalar_prefetch=2,
            grid=(tiles // GROUP,),
            in_specs=[whole(row_points), whole(col_points), whole(scale)],
            out_specs=(out_spec, out_spec),
            scratch_shapes=[
                pltpu.VMEM((64, row_points.shape[0] * 1024), BF16),
                pltpu.VMEM((64, col_points.shape[0] * 1024), BF16),
            ],
        ),
        compiler_params=pltpu.CompilerParams(vmem_limit_bytes=48 << 20),
        cost_estimate=pl.CostEstimate(
            flops=tiles * 30 * BLOCK * BLOCK,
            bytes_accessed=tiles * 8 * BLOCK * BLOCK,
            transcendentals=tiles * 2 * BLOCK * BLOCK,
        ),
        name="make_tiles",
    )(row_at, col_at, row_points, col_points, scale)


def product_kernel(row_count, col_count, flat, index, tiles, *refs):
    row_in, refs = refs[:row_count], refs[row_count:]
    col_in, refs = refs[:col_count], refs[col_count:]
    outs, refs = refs[: 3 if flat else 6], refs[3 if flat else 6 :]
    tiles_here, row_held, col_held, row_total, col_total, arrived, left = refs

    def fetch(step):
        some = pl.ds(step * GROUP, GROUP)
        return pltpu.make_async_copy(tiles.at[some], tiles_here.at[some], arrived.at[step])

    steps = tiles.shape[0] // GROUP

    @pl.loop(0, steps)
    def _(step):
        fetch(step).start()

    def hold(held, arrays):
        slot = 0
        for array in arrays:
            if len(array.shape) == 3:
                pieces = [array.at[k] for k in range(array.shape[0])]
            else:
                pieces = [array.at[:, pl.ds(k * 1024, 1024)] for k in range(array.shape[1] // 1024)]
            for piece in pieces:
                value = piece[...]
                high = value.astype(BF16)
                held[slot, 0:64] = high
                held[slot, 64:128] = (value - high.astype(F32)).astype(BF16)
                slot += 1

    hold(row_held, row_in)
    hold(col_held, col_in)
    row_total[...] = jnp.zeros_like(row_total)
    col_total[...] = jnp.zeros_like(col_total)

    def times(values, tile_high, tile_low, contract):
        dims = (((1,), (contract,)), ((), ()))
        both = lax.dot_general(values, tile_high, dims, preferred_element_type=F32)
        low = lax.dot_general(values[:64], tile_low, dims, preferred_element_type=F32)
        return both[:64] + both[64:] + low

    @pl.loop(0, steps)
    def _(step):
        fetch(step).wait()
        for g in range(GROUP):
            t = step * GROUP + g
            row_lane = pl.ds(pl.multiple_of(index[4, t], BLOCK), BLOCK)
            col_lane = pl.ds(pl.multiple_of(index[5, t], BLOCK), BLOCK)
            mirror = index[6, t].astype(F32)
            high, low = tiles_here[t, 0], tiles_here[t, 1]
            direct = times(col_held[index[1, t], :, col_lane], high, low, 1)
            mirrored = times(row_held[index[0, t], :, row_lane], high, low, 0)
            row_total[index[2, t], :, row_lane] += direct
            col_total[index[3, t], :, col_lane] += mirrored * mirror

    if flat:
        slots = [row_total.at[k] for k in range(16)] + [col_total.at[k] for k in range(8)]
        places = [out.at[:, pl.ds(k * 1024, 1024)] for out in outs for k in range(8)]
    else:
        slots = [row_total.at[pl.ds(k * 8, 8)] for k in (0, 1)]
        slots += [col_total.at[pl.ds(k * 2, 2)] for k in range(4)]
        places = outs
    copies = [
        pltpu.make_async_copy(slot, place, left.at[k])
        for k, (slot, place) in enumerate(zip(slots, places))
    ]
    for copy in copies:
        copy.start()
    for copy in copies:
        copy.wait()


def products(index, tiles, row_in, col_in, flat):
    count = tiles.shape[0]
    here = pl.BlockSpec(memory_space=pltpu.VMEM)
    if flat:
        outs = [jax.ShapeDtypeStruct((64, 8 * 1024), F32)] * 3
    else:
        outs = [jax.ShapeDtypeStruct((8, 64, 1024), F32)] * 2
        outs += [jax.ShapeDtypeStruct((2, 64, 1024), F32)] * 4
    return pl.pallas_call(
        functools.partial(product_kernel, len(row_in), len(col_in), flat),
        out_shape=tuple(outs),
        in_specs=[pl.BlockSpec(memory_space=pltpu.SMEM), pl.BlockSpec(memory_space=pltpu.HBM)]
        + [here] * (len(row_in) + len(col_in)),
        out_specs=tuple(pl.BlockSpec(memory_space=pltpu.HBM) for _ in outs),
        scratch_shapes=[
            pltpu.VMEM(tiles.shape, BF16),
            pltpu.VMEM((16, 128, 1024), BF16),
            pltpu.VMEM((8, 128, 1024), BF16),
            pltpu.VMEM((16, 64, 1024), F32),
            pltpu.VMEM((8, 64, 1024), F32),
            pltpu.SemaphoreType.DMA((count // GROUP,)),
            pltpu.SemaphoreType.DMA((24,)),
        ],
        compiler_params=pltpu.CompilerParams(vmem_limit_bytes=60_200_000),
        cost_estimate=pl.CostEstimate(
            flops=count * 12 * 64 * BLOCK * BLOCK,
            bytes_accessed=count * 4 * BLOCK * BLOCK + (12 << 20),
            transcendentals=0,
        ),
        name="slope_products" if flat else "kernel_products",
    )(index, tiles, *row_in, *col_in)


def column_sums(pairs, columns):
    lane = lax.broadcasted_iota(jnp.int32, (8, columns), 1)
    held = jnp.zeros((8, columns), F32)
    for k, (a, b) in enumerate(pairs):
        held = jnp.where(lane == k, jnp.sum(a * b, axis=1, keepdims=True), held)
    return held


def row_blocks_of(rows):
    return lambda body: pl.loop(0, rows // 8)(
        lambda step: body(pl.ds(pl.multiple_of(step * 8, 8), 8))
    )


def vectors_at(earlier, extra, at):
    return [earlier[h, at] for h in range(earlier.shape[0])] + [v[at] for v in extra]


def dots_kernel(piece_count, extra_count, earlier, noise, *refs):
    pieces, refs = refs[:piece_count], refs[piece_count:]
    extra, (image_out, dots_out, held) = refs[:extra_count], refs[extra_count:]
    held[...] = jnp.zeros_like(held)

    @row_blocks_of(image_out.shape[0])
    def _(at):
        image = noise[...] * extra[-1][at]
        for piece in pieces:
            if len(piece.shape) == 3:
                image = image + piece[0, at]
            else:
                image = image + piece[at]
        image_out[at] = image
        vectors = vectors_at(earlier, extra, at) + [image]
        held[at] = column_sums([(v, image) for v in vectors], 128)

    dots_out[...] = held[...].T[: dots_out.shape[0]]


def image_dots(earlier, noise, pieces, extra):
    rows, lanes = extra[-1].shape
    return pl.pallas_call(
        functools.partial(dots_kernel, len(pieces), len(extra)),
        out_shape=(
            jax.ShapeDtypeStruct((rows, lanes), F32),
            jax.ShapeDtypeStruct((24, 128), F32),
        ),
        scratch_shapes=[pltpu.VMEM((128, 128), F32)],
        compiler_params=pltpu.CompilerParams(vmem_limit_bytes=2 << 20),
        cost_estimate=pl.CostEstimate(
            flops=rows * lanes * 60, bytes_accessed=rows * lanes * 4 * 30, transcendentals=0
        ),
        name="image_dots",
    )(earlier, noise, *pieces, *extra)


def gram_kernel(earlier, first, out, held):
    held[...] = jnp.zeros_like(held)

    @row_blocks_of(first.shape[0])
    def _(at):
        vectors = vectors_at(earlier, [first], at)
        count = len(vectors)
        pairs = [(vectors[i], vectors[i + d]) for d in range(count) for i in range(count - d)]
        held[at, 0:128] = column_sums(pairs[:128], 128)
        held[at, 128:256] = column_sums(pairs[128:], 128)

    out[0:128] = held[:, 0:128].T
    out[128:160] = held[:, 128:256].T[:32]


def gram_sums(earlier, first):
    rows, lanes = first.shape
    return pl.pallas_call(
        gram_kernel,
        out_shape=jax.ShapeDtypeStruct((160, 128), F32),
        scratch_shapes=[pltpu.VMEM((128, 256), F32)],
        compiler_params=pltpu.CompilerParams(vmem_limit_bytes=2 << 20),
        cost_estimate=pl.CostEstimate(
            flops=rows * lanes * 400, bytes_accessed=rows * lanes * 4 * 18, transcendentals=0
        ),
        name="gram_sums",
    )(earlier, first)


def turned(values):
    rows = values.shape[0]
    return jnp.concatenate([values, jnp.zeros((128 - rows, 128), F32)], axis=0).T


def combine(columns, image, vectors):
    total = columns[:, 0:1] * image
    for k, v in enumerate(vectors):
        total = total - columns[:, k + 1 : k + 2] * v
    return total


def first_rest_kernel(total, sums, image, earlier, first, rest, held):
    means = sums[0:17] * (1.0 / total)
    held[...] = turned(jnp.concatenate([jnp.ones((1, 128), F32), means], axis=0))

    @row_blocks_of(rest.shape[0])
    def _(at):
        rest[at] = combine(held[at], image[at], vectors_at(earlier, [first], at))


def last_rest_kernel(
    total, sums, next_sums, gram, image, earlier, first, second, out, coefficients, held
):
    count = 17
    means = sums[...] * (1.0 / total)
    along = means[0:count]
    turned_along = jnp.zeros((count, 128), F32)
    at = 0
    diagonals = []
    for d in range(count):
        size = count - d
        diagonal = gram[at : at + size] * (1.0 / total)
        diagonals.append(diagonal)
        part = diagonal * along[d:]
        if d:
            other = diagonal * along[:size]
            blank = jnp.zeros((d, 128), F32)
            part = jnp.concatenate([part, blank], axis=0) + jnp.concatenate([blank, other], axis=0)
        turned_along = turned_along + part
        at += size
    rest_means = along - turned_along
    column = lambda v: jnp.sum(v, axis=0, keepdims=True)
    norm = means[17:18] - 2.0 * column(along * along) + column(along * turned_along)
    norm = jnp.maximum(norm, 0.0)
    norm_sq = norm + EPSILON
    scale = 1.0 / jnp.sqrt(norm_sq)

    next_means = next_sums[...] * (1.0 / total)
    next_along = next_means[0:count] * scale
    alpha = next_means[17:18] * (scale * scale)
    beside = alpha * scale
    rest_sq = (
        next_means[18:19] * (scale * scale)
        - 2.0 * (column(next_along * next_along) + alpha * alpha)
        + 2.0 * beside * column(next_along * rest_means)
        + beside * beside * norm
    )
    for d in range(count):
        part = column(next_along[: count - d] * next_along[d:] * diagonals[d])
        rest_sq = rest_sq + (1.0 if d == 0 else 2.0) * part
    beta = jnp.sqrt(jnp.maximum(rest_sq, 0.0) + EPSILON)
    held[...] = turned(jnp.concatenate([scale, next_along, beside], axis=0) / beta)
    coefficients[...] = jnp.concatenate(
        [along[16:17], jnp.sqrt(norm_sq), alpha, beta, jnp.zeros((4, 128), F32)], axis=0
    )

    @row_blocks_of(out.shape[0])
    def _(at):
        out[at] = combine(held[at], image[at], vectors_at(earlier, [first, second], at))


def rest_call(kernel, total, smalls, image, earlier, extra, with_coefficients):
    rows, lanes = image.shape
    out_shape = [jax.ShapeDtypeStruct((rows, lanes), F32)]
    if with_coefficients:
        out_shape.append(jax.ShapeDtypeStruct((8, 128), F32))
    return pl.pallas_call(
        functools.partial(kernel, float(total)),
        out_shape=tuple(out_shape),
        scratch_shapes=[pltpu.VMEM((128, 128), F32)],
        compiler_params=pltpu.CompilerParams(vmem_limit_bytes=2 << 20),
        cost_estimate=pl.CostEstimate(
            flops=rows * lanes * 40, bytes_accessed=rows * lanes * 4 * 20, transcendentals=0
        ),
    )(*smalls, image, earlier, *extra)


def reduce_parts(parts):
    row_keep, row_send, cols = parts[0], parts[1], parts[2:]
    row_got = flip_core(row_send)
    col_got = []
    for s in (2, 1, 3):
        col_got.append(shift_x(cols[s], s))
    own = [row_keep[2 * s : 2 * s + 2] + row_got[2 * s : 2 * s + 2] for s in range(4)]
    row_got = []
    for s in (2, 1, 3):
        row_got.append(shift_y(own[s], s))
    col_sum = cols[0] + col_got[0] + col_got[1] + col_got[2]
    row_sum = own[0] + row_got[0] + row_got[1] + row_got[2]
    return [col_sum, row_sum, flip_z_hi(col_sum[1]), flip_z_lo(row_sum[1])]


def on_device(
    points, point_order, noise_var, inv_scale, basis_vectors, current, tile_rows, tile_cols
):
    per_device = points.shape[1]
    row_at = lax.axis_index("row")
    col_at = lax.axis_index("col")
    point_total = per_device * 128
    arrangement = point_order[0]
    arranged = jnp.take(points, arrangement, axis=1)
    noise_here = jnp.take(noise_var, arrangement)
    row_blocks = tile_rows[0, 0]
    col_blocks = tile_cols[0, 0]
    row_owner, row_sub = row_blocks // 4, row_blocks % 4
    col_owner, col_sub = col_blocks // 4, col_blocks % 4
    mirror = ((row_at * 16 + row_owner) * 4 + row_sub) != (
        (col_owner * 16 + col_at) * 4 + col_sub
    )
    core_rel = (row_owner ^ col_at) & 1
    zlo_rel = ((row_owner ^ col_at) >> 1) & 1
    y_to = (row_owner // 4 - col_at // 4) & 3
    zhi_rel = (col_owner ^ row_at) & 1
    x_to = (col_owner // 2 - row_at // 2) & 3
    row_from = core_rel * 8 + ((4 - y_to) & 3) * 2 + zlo_rel
    row_to = core_rel * 8 + y_to * 2 + zlo_rel
    col_from = ((4 - x_to) & 3) * 2 + zhi_rel
    col_to = x_to * 2 + zhi_rel

    def table(row_in, col_in, row_out, col_out):
        rows = [row_in, col_in, row_out, col_out, row_sub * BLOCK, col_sub * BLOCK, mirror]
        return jnp.stack([v.astype(jnp.int32) for v in rows])

    row_points, col_points = gather_points(arranged)
    row_xor, col_xor = row_owner ^ col_at, col_owner ^ row_at
    kern, slope = make_tiles(
        ((row_xor & 1) * 8 + (row_xor >> 1)) * 1024 + row_sub * BLOCK,
        col_xor * 1024 + col_sub * BLOCK,
        row_points,
        col_points,
        inv_scale[:, None],
    )

    noise = noise_here[None]
    row_in = [lax.all_gather(current, "col", axis=1, tiled=True)]
    kern, current_later = lax.optimization_barrier((kern, current))
    first_table = table(row_owner, col_from, row_to, col_to)
    gram, first_table = lax.optimization_barrier(
        (gram_sums(basis_vectors, current_later), first_table)
    )
    gram = lax.psum(gram, ("row", "col"))
    col_in = gather_row_group(current)
    parts = products(first_table, kern, row_in, col_in, False)
    pieces = reduce_parts(parts)
    slope_to = core_rel * 8 + (row_owner >> 1)
    row_keep, row_send, col_part = products(
        table(row_owner, col_from, slope_to, col_owner), slope, row_in, col_in, True
    )
    col_sum = lax.psum_scatter(col_part, "row", scatter_dimension=1, tiled=True)
    row_part = row_keep + flip_core(row_send)
    row_sum = lax.psum_scatter(
        row_part,
        "col",
        scatter_dimension=1,
        tiled=True,
        axis_index_groups=[[i * 2 + core for i in range(8)] for core in range(2)],
    )
    gradient_product = row_sum + col_sum
    image, sums = image_dots(basis_vectors, noise, pieces, [current])
    sums = sum_everywhere(sums)
    (rest,) = rest_call(
        first_rest_kernel, point_total, [sums], image, basis_vectors, [current], False
    )

    row_in = gather_col_group(rest)
    col_in = gather_row_group(rest)
    parts = products(table(row_from, col_from, row_to, col_to), kern, row_in, col_in, False)
    pieces = reduce_parts(parts)
    image, next_sums = image_dots(basis_vectors, noise, pieces, [current, rest])
    next_sums = sum_everywhere(next_sums)
    lanczos_next, rows = rest_call(
        last_rest_kernel,
        point_total,
        [sums, next_sums, gram],
        image,
        basis_vectors,
        [current, rest],
        True,
    )
    return (lanczos_next, rows[:4, :64], gradient_product)


def solution(mesh):
    return jax.shard_map(
        on_device,
        mesh=mesh,
        in_specs=(
            P(None, ("row", "col")),
            P(("row", "col"), None),
            P(("row", "col")),
            P(),
            P(None, None, ("row", "col")),
            P(None, ("row", "col")),
            P("row", "col", None),
            P("row", "col", None),
        ),
        out_specs=(P(None, ("row", "col")), P(), P(None, ("row", "col"))),
        check_vma=False,
    )
```

profile of v0, /device:TPU:1, one launch (start us, length us, event | category | flops | bytes accessed | tf_op | source)
XLA Modules:
  0.0 475.9 jit_solution(16069156787223054018)
XLA Ops:
  10.5 2.8 gather_fusion.1
  14.2 2.5 collective-permute-start
  16.7 3.3 collective-permute-start.4
  23.3 1.4 collective-permute-start.1
  25.9 2.4 collective-permute-done.1
  28.3 2.9 collective-permute-start.2
  31.2 2.7 collective-permute-start.6
  38.4 4.0 collective-permute-start.3
  43.7 24.8 %make_tiles.1 = (bf16[64,2,256,256]{3,2,1,0:T(8,128)(2,1)}, bf16[64,2,256,256]{3,2,1,0:T(8,128)(2,1)}) custom-call(s32[64]{0:T(128)S(1)} %get-tuple-element.82.row_at, s32[64]{0:T(128)S(1)} %get-tuple-element.83.col_at, f32[16,8,1024]{2,1,0:T(8,128)S(1)} %constant_dynamic-update-slice_fusion.row_points, f32[8,8,1024]{2,1,0:T(8,128)S(1)} %get-tuple-element.75.col_points, ...), custom_call_target="tpu_custom_call" | custom-call | flops 125829120 | bytes 33554432 | tf_op jit(solution)/shard_map/make_tiles/pallas_call | solution.py:137
  68.5 4.3 gram_sums.1
  73.9 16.8 %kernel_products.2 = (f32[8,64,1024]{2,1,0:T(8,128)}, f32[8,64,1024]{2,1,0:T(8,128)}, f32[2,64,1024]{2,1,0:T(8,128)}, f32[2,64,1024]{2,1,0:T(8,128)}, f32[2,64,1024]{2,1,0:T(8,128)}, /*index=5*/f32[2,64,1024]{2,1,0:T(8,128)}) custom-call(s32[7,64]{1,0:T(8,128)} %stack.22.index, bf16[64,2,256,256]{3,2,1,0:T(8,128)(2,1)} %get-tuple-element.33.tiles, ...), custom_call_target="tpu_custom_call" | custom-call | flops 3221225472 | bytes 29360128 | tf_op jit(solution)/shard_map/kernel_products/pallas_call | solution.py:240
  91.8 16.8 %slope_products.1 = (f32[64,8192]{1,0:T(8,128)}, f32[64,8192]{1,0:T(8,128)}, f32[64,8192]{1,0:T(8,128)}) custom-call(s32[7,64]{1,0:T(8,128)} %stack.32.index, bf16[64,2,256,256]{3,2,1,0:T(8,128)(2,1)} %get-tuple-element.53.tiles, f32[64,16384]{1,0:T(8,128)} %all-gather.2.cloned.1.call-done.refs_0_, f32[2,64,1024]{2,1,0:T(8,128)} %copy-done.9, ...), custom_call_target="tpu_custom_call" | custom-call | flops 3221225472 | bytes 29360128 | tf_op jit(solution)/shard_map/slope_products/pallas_call | solution.py:240
  108.6 2.8 collective-permute-start.11
  111.8 2.4 collective-permute-start.13
  115.2 1.7 slice_add_fusion.6
  116.9 1.6 collective-permute-start.15
  118.5 6.7 %collective-permute-done.11 = f32[2,64,1024]{2,1,0:T(8,128)S(1)} collective-permute-done((f32[2,64,1024]{2,1,0:T(8,128)}, f32[2,64,1024]{2,1,0:T(8,128)S(1)}, u32[]{:S(2)}, u32[]{:S(2)}) %collective-permute-start.11) | collective-permute-done | bytes 524320 | tf_op jit(solution)/shard_map/ppermute | solution.py:27
  125.8 15.8 %collective-permute-done.12 = f32[2,64,1024]{2,1,0:T(8,128)S(1)} collective-permute-done((f32[2,64,1024]{2,1,0:T(8,128)}, f32[2,64,1024]{2,1,0:T(8,128)S(1)}, u32[]{:S(2)}, u32[]{:S(2)}) %collective-permute-start.12) | collective-permute-done | bytes 524320 | tf_op jit(solution)/shard_map/ppermute | solution.py:27
  141.6 2.7 collective-permute-start.17
  144.5 2.0 collective-permute-start.18
  146.5 8.7 %collective-permute-done.17 = f32[2,64,1024]{2,1,0:T(8,128)S(1)} collective-permute-done((f32[2,64,1024]{2,1,0:T(8,128)S(1)}, f32[2,64,1024]{2,1,0:T(8,128)S(1)}, u32[]{:S(2)}, u32[]{:S(2)}) %collective-permute-start.17) | collective-permute-done | bytes 524320 | tf_op jit(solution)/shard_map/ppermute | solution.py:23
  155.2 1.5 fusion.5.refs_1_
  156.8 4.5 gather_fusion
  161.3 4.0 collective-permute-done.19.refs_3_
  165.4 2.2 copy-done.3
  168.6 1.6 collective-permute-start.20
  171.5 2.1 collective-permute-done.21
  173.8 2.4 collective-permute-done.22
  176.1 2.0 collective-permute-start.23
  178.2 2.5 collective-permute-done.23
  180.7 2.3 collective-permute-start.24
  183.0 1.7 collective-permute-done.24
  184.7 3.0 collective-permute-done.25
  188.7 3.2 collective-permute-done.26
  193.0 2.7 collective-permute-start.35
  195.7 2.5 collective-permute-done.27
  198.2 4.0 collective-permute-done.35
  203.1 2.7 collective-permute-start.29
  206.4 8.1 %collective-permute-start.31 = (f32[2,64,1024]{2,1,0:T(8,128)S(1)}, f32[2,64,1024]{2,1,0:T(8,128)S(1)}, u32[]{:S(2)}, u32[]{:S(2)}) collective-permute-start(f32[2,64,1024]{2,1,0:T(8,128)S(1)} %get-tuple-element.74.refs_0_), channel_id=1, source_target_pairs={{0,1},{1,0},{2,3},{3,2},{4,5},{5,4},{6,7},{7,6},{8,9},{9,8},{10,11... | collective-permute-start | bytes 1572872 | tf_op jit(solution)/shard_map/ppermute | solution.py:31
  215.8 5.4 %collective-permute-done.29.refs_2_ = f32[2,64,1024]{2,1,0:T(8,128)S(1)} collective-permute-done((f32[2,64,1024]{2,1,0:T(8,128)S(1)}, f32[2,64,1024]{2,1,0:T(8,128)S(1)}, u32[]{:S(2)}, u32[]{:S(2)}) %collective-permute-start.29) | collective-permute-done | bytes 524320 | tf_op jit(solution)/shard_map/ppermute | solution.py:23
  221.2 3.8 collective-permute-done.30.refs_3_
  225.0 8.0 %collective-permute-start.32 = (f32[2,64,1024]{2,1,0:T(8,128)S(1)}, f32[2,64,1024]{2,1,0:T(8,128)}, u32[]{:S(2)}, u32[]{:S(2)}) collective-permute-start(f32[2,64,1024]{2,1,0:T(8,128)S(1)} %collective-permute-done.28.refs_1_), channel_id=1, source_target_pairs={{0,1},{1,0},{2,3},{3,2},{4,5},{5,4},{6,7},{7,6},{8,9},{9,8},{10,11... | collective-permute-start | bytes 1572872 | tf_op jit(solution)/shard_map/ppermute | solution.py:31
  233.1 7.4 %collective-permute-done.36.refs_9_ = f32[2,64,1024]{2,1,0:T(8,128)S(1)} collective-permute-done((f32[2,64,1024]{2,1,0:T(8,128)S(1)}, f32[2,64,1024]{2,1,0:T(8,128)S(1)}, u32[]{:S(2)}, u32[]{:S(2)}) %collective-permute-start.36) | collective-permute-done | bytes 524320 | tf_op jit(solution)/shard_map/ppermute | solution.py:27
  241.4 3.1 add.432
  245.8 16.8 %kernel_products.3 = (f32[8,64,1024]{2,1,0:T(8,128)}, f32[8,64,1024]{2,1,0:T(8,128)}, f32[2,64,1024]{2,1,0:T(8,128)}, f32[2,64,1024]{2,1,0:T(8,128)}, f32[2,64,1024]{2,1,0:T(8,128)}, /*index=5*/f32[2,64,1024]{2,1,0:T(8,128)}) custom-call(s32[7,64]{1,0:T(8,128)} %stack.26.index, bf16[64,2,256,256]{3,2,1,0:T(8,128)(2,1)} %get-tuple-element.33.tiles, ...), custom_call_target="tpu_custom_call" | custom-call | flops 3221225472 | bytes 29360128 | tf_op jit(solution)/shard_map/kernel_products/pallas_call | solution.py:240
  264.0 2.7 collective-permute-start.41
  267.5 1.7 slice_add_fusion.2
  269.3 1.6 collective-permute-start.43
  270.9 7.6 %collective-permute-done.39 = f32[2,64,1024]{2,1,0:T(8,128)S(1)} collective-permute-done((f32[2,64,1024]{2,1,0:T(8,128)}, f32[2,64,1024]{2,1,0:T(8,128)S(1)}, u32[]{:S(2)}, u32[]{:S(2)}) %collective-permute-start.39) | collective-permute-done | bytes 524320 | tf_op jit(solution)/shard_map/ppermute | solution.py:27
  278.7 11.7 %collective-permute-done.40 = f32[2,64,1024]{2,1,0:T(8,128)S(1)} collective-permute-done((f32[2,64,1024]{2,1,0:T(8,128)}, f32[2,64,1024]{2,1,0:T(8,128)S(1)}, u32[]{:S(2)}, u32[]{:S(2)}) %collective-permute-start.40) | collective-permute-done | bytes 524320 | tf_op jit(solution)/shard_map/ppermute | solution.py:27
  291.3 4.7 collective-permute-done.44
  296.0 7.7 %collective-permute-done.45 = f32[2,64,1024]{2,1,0:T(8,128)S(1)} collective-permute-done((f32[2,64,1024]{2,1,0:T(8,128)S(1)}, f32[2,64,1024]{2,1,0:T(8,128)S(1)}, u32[]{:S(2)}, u32[]{:S(2)}) %collective-permute-start.45) | collective-permute-done | bytes 524320 | tf_op jit(solution)/shard_map/ppermute | solution.py:23
  306.3 6.0 %collective-permute-done.47.refs_3_ = f32[64,1024]{1,0:T(8,128)S(1)} collective-permute-done((f32[64,1024]{1,0:T(8,128)S(1)}, f32[64,1024]{1,0:T(8,128)S(1)}, u32[]{:S(2)}, u32[]{:S(2)}) %collective-permute-start.47) | collective-permute-done | bytes 262176 | tf_op jit(solution)/shard_map/ppermute | solution.py:35
  313.5 1.6 collective-permute-start.48
  318.4 1.7 collective-permute-start.50
  322.5 2.7 collective-permute-done.51
  325.3 1.6 collective-permute-start.52
  326.9 2.4 collective-permute-done.52
  329.4 2.4 collective-permute-done.53
  331.9 2.1 collective-permute-start.54
  334.0 1.8 add.433
  335.9 127.3 %all-reduce.2.cloned.1.call-done.gram = f32[160,128]{1,0:T(8,128)} async-done(((f32[160,128]{1,0:T(8,128)}), f32[160,128]{1,0:T(8,128)}) %all-reduce.2.cloned.1.call-update) | async-done | bytes 81936 | tf_op jit(solution)/shard_map/psum | solution.py:500
  463.2 2.2 copy-done.6
  466.3 1.8 shard_map.104
  (189 shorter events, 41.9 us)
Async XLA Ops:
  8.0 148.8 %copy-start = (f32[1024]{0:T(1024)S(1)}, f32[1024]{0:T(1024)}, u32[]{:S(2)}) copy-start(f32[1024]{0:T(1024)} %param.10) | copy-start | bytes 12292
  8.0 64.8 %all-gather.2.cloned.1.call-start = ((), (), s32[]{:S(2)}) async-start(), calls=%async_computation.2 | async-start | bytes 4456448 | tf_op jit(solution)/shard_map/all_gather | solution.py:494
  8.8 325.2 %reduce-scatter.5.cloned.1.call-start = ((), (), s32[]{:S(2)}) async-start(), calls=%async_computation.5 | async-start | bytes 2359296 | tf_op jit(solution)/shard_map/reduce_scatter | solution.py:508
  14.2 9.1 %collective-permute-start = (f32[1,8,1024]{2,1,0:T(8,128)S(1)}, f32[1,8,1024]{2,1,0:T(8,128)S(1)}, u32[]{:S(2)}, u32[]{:S(2)}) collective-permute-start(f32[1,8,1024]{2,1,0:T(8,128)S(1)} %get-tuple-element.66), channel_id=1, source_target_pairs={{0,2},{1,3},{2,0},{3,1},{4,6},{5,7},{6,4},{7,5},{8,10},{9,11},{10,... | collective-permute-start | bytes 98312 | tf_op jit(solution)/shard_map/ppermute | solution.py:52
  16.7 6.5 %collective-permute-start.4 = (f32[1,8,1024]{2,1,0:T(8,128)S(1)}, f32[1,8,1024]{2,1,0:T(8,128)S(1)}, u32[]{:S(2)}, u32[]{:S(2)}) collective-permute-start(f32[1,8,1024]{2,1,0:T(8,128)S(1)} %get-tuple-element.66), channel_id=1, source_target_pairs={{0,16},{16,0},{32,48},{48,32},{64,80},{80,64},{96,112},{112,96},{1... | collective-permute-start | bytes 98312 | tf_op jit(solution)/shard_map/ppermute | solution.py:55
  20.0 14.6 %collective-permute-start.7 = (f32[64,1024]{1,0:T(8,128)}, f32[64,1024]{1,0:T(8,128)S(1)}, u32[]{:S(2)}, u32[]{:S(2)}) collective-permute-start(f32[64,1024]{1,0:T(8,128)} %first.4), channel_id=1, source_target_pairs={{0,16},{16,0},{32,48},{48,32},{64,80},{80,64},{96,112},{112,96},{1... | collective-permute-start | bytes 786440 | tf_op jit(solution)/shard_map/ppermute | solution.py:39
  23.3 5.0 %collective-permute-start.1 = (f32[2,8,1024]{2,1,0:T(8,128)S(1)}, f32[2,8,1024]{2,1,0:T(8,128)S(1)}, u32[]{:S(2)}, u32[]{:S(2)}) collective-permute-start(f32[2,8,1024]{2,1,0:T(8,128)S(1)} %get-tuple-element.80), channel_id=1, source_target_pairs={{0,4},{1,5},{2,6},{3,7},{4,0},{5,1},{6,2},{7,3},{8,12},{9,13},{10,... | collective-permute-start | bytes 196616 | tf_op jit(solution)/shard_map/ppermute | solution.py:52
  24.7 3.6 collective-permute-start.5
  28.3 9.2 %collective-permute-start.2 = (f32[4,8,1024]{2,1,0:T(8,128)S(1)}, f32[4,8,1024]{2,1,0:T(8,128)S(1)}, u32[]{:S(2)}, u32[]{:S(2)}) collective-permute-start(f32[4,8,1024]{2,1,0:T(8,128)S(1)} %get-tuple-element.78), channel_id=1, source_target_pairs={{0,8},{1,9},{2,10},{3,11},{4,12},{5,13},{6,14},{7,15},{8,0},{9,1},... | collective-permute-start | bytes 393224 | tf_op jit(solution)/shard_map/ppermute | solution.py:52
  31.2 6.3 %collective-permute-start.6 = (f32[4,8,1024]{2,1,0:T(8,128)S(1)}, f32[4,8,1024]{2,1,0:T(8,128)}, u32[]{:S(2)}, u32[]{:S(2)}) collective-permute-start(f32[4,8,1024]{2,1,0:T(8,128)S(1)} %get-tuple-element.77), channel_id=1, source_target_pairs={{0,64},{16,80},{32,96},{48,112},{64,0},{80,16},{96,32},{112,48},{1... | collective-permute-start | bytes 393224 | tf_op jit(solution)/shard_map/ppermute | solution.py:55
  34.7 38.0 %collective-permute-start.10 = (f32[2,64,1024]{2,1,0:T(8,128)S(1)}, f32[2,64,1024]{2,1,0:T(8,128)S(1)}, u32[]{:S(2)}, u32[]{:S(2)}) collective-permute-start(f32[2,64,1024]{2,1,0:T(8,128)S(1)} %pad_maximum_fusion.2.refs_1_), channel_id=1, source_target_pairs={{0,96},{16,112},{32,0},{48,16},{64,32},{80,48},{96,64},{112,80},{1... | collective-permute-start | bytes 1572872 | tf_op jit(solution)/shard_map/ppermute | solution.py:27
  35.7 37.1 %collective-permute-start.8 = (f32[2,64,1024]{2,1,0:T(8,128)S(1)}, f32[2,64,1024]{2,1,0:T(8,128)S(1)}, u32[]{:S(2)}, u32[]{:S(2)}) collective-permute-start(f32[2,64,1024]{2,1,0:T(8,128)S(1)} %pad_maximum_fusion.2.refs_1_), channel_id=1, source_target_pairs={{0,32},{16,48},{32,64},{48,80},{64,96},{80,112},{96,0},{112,16},{1... | collective-permute-start | bytes 1572872 | tf_op jit(solution)/shard_map/ppermute | solution.py:27
  36.2 36.5 %collective-permute-start.9 = (f32[2,64,1024]{2,1,0:T(8,128)S(1)}, f32[2,64,1024]{2,1,0:T(8,128)S(1)}, u32[]{:S(2)}, u32[]{:S(2)}) collective-permute-start(f32[2,64,1024]{2,1,0:T(8,128)S(1)} %pad_maximum_fusion.2.refs_1_), channel_id=1, source_target_pairs={{0,64},{16,80},{32,96},{48,112},{64,0},{80,16},{96,32},{112,48},{1... | collective-permute-start | bytes 1572872 | tf_op jit(solution)/shard_map/ppermute | solution.py:27
  38.4 5.2 %collective-permute-start.3 = (f32[8,8,1024]{2,1,0:T(8,128)S(1)}, f32[8,8,1024]{2,1,0:T(8,128)S(1)}, u32[]{:S(2)}, u32[]{:S(2)}) collective-permute-start(f32[8,8,1024]{2,1,0:T(8,128)S(1)} %get-tuple-element.76), channel_id=1, source_target_pairs={{0,1},{1,0},{2,3},{3,2},{4,5},{5,4},{6,7},{7,6},{8,9},{9,8},{10,11... | collective-permute-start | bytes 786440 | tf_op jit(solution)/shard_map/ppermute | solution.py:52
  90.7 24.5 %collective-permute-start.14 = (f32[8,64,1024]{2,1,0:T(8,128)}, f32[8,64,1024]{2,1,0:T(8,128)}, u32[]{:S(2)}, u32[]{:S(2)}) collective-permute-start(f32[8,64,1024]{2,1,0:T(8,128)} %get-tuple-element.39), channel_id=1, source_target_pairs={{0,1},{1,0},{2,3},{3,2},{4,5},{5,4},{6,7},{7,6},{8,9},{9,8},{10,11... | collective-permute-start | bytes 6291464 | tf_op jit(solution)/shard_map/ppermute | solution.py:31
  108.6 225.4 %reduce-scatter.3.cloned.1.call-start = ((), (), s32[]{:S(2)}) async-start(), calls=%async_computation.4 | async-start | bytes 2359296 | tf_op jit(solution)/shard_map/reduce_scatter | solution.py:510
  108.6 16.6 %collective-permute-start.11 = (f32[2,64,1024]{2,1,0:T(8,128)}, f32[2,64,1024]{2,1,0:T(8,128)S(1)}, u32[]{:S(2)}, u32[]{:S(2)}) collective-permute-start(f32[2,64,1024]{2,1,0:T(8,128)} %get-tuple-element.35), channel_id=1, source_target_pairs={{0,64},{16,80},{32,96},{48,112},{64,0},{80,16},{96,32},{112,48},{1... | collective-permute-start | bytes 1572872 | tf_op jit(solution)/shard_map/ppermute | solution.py:27
  111.5 30.1 %collective-permute-start.12 = (f32[2,64,1024]{2,1,0:T(8,128)}, f32[2,64,1024]{2,1,0:T(8,128)S(1)}, u32[]{:S(2)}, u32[]{:S(2)}) collective-permute-start(f32[2,64,1024]{2,1,0:T(8,128)} %get-tuple-element.36), channel_id=1, source_target_pairs={{0,32},{16,48},{32,64},{48,80},{64,96},{80,112},{96,0},{112,16},{1... | collective-permute-start | bytes 1572872 | tf_op jit(solution)/shard_map/ppermute | solution.py:27
  111.8 32.5 %collective-permute-start.13 = (f32[2,64,1024]{2,1,0:T(8,128)S(1)}, f32[2,64,1024]{2,1,0:T(8,128)S(1)}, u32[]{:S(2)}, u32[]{:S(2)}) collective-permute-start(f32[2,64,1024]{2,1,0:T(8,128)S(1)} %copy-done.31), channel_id=1, source_target_pairs={{0,96},{16,112},{32,0},{48,16},{64,32},{80,48},{96,64},{112,80},{1... | collective-permute-start | bytes 1572872 | tf_op jit(solution)/shard_map/ppermute | solution.py:27
  114.2 100.4 %collective-permute-start.55 = (f32[64,8192]{1,0:T(8,128)}, f32[64,8192]{1,0:T(8,128)}, u32[]{:S(2)}, u32[]{:S(2)}) collective-permute-start(f32[64,8192]{1,0:T(8,128)} %get-tuple-element.55), channel_id=1, source_target_pairs={{0,1},{1,0},{2,3},{3,2},{4,5},{5,4},{6,7},{7,6},{8,9},{9,8},{10,11... | collective-permute-start | bytes 6291464 | tf_op jit(solution)/shard_map/ppermute | solution.py:31
  116.9 29.5 %collective-permute-start.15 = (f32[2,64,1024]{2,1,0:T(8,128)S(1)}, f32[2,64,1024]{2,1,0:T(8,128)S(1)}, u32[]{:S(2)}, u32[]{:S(2)}) collective-permute-start(f32[2,64,1024]{2,1,0:T(8,128)S(1)} %get-tuple-element.70), channel_id=1, source_target_pairs={{0,8},{1,9},{2,10},{3,11},{4,12},{5,13},{6,14},{7,15},{8,0},{9,1},... | collective-permute-start | bytes 1572872 | tf_op jit(solution)/shard_map/ppermute | solution.py:23
  125.2 21.2 %collective-permute-start.16 = (f32[2,64,1024]{2,1,0:T(8,128)S(1)}, f32[2,64,1024]{2,1,0:T(8,128)S(1)}, u32[]{:S(2)}, u32[]{:S(2)}) collective-permute-start(f32[2,64,1024]{2,1,0:T(8,128)S(1)} %get-tuple-element.72), channel_id=1, source_target_pairs={{0,4},{1,5},{2,6},{3,7},{4,8},{5,9},{6,10},{7,11},{8,12},{9,13},{1... | collective-permute-start | bytes 1572872 | tf_op jit(solution)/shard_map/ppermute | solution.py:23
  141.6 13.6 %collective-permute-start.17 = (f32[2,64,1024]{2,1,0:T(8,128)S(1)}, f32[2,64,1024]{2,1,0:T(8,128)S(1)}, u32[]{:S(2)}, u32[]{:S(2)}) collective-permute-start(f32[2,64,1024]{2,1,0:T(8,128)S(1)} %get-tuple-element.71), channel_id=1, source_target_pairs={{0,12},{1,13},{2,14},{3,15},{4,0},{5,1},{6,2},{7,3},{8,4},{9,5},{1... | collective-permute-start | bytes 1572872 | tf_op jit(solution)/shard_map/ppermute | solution.py:23
  144.5 16.9 %collective-permute-start.18 = (f32[64,1024]{1,0:T(8,128)S(1)}, f32[64,1024]{1,0:T(8,128)S(1)}, u32[]{:S(2)}, u32[]{:S(2)}) collective-permute-start(f32[64,1024]{1,0:T(8,128)S(1)} %slice_bitcast_fusion.3), channel_id=1, source_target_pairs={{0,16},{16,0},{32,48},{48,32},{64,80},{80,64},{96,112},{112,96},{1... | collective-permute-start | bytes 786440 | tf_op jit(solution)/shard_map/ppermute | solution.py:39
  156.7 8.7 %collective-permute-start.19 = (f32[64,1024]{1,0:T(8,128)S(1)}, f32[64,1024]{1,0:T(8,128)S(1)}, u32[]{:S(2)}, u32[]{:S(2)}) collective-permute-start(f32[64,1024]{1,0:T(8,128)S(1)} %slice_bitcast_fusion.2), channel_id=1, source_target_pairs={{0,2},{1,3},{2,0},{3,1},{4,6},{5,7},{6,4},{7,5},{8,10},{9,11},{10,... | collective-permute-start | bytes 786440 | tf_op jit(solution)/shard_map/ppermute | solution.py:35
  168.6 2.4 collective-permute-start.20
  171.0 2.5 collective-permute-start.21
  173.6 2.5 collective-permute-start.22
  176.1 4.5 collective-permute-start.23
  180.7 4.0 collective-permute-start.24
  184.7 3.0 collective-permute-start.25
  187.8 4.1 collective-permute-start.26
  191.9 49.5 %copy-start.10 = (f32[64,8192]{1,0:T(8,128)S(1)}, f32[64,8192]{1,0:T(8,128)}, u32[]{:S(2)}) copy-start(f32[64,8192]{1,0:T(8,128)} %get-tuple-element.54) | copy-start | bytes 6291460
  192.9 5.3 %collective-permute-start.27 = (f32[64,1024]{1,0:T(8,128)S(1)}, f32[64,1024]{1,0:T(8,128)S(1)}, u32[]{:S(2)}, u32[]{:S(2)}) collective-permute-start(f32[64,1024]{1,0:T(8,128)S(1)} %shard_map.103.refs_5_.second), channel_id=1, source_target_pairs={{0,2},{1,3},{2,0},{3,1},{4,6},{5,7},{6,4},{7,5},{8,10},{9,11},{10,... | collective-permute-start | bytes 786440 | tf_op jit(solution)/shard_map/ppermute | solution.py:35
  193.0 9.2 %collective-permute-start.35 = (f32[64,1024]{1,0:T(8,128)S(1)}, f32[64,1024]{1,0:T(8,128)S(1)}, u32[]{:S(2)}, u32[]{:S(2)}) collective-permute-start(f32[64,1024]{1,0:T(8,128)S(1)} %shard_map.103.refs_5_.second), channel_id=1, source_target_pairs={{0,16},{16,0},{32,48},{48,32},{64,80},{80,64},{96,112},{112,96},{1... | collective-permute-start | bytes 786440 | tf_op jit(solution)/shard_map/ppermute | solution.py:39
  202.3 42.2 %copy-start.11 = (f32[2,64,1024]{2,1,0:T(8,128)}, f32[2,64,1024]{2,1,0:T(8,128)S(1)}, u32[]{:S(2)}) copy-start(f32[2,64,1024]{2,1,0:T(8,128)S(1)} %get-tuple-element.73.refs_8_) | copy-start | bytes 1572868
  202.3 42.2 %copy-start.12 = (f32[2,64,1024]{2,1,0:T(8,128)}, f32[2,64,1024]{2,1,0:T(8,128)S(1)}, u32[]{:S(2)}) copy-start(f32[2,64,1024]{2,1,0:T(8,128)S(1)} %get-tuple-element.74.refs_0_) | copy-start | bytes 1572868
  202.3 12.4 %collective-permute-start.28 = (f32[2,64,1024]{2,1,0:T(8,128)S(1)}, f32[2,64,1024]{2,1,0:T(8,128)S(1)}, u32[]{:S(2)}, u32[]{:S(2)}) collective-permute-start(f32[2,64,1024]{2,1,0:T(8,128)S(1)} %get-tuple-element.74.refs_0_), channel_id=1, source_target_pairs={{0,4},{1,5},{2,6},{3,7},{4,8},{5,9},{6,10},{7,11},{8,12},{9,13},{1... | collective-permute-start | bytes 1572872 | tf_op jit(solution)/shard_map/ppermute | solution.py:23
  203.1 18.1 %collective-permute-start.29 = (f32[2,64,1024]{2,1,0:T(8,128)S(1)}, f32[2,64,1024]{2,1,0:T(8,128)S(1)}, u32[]{:S(2)}, u32[]{:S(2)}) collective-permute-start(f32[2,64,1024]{2,1,0:T(8,128)S(1)} %get-tuple-element.74.refs_0_), channel_id=1, source_target_pairs={{0,8},{1,9},{2,10},{3,11},{4,12},{5,13},{6,14},{7,15},{8,0},{9,1},... | collective-permute-start | bytes 1572872 | tf_op jit(solution)/shard_map/ppermute | solution.py:23
  205.8 19.2 %collective-permute-start.30 = (f32[2,64,1024]{2,1,0:T(8,128)S(1)}, f32[2,64,1024]{2,1,0:T(8,128)S(1)}, u32[]{:S(2)}, u32[]{:S(2)}) collective-permute-start(f32[2,64,1024]{2,1,0:T(8,128)S(1)} %get-tuple-element.74.refs_0_), channel_id=1, source_target_pairs={{0,12},{1,13},{2,14},{3,15},{4,0},{5,1},{6,2},{7,3},{8,4},{9,5},{1... | collective-permute-start | bytes 1572872 | tf_op jit(solution)/shard_map/ppermute | solution.py:23
  206.4 26.6 %collective-permute-start.31 = (f32[2,64,1024]{2,1,0:T(8,128)S(1)}, f32[2,64,1024]{2,1,0:T(8,128)S(1)}, u32[]{:S(2)}, u32[]{:S(2)}) collective-permute-start(f32[2,64,1024]{2,1,0:T(8,128)S(1)} %get-tuple-element.74.refs_0_), channel_id=1, source_target_pairs={{0,1},{1,0},{2,3},{3,2},{4,5},{5,4},{6,7},{7,6},{8,9},{9,8},{10,11... | collective-permute-start | bytes 1572872 | tf_op jit(solution)/shard_map/ppermute | solution.py:31
  214.6 25.9 %collective-permute-start.36 = (f32[2,64,1024]{2,1,0:T(8,128)S(1)}, f32[2,64,1024]{2,1,0:T(8,128)S(1)}, u32[]{:S(2)}, u32[]{:S(2)}) collective-permute-start(f32[2,64,1024]{2,1,0:T(8,128)S(1)} %get-tuple-element.73.refs_8_), channel_id=1, source_target_pairs={{0,32},{16,48},{32,64},{48,80},{64,96},{80,112},{96,0},{112,16},{1... | collective-permute-start | bytes 1572872 | tf_op jit(solution)/shard_map/ppermute | solution.py:27
  214.7 31.1 %collective-permute-start.37 = (f32[2,64,1024]{2,1,0:T(8,128)S(1)}, f32[2,64,1024]{2,1,0:T(8,128)}, u32[]{:S(2)}, u32[]{:S(2)}) collective-permute-start(f32[2,64,1024]{2,1,0:T(8,128)S(1)} %get-tuple-element.73.refs_8_), channel_id=1, source_target_pairs={{0,64},{16,80},{32,96},{48,112},{64,0},{80,16},{96,32},{112,48},{1... | collective-permute-start | bytes 1572872 | tf_op jit(solution)/shard_map/ppermute | solution.py:27
  221.2 24.6 %collective-permute-start.38 = (f32[2,64,1024]{2,1,0:T(8,128)S(1)}, f32[2,64,1024]{2,1,0:T(8,128)}, u32[]{:S(2)}, u32[]{:S(2)}) collective-permute-start(f32[2,64,1024]{2,1,0:T(8,128)S(1)} %get-tuple-element.73.refs_8_), channel_id=1, source_target_pairs={{0,96},{16,112},{32,0},{48,16},{64,32},{80,48},{96,64},{112,80},{1... | collective-permute-start | bytes 1572872 | tf_op jit(solution)/shard_map/ppermute | solution.py:27
  225.0 20.8 %collective-permute-start.32 = (f32[2,64,1024]{2,1,0:T(8,128)S(1)}, f32[2,64,1024]{2,1,0:T(8,128)}, u32[]{:S(2)}, u32[]{:S(2)}) collective-permute-start(f32[2,64,1024]{2,1,0:T(8,128)S(1)} %collective-permute-done.28.refs_1_), channel_id=1, source_target_pairs={{0,1},{1,0},{2,3},{3,2},{4,5},{5,4},{6,7},{7,6},{8,9},{9,8},{10,11... | collective-permute-start | bytes 1572872 | tf_op jit(solution)/shard_map/ppermute | solution.py:31
  233.0 12.8 %collective-permute-start.33 = (f32[2,64,1024]{2,1,0:T(8,128)S(1)}, f32[2,64,1024]{2,1,0:T(8,128)}, u32[]{:S(2)}, u32[]{:S(2)}) collective-permute-start(f32[2,64,1024]{2,1,0:T(8,128)S(1)} %collective-permute-done.29.refs_2_), channel_id=1, source_target_pairs={{0,1},{1,0},{2,3},{3,2},{4,5},{5,4},{6,7},{7,6},{8,9},{9,8},{10,11... | collective-permute-start | bytes 1572872 | tf_op jit(solution)/shard_map/ppermute | solution.py:31
  240.5 5.4 %collective-permute-start.34 = (f32[2,64,1024]{2,1,0:T(8,128)S(1)}, f32[2,64,1024]{2,1,0:T(8,128)}, u32[]{:S(2)}, u32[]{:S(2)}) collective-permute-start(f32[2,64,1024]{2,1,0:T(8,128)S(1)} %collective-permute-done.30.refs_3_), channel_id=1, source_target_pairs={{0,1},{1,0},{2,3},{3,2},{4,5},{5,4},{6,7},{7,6},{8,9},{9,8},{10,11... | collective-permute-start | bytes 1572872 | tf_op jit(solution)/shard_map/ppermute | solution.py:31
  244.6 218.7 %all-reduce.2.cloned.1.call-start = ((), (), s32[]{:S(2)}) async-start(), calls=%async_computation.3 | async-start | bytes 163840 | tf_op jit(solution)/shard_map/psum | solution.py:500
  262.7 4.9 %collective-permute-start.42 = (f32[8,64,1024]{2,1,0:T(8,128)}, f32[8,64,1024]{2,1,0:T(8,128)S(1)}, u32[]{:S(2)}, u32[]{:S(2)}) collective-permute-start(f32[8,64,1024]{2,1,0:T(8,128)} %get-tuple-element.47), channel_id=1, source_target_pairs={{0,1},{1,0},{2,3},{3,2},{4,5},{5,4},{6,7},{7,6},{8,9},{9,8},{10,11... | collective-permute-start | bytes 6291464 | tf_op jit(solution)/shard_map/ppermute | solution.py:31
  263.5 15.0 %collective-permute-start.39 = (f32[2,64,1024]{2,1,0:T(8,128)}, f32[2,64,1024]{2,1,0:T(8,128)S(1)}, u32[]{:S(2)}, u32[]{:S(2)}) collective-permute-start(f32[2,64,1024]{2,1,0:T(8,128)} %get-tuple-element.43), channel_id=1, source_target_pairs={{0,64},{16,80},{32,96},{48,112},{64,0},{80,16},{96,32},{112,48},{1... | collective-permute-start | bytes 1572872 | tf_op jit(solution)/shard_map/ppermute | solution.py:27
  264.0 26.5 %collective-permute-start.40 = (f32[2,64,1024]{2,1,0:T(8,128)}, f32[2,64,1024]{2,1,0:T(8,128)S(1)}, u32[]{:S(2)}, u32[]{:S(2)}) collective-permute-start(f32[2,64,1024]{2,1,0:T(8,128)} %get-tuple-element.44), channel_id=1, source_target_pairs={{0,32},{16,48},{32,64},{48,80},{64,96},{80,112},{96,0},{112,16},{1... | collective-permute-start | bytes 1572872 | tf_op jit(solution)/shard_map/ppermute | solution.py:27
  264.0 26.5 %collective-permute-start.41 = (f32[2,64,1024]{2,1,0:T(8,128)}, f32[2,64,1024]{2,1,0:T(8,128)S(1)}, u32[]{:S(2)}, u32[]{:S(2)}) collective-permute-start(f32[2,64,1024]{2,1,0:T(8,128)} %get-tuple-element.45), channel_id=1, source_target_pairs={{0,96},{16,112},{32,0},{48,16},{64,32},{80,48},{96,64},{112,80},{1... | collective-permute-start | bytes 1572872 | tf_op jit(solution)/shard_map/ppermute | solution.py:27
  269.3 22.1 %collective-permute-start.43 = (f32[2,64,1024]{2,1,0:T(8,128)S(1)}, f32[2,64,1024]{2,1,0:T(8,128)S(1)}, u32[]{:S(2)}, u32[]{:S(2)}) collective-permute-start(f32[2,64,1024]{2,1,0:T(8,128)S(1)} %get-tuple-element.67), channel_id=1, source_target_pairs={{0,8},{1,9},{2,10},{3,11},{4,12},{5,13},{6,14},{7,15},{8,0},{9,1},... | collective-permute-start | bytes 1572872 | tf_op jit(solution)/shard_map/ppermute | solution.py:23
  270.9 25.1 %collective-permute-start.44 = (f32[2,64,1024]{2,1,0:T(8,128)S(1)}, f32[2,64,1024]{2,1,0:T(8,128)S(1)}, u32[]{:S(2)}, u32[]{:S(2)}) collective-permute-start(f32[2,64,1024]{2,1,0:T(8,128)S(1)} %get-tuple-element.69), channel_id=1, source_target_pairs={{0,4},{1,5},{2,6},{3,7},{4,8},{5,9},{6,10},{7,11},{8,12},{9,13},{1... | collective-permute-start | bytes 1572872 | tf_op jit(solution)/shard_map/ppermute | solution.py:23
  278.6 25.2 %collective-permute-start.45 = (f32[2,64,1024]{2,1,0:T(8,128)S(1)}, f32[2,64,1024]{2,1,0:T(8,128)S(1)}, u32[]{:S(2)}, u32[]{:S(2)}) collective-permute-start(f32[2,64,1024]{2,1,0:T(8,128)S(1)} %get-tuple-element.68), channel_id=1, source_target_pairs={{0,12},{1,13},{2,14},{3,15},{4,0},{5,1},{6,2},{7,3},{8,4},{9,5},{1... | collective-permute-start | bytes 1572872 | tf_op jit(solution)/shard_map/ppermute | solution.py:23
  290.6 15.7 %collective-permute-start.46 = (f32[64,1024]{1,0:T(8,128)S(1)}, f32[64,1024]{1,0:T(8,128)S(1)}, u32[]{:S(2)}, u32[]{:S(2)}) collective-permute-start(f32[64,1024]{1,0:T(8,128)S(1)} %slice_bitcast_fusion.1), channel_id=1, source_target_pairs={{0,16},{16,0},{32,48},{48,32},{64,80},{80,64},{96,112},{112,96},{1... | collective-permute-start | bytes 786440 | tf_op jit(solution)/shard_map/ppermute | solution.py:39
  305.1 7.3 %collective-permute-start.47 = (f32[64,1024]{1,0:T(8,128)S(1)}, f32[64,1024]{1,0:T(8,128)S(1)}, u32[]{:S(2)}, u32[]{:S(2)}) collective-permute-start(f32[64,1024]{1,0:T(8,128)S(1)} %slice_bitcast_fusion), channel_id=1, source_target_pairs={{0,2},{1,3},{2,0},{3,1},{4,6},{5,7},{6,4},{7,5},{8,10},{9,11},{10,... | collective-permute-start | bytes 786440 | tf_op jit(solution)/shard_map/ppermute | solution.py:35
  313.5 2.4 collective-permute-start.48
  315.9 2.5 collective-permute-start.49
  318.4 2.8 collective-permute-start.50
  321.2 4.0 collective-permute-start.51
  325.3 4.0 collective-permute-start.52
  329.3 2.5 collective-permute-start.53
  331.9 4.0 collective-permute-start.54
  (28 other events, 399.3 us)
Sparse Core Ops, SparseCore 0:
  10.5 44.2 all-gather.1
  108.7 81.2 reduce-scatter.4
  244.7 57.8 reduce-scatter.2
Sparse Core Ops, SparseCore 1:
  322.6 140.6 all-reduce.1
where the time goes:
time: 476 us
  waiting for transfers between devices  256 us (54%)
  Pallas kernels  84.4 us (18%)
  starting transfers between devices  84.3 us (18%)
  local copies, waits for them, and re-layouts  18.1 us (4%)
  other arithmetic  17.3 us (4%)
  between operations  15.7 us (3%)
    psum x1, waiting for transfers between devices, on_device(): gram = lax.psum(gram, ('row', 'col'))  127 us
    pallas_call x3, Pallas kernels, products(): pl.pallas_call(functools.partial(product_kernel, len(row_in), len(col_in)...  50.4 us
    ppermute x12, waiting for transfers between devices, shift_x(): return lax.ppermute(v, 'row', [(i, (i + 2 * s) % 8) for i in range(8)])  49.3 us
    ppermute x9, waiting for transfers between devices, shift_y(): return lax.ppermute(v, 'col', [(i, (i + 4 * s) % 16) for i in range(16)])  30.3 us
    ppermute x14, waiting for transfers between devices, sum_everywhere(): v = v + lax.ppermute(v, axis, [(i, i ^ bit) for i in range(size)])  26.7 us
    pallas_call x1, Pallas kernels, make_tiles(): pl.pallas_call(tile_kernel, out_shape=(out, out), grid_spec=pltpu.Prefetc...  24.8 us
    ppermute x7, starting transfers between devices, flip_core(): return lax.ppermute(v, 'col', [(i, i ^ 1) for i in range(16)])  19.4 us
    ppermute x14, starting transfers between devices, sum_everywhere(): v = v + lax.ppermute(v, axis, [(i, i ^ bit) for i in range(size)])  17.1 us
  transfers between devices with their start and end apart: 60, of which 33 were waited for; matrix products, arithmetic and copies ran while one was open for 6% of the time, Pallas kernels for 14%

commit v1 on v0

--- a/solution.py
+++ b/solution.py
@@ -59,7 +59,10 @@
 
 def gather_row_group(v):
     pair = jnp.stack([v, flip_z_hi(v)])
-    return [pair] + [shift_x(pair, s) for s in (1, 2, 3)]
+    gathered = [pair]
+    for s in (1, 2, 3):
+        gathered.append(shift_x(pair, s))
+    return gathered
 
 
 def gather_col_group(v):
@@ -81,97 +84,63 @@
     return high, v - high
 
 
-def tile_kernel(row_at, col_at, row_points, col_points, scale, kern, slope, left, right):
-    @pl.when(pl.program_id(0) == 0)
-    def _():
-        def features(points, is_left):
-            scaled = points * scale[...]
-            size = scaled.shape[1]
-            norm = split_three(jnp.sum(scaled * scaled, axis=0, keepdims=True))
-            one = jnp.ones((1, size), F32)
-            none = jnp.zeros((2, size), F32)
-            if is_left:
-                high, middle, low = split_three(scaled)
-                parts = [high, high, middle, middle, high, low, *norm, one, one, one]
-            else:
-                high, middle, low = split_three(-2.0 * scaled)
-                parts = [high, middle, high, middle, low, high, one, one, one, *norm]
-            parts += [none, jnp.zeros((8, size), F32)]
-            return jnp.concatenate(parts, axis=0).astype(BF16)
-
-        width = row_points.shape[2]
+def features(points, is_left):
+    size = points.shape[1]
+    norm = split_three(jnp.sum(points * points, axis=0, keepdims=True))
+    one = jnp.ones((1, size), F32)
+    if is_left:
+        high, middle, low = split_three(points)
+        parts = [high, high, middle, middle, high, low, *norm, one, one, one]
+    else:
+        high, middle, low = split_three(-2.0 * points)
+        parts = [high, middle, high, middle, low, high, one, one, one, *norm]
+    parts += [jnp.zeros((10, size), F32)]
+    return jnp.concatenate(parts, axis=0).astype(BF16)
+
+
+def tile_of(dist_sq, is_slope):
+    shifted = jnp.maximum(dist_sq, 0.0) + EPSILON
+    radius = shifted * lax.rsqrt(shifted)
+    decaying = jnp.exp2(radius * (-ROOT_THREE / math.log(2.0)))
+    tapered = jnp.maximum(1.0 - radius * (1.0 / SUPPORT), 0.0)
+    common = decaying * (tapered * tapered * tapered)
+    weight = tapered * (3.0 + (12.0 / SUPPORT) * radius)
+    growing = (1.0 / 3.0) + (ROOT_THREE / 3.0) * radius
+    if is_slope:
+        return shifted * common * (weight + (60.0 / (SUPPORT * SUPPORT)) * growing)
+    return common * weight * growing
+
+
+def product_kernel(row_count, col_count, kind, index, *refs):
+    if kind == "again":
+        tiles, refs = refs[0], refs[1:]
+    else:
+        (row_points, col_points, scale), refs = refs[:3], refs[3:]
+    row_in, refs = refs[:row_count], refs[row_count:]
+    col_in, refs = refs[:col_count], refs[col_count:]
+    if kind == "kernel":
+        tiles, refs = refs[0], refs[1:]
+    outs, refs = refs[: 3 if kind == "slope" else 6], refs[3 if kind == "slope" else 6 :]
+    here, row_held, col_held, row_total, col_total, moved, left_at = refs[:7]
+    steps = index.shape[1] // GROUP
+
+    def move(step):
+        some = pl.ds(step * GROUP, GROUP)
+        if kind == "again":
+            return pltpu.make_async_copy(tiles.at[some], here.at[some], moved.at[step])
+        return pltpu.make_async_copy(here.at[some], tiles.at[some], moved.at[step])
+
+    if kind == "again":
+
+        @pl.loop(0, steps)
+        def _(step):
+            move(step).start()
+
+    else:
+        left, right = refs[7:]
         for held, points in ((left, row_points), (right, col_points)):
             for k in range(points.shape[0]):
-                held[:, pl.ds(k * width, width)] = features(points[k], held is left)
-
-    base = pl.program_id(0) * GROUP
-    for g in range(GROUP):
-        row_lane = pl.multiple_of(row_at[base + g], BLOCK)
-        col_lane = pl.multiple_of(col_at[base + g], BLOCK)
-        dist_sq = lax.dot_general(
-            left[:, pl.ds(row_lane, BLOCK)],
-            right[:, pl.ds(col_lane, BLOCK)],
-            (((0,), (0,)), ((), ())),
-            preferred_element_type=F32,
-        )
-        shifted = jnp.maximum(dist_sq, 0.0) + EPSILON
-        radius = shifted * lax.rsqrt(shifted)
-        decaying = jnp.exp2(radius * (-ROOT_THREE / math.log(2.0)))
-        tapered = jnp.maximum(1.0 - radius * (1.0 / SUPPORT), 0.0)
-        common = decaying * (tapered * tapered * tapered)
-        weight = tapered * (3.0 + (12.0 / SUPPORT) * radius)
-        growing = (1.0 / 3.0) + (ROOT_THREE / 3.0) * radius
-        kernel_tile = common * weight * growing
-        slope_tile = shifted * common * (weight + (60.0 / (SUPPORT * SUPPORT)) * growing)
-        for out, tile in ((kern, kernel_tile), (slope, slope_tile)):
-            high, low = split_two(tile)
-            out[g, 0] = high.astype(BF16)
-            out[g, 1] = low.astype(BF16)
-
-
-def make_tiles(row_at, col_at, row_points, col_points, scale):
-    tiles = row_at.shape[0]
-    whole = lambda v: pl.BlockSpec(v.shape, lambda i, *_: (0,) * v.ndim)
-    out_spec = pl.BlockSpec((GROUP, 2, BLOCK, BLOCK), lambda i, *_: (i, 0, 0, 0))
-    out = jax.ShapeDtypeStruct((tiles, 2, BLOCK, BLOCK), BF16)
-    return pl.pallas_call(
-        tile_kernel,
-        out_shape=(out, out),
-        grid_spec=pltpu.PrefetchScalarGridSpec(
-            num_scalar_prefetch=2,
-            grid=(tiles // GROUP,),
-            in_specs=[whole(row_points), whole(col_points), whole(scale)],
-            out_specs=(out_spec, out_spec),
-            scratch_shapes=[
-                pltpu.VMEM((64, row_points.shape[0] * 1024), BF16),
-                pltpu.VMEM((64, col_points.shape[0] * 1024), BF16),
-            ],
-        ),
-        compiler_params=pltpu.CompilerParams(vmem_limit_bytes=48 << 20),
-        cost_estimate=pl.CostEstimate(
-            flops=tiles * 30 * BLOCK * BLOCK,
-            bytes_accessed=tiles * 8 * BLOCK * BLOCK,
-            transcendentals=tiles * 2 * BLOCK * BLOCK,
-        ),
-        name="make_tiles",
-    )(row_at, col_at, row_points, col_points, scale)
-
-
-def product_kernel(row_count, col_count, flat, index, tiles, *refs):
-    row_in, refs = refs[:row_count], refs[row_count:]
-    col_in, refs = refs[:col_count], refs[col_count:]
-    outs, refs = refs[: 3 if flat else 6], refs[3 if flat else 6 :]
-    tiles_here, row_held, col_held, row_total, col_total, arrived, left = refs
-
-    def fetch(step):
-        some = pl.ds(step * GROUP, GROUP)
-        return pltpu.make_async_copy(tiles.at[some], tiles_here.at[some], arrived.at[step])
-
-    steps = tiles.shape[0] // GROUP
-
-    @pl.loop(0, steps)
-    def _(step):
-        fetch(step).start()
+                held[:, pl.ds(k * 1024, 1024)] = features(points[k] * scale[...], held is left)
 
     def hold(held, arrays):
         slot = 0
@@ -200,66 +169,93 @@
 
     @pl.loop(0, steps)
     def _(step):
-        fetch(step).wait()
+        if kind == "again":
+            move(step).wait()
         for g in range(GROUP):
             t = step * GROUP + g
+            at = g if kind == "slope" else t
+            if kind != "again":
+                row_point = pl.ds(pl.multiple_of(index[7, t], BLOCK), BLOCK)
+                col_point = pl.ds(pl.multiple_of(index[8, t], BLOCK), BLOCK)
+                dist_sq = lax.dot_general(
+                    left[:, row_point],
+                    right[:, col_point],
+                    (((0,), (0,)), ((), ())),
+                    preferred_element_type=F32,
+                )
+                high, low = split_two(tile_of(dist_sq, kind == "slope"))
+                here[at, 0] = high.astype(BF16)
+                here[at, 1] = low.astype(BF16)
             row_lane = pl.ds(pl.multiple_of(index[4, t], BLOCK), BLOCK)
             col_lane = pl.ds(pl.multiple_of(index[5, t], BLOCK), BLOCK)
             mirror = index[6, t].astype(F32)
-            high, low = tiles_here[t, 0], tiles_here[t, 1]
+            high, low = here[at, 0], here[at, 1]
             direct = times(col_held[index[1, t], :, col_lane], high, low, 1)
             mirrored = times(row_held[index[0, t], :, row_lane], high, low, 0)
             row_total[index[2, t], :, row_lane] += direct
             col_total[index[3, t], :, col_lane] += mirrored * mirror
-
-    if flat:
+        if kind == "kernel":
+            move(step).start()
+
+    if kind == "slope":
         slots = [row_total.at[k] for k in range(16)] + [col_total.at[k] for k in range(8)]
         places = [out.at[:, pl.ds(k * 1024, 1024)] for out in outs for k in range(8)]
     else:
-        slots = [row_total.at[pl.ds(k * 8, 8)] for k in (0, 1)]
+        slots = [row_total.at[pl.ds(k * 8, 8)] for k in (1, 0)]
         slots += [col_total.at[pl.ds(k * 2, 2)] for k in range(4)]
         places = outs
     copies = [
-        pltpu.make_async_copy(slot, place, left.at[k])
+        pltpu.make_async_copy(slot, place, left_at.at[k])
         for k, (slot, place) in enumerate(zip(slots, places))
     ]
     for copy in copies:
         copy.start()
     for copy in copies:
         copy.wait()
-
-
-def products(index, tiles, row_in, col_in, flat):
-    count = tiles.shape[0]
-    here = pl.BlockSpec(memory_space=pltpu.VMEM)
-    if flat:
+    if kind == "kernel":
+
+        @pl.loop(0, steps)
+        def _(step):
+            move(step).wait()
+
+
+def products(kind, index, sources, row_in, col_in):
+    count = index.shape[1]
+    tiles = jax.ShapeDtypeStruct((count, 2, BLOCK, BLOCK), BF16)
+    near, far = pl.BlockSpec(memory_space=pltpu.VMEM), pl.BlockSpec(memory_space=pltpu.HBM)
+    if kind == "slope":
         outs = [jax.ShapeDtypeStruct((64, 8 * 1024), F32)] * 3
     else:
         outs = [jax.ShapeDtypeStruct((8, 64, 1024), F32)] * 2
         outs += [jax.ShapeDtypeStruct((2, 64, 1024), F32)] * 4
+    if kind == "kernel":
+        outs = [tiles] + outs
+    scratch = [
+        pltpu.VMEM((GROUP if kind == "slope" else count, 2, BLOCK, BLOCK), BF16),
+        pltpu.VMEM((16, 128, 1024), BF16),
+        pltpu.VMEM((8, 128, 1024), BF16),
+        pltpu.VMEM((16, 64, 1024), F32),
+        pltpu.VMEM((8, 64, 1024), F32),
+        pltpu.SemaphoreType.DMA((count // GROUP,)),
+        pltpu.SemaphoreType.DMA((24,)),
+    ]
+    if kind != "again":
+        scratch += [pltpu.VMEM((64, 16 * 1024), BF16), pltpu.VMEM((64, 8 * 1024), BF16)]
     return pl.pallas_call(
-        functools.partial(product_kernel, len(row_in), len(col_in), flat),
+        functools.partial(product_kernel, len(row_in), len(col_in), kind),
         out_shape=tuple(outs),
-        in_specs=[pl.BlockSpec(memory_space=pltpu.SMEM), pl.BlockSpec(memory_space=pltpu.HBM)]
-        + [here] * (len(row_in) + len(col_in)),
-        out_specs=tuple(pl.BlockSpec(memory_space=pltpu.HBM) for _ in outs),
-        scratch_shapes=[
-            pltpu.VMEM(tiles.shape, BF16),
-            pltpu.VMEM((16, 128, 1024), BF16),
-            pltpu.VMEM((8, 128, 1024), BF16),
-            pltpu.VMEM((16, 64, 1024), F32),
-            pltpu.VMEM((8, 64, 1024), F32),
-            pltpu.SemaphoreType.DMA((count // GROUP,)),
-            pltpu.SemaphoreType.DMA((24,)),
-        ],
-        compiler_params=pltpu.CompilerParams(vmem_limit_bytes=60_200_000),
+        in_specs=[pl.BlockSpec(memory_space=pltpu.SMEM)]
+        + [far if kind == "again" else near] * len(sources)
+        + [near] * (len(row_in) + len(col_in)),
+        out_specs=tuple(far for _ in outs),
+        scratch_shapes=scratch,
+        compiler_params=pltpu.CompilerParams(vmem_limit_bytes=59_000_000),
         cost_estimate=pl.CostEstimate(
             flops=count * 12 * 64 * BLOCK * BLOCK,
             bytes_accessed=count * 4 * BLOCK * BLOCK + (12 << 20),
             transcendentals=0,
         ),
-        name="slope_products" if flat else "kernel_products",
-    )(index, tiles, *row_in, *col_in)
+    )(index, *sources, *row_in, *col_in)
 
 
 def column_sums(pairs, columns):
@@ -435,7 +431,7 @@
 
 
 def reduce_parts(parts):
-    row_keep, row_send, cols = parts[0], parts[1], parts[2:]
+    row_send, row_keep, cols = parts[0], parts[1], parts[2:]
     row_got = flip_core(row_send)
     col_got = []
     for s in (2, 1, 3):
@@ -476,34 +472,28 @@
     col_from = ((4 - x_to) & 3) * 2 + zhi_rel
     col_to = x_to * 2 + zhi_rel
 
+    row_points, col_points = gather_points(arranged)
+    row_xor, col_xor = row_owner ^ col_at, col_owner ^ row_at
+    row_point = ((row_xor & 1) * 8 + (row_xor >> 1)) * 1024 + row_sub * BLOCK
+    col_point = col_xor * 1024 + col_sub * BLOCK
+
     def table(row_in, col_in, row_out, col_out):
         rows = [row_in, col_in, row_out, col_out, row_sub * BLOCK, col_sub * BLOCK, mirror]
-        return jnp.stack([v.astype(jnp.int32) for v in rows])
-
-    row_points, col_points = gather_points(arranged)
-    row_xor, col_xor = row_owner ^ col_at, col_owner ^ row_at
-    kern, slope = make_tiles(
-        ((row_xor & 1) * 8 + (row_xor >> 1)) * 1024 + row_sub * BLOCK,
-        col_xor * 1024 + col_sub * BLOCK,
-        row_points,
-        col_points,
-        inv_scale[:, None],
-    )
+        return jnp.stack([v.astype(jnp.int32) for v in rows + [row_point, col_point]])
 
     noise = noise_here[None]
     row_in = [lax.all_gather(current, "col", axis=1, tiled=True)]
-    kern, current_later = lax.optimization_barrier((kern, current))
-    first_table = table(row_owner, col_from, row_to, col_to)
-    gram, first_table = lax.optimization_barrier(
-        (gram_sums(basis_vectors, current_later), first_table)
-    )
+    col_in = gather_row_group(current)
+    gram = gram_sums(basis_vectors, current)
     gram = lax.psum(gram, ("row", "col"))
-    col_in = gather_row_group(current)
-    parts = products(first_table, kern, row_in, col_in, False)
+    sources = [row_points, col_points, inv_scale[:, None]]
+    kern, *parts = products(
+        "kernel", table(row_owner, col_from, row_to, col_to), sources, row_in, col_in
+    )
     pieces = reduce_parts(parts)
     slope_to = core_rel * 8 + (row_owner >> 1)
     row_keep, row_send, col_part = products(
-        table(row_owner, col_from, slope_to, col_owner), slope, row_in, col_in, True
+        "slope", table(row_owner, col_from, slope_to, col_owner), sources, row_in, col_in
     )
     col_sum = lax.psum_scatter(col_part, "row", scatter_dimension=1, tiled=True)
     row_part = row_keep + flip_core(row_send)
@@ -523,7 +513,7 @@
 
     row_in = gather_col_group(rest)
     col_in = gather_row_group(rest)
-    parts = products(table(row_from, col_from, row_to, col_to), kern, row_in, col_in, False)
+    parts = products("again", table(row_from, col_from, row_to, col_to), [kern], row_in, col_in)
     pieces = reduce_parts(parts)
     image, next_sums = image_dots(basis_vectors, noise, pieces, [current, rest])
     next_sums = sum_everywhere(next_sums)

time: 476 us -> 513 us (1.078)
  waiting for transfers between devices: 256 us -> 276 us
  Pallas kernels: 84.4 us -> 103 us
    pallas_call x3, Pallas kernels: 50.4 us -> 94 us  [products(): pl.pallas_call(functools.partial(product_kernel, len(row_in), len(col_in)...]
    pallas_call x1 -> x0, Pallas kernels: 24.8 us -> none  [make_tiles(): pl.pallas_call(tile_kernel, out_shape=(out, out), grid_spec=pltpu.Prefetc...]
    ppermute x12, waiting for transfers between devices: 49.3 us -> 67.7 us  [shift_x(): return lax.ppermute(v, 'row', [(i, (i + 2 * s) % 8) for i in range(8)])]
  transfers between devices with their start and end apart: 60 -> 60, of which waited for: 33 -> 35; matrix products, arithmetic and copies ran while one was open for 6% -> 6% of each run, Pallas kernels for 14% -> 12%
where the time goes in v1:
time: 513 us; the launch traced here: 512 us
  waiting for transfers between devices  276 us (54%)
  Pallas kernels  103 us (20%)
  starting transfers between devices  82.5 us (16%)
  local copies, waits for them, and re-layouts  18.8 us (4%)
  other arithmetic  15.9 us (3%)
  between operations  15.7 us (3%)
    psum x1, waiting for transfers between devices, on_device(): gram = lax.psum(gram, ('row', 'col'))  129 us
    pallas_call x3, Pallas kernels, products(): pl.pallas_call(functools.partial(product_kernel, len(row_in), len(col_in)...  94 us
    ppermute x12, waiting for transfers between devices, shift_x(): return lax.ppermute(v, 'row', [(i, (i + 2 * s) % 8) for i in range(8)])  67.7 us
    ppermute x9, waiting for transfers between devices, shift_y(): return lax.ppermute(v, 'col', [(i, (i + 4 * s) % 16) for i in range(16)])  31.9 us
    ppermute x14, waiting for transfers between devices, sum_everywhere(): v = v + lax.ppermute(v, axis, [(i, i ^ bit) for i in range(size)])  26 us
    ppermute x7, starting transfers between devices, flip_core(): return lax.ppermute(v, 'col', [(i, i ^ 1) for i in range(16)])  22.4 us
    ppermute x14, starting transfers between devices, sum_everywhere(): v = v + lax.ppermute(v, axis, [(i, i ^ bit) for i in range(size)])  15.7 us
    ppermute x3, waiting for transfers between devices, flip_z_lo(): return lax.ppermute(v, 'col', [(i, i ^ 2) for i in range(16)])  12.4 us
  transfers between devices with their start and end apart: 60, of which 35 were waited for; matrix products, arithmetic and copies ran while one was open for 6% of the time, Pallas kernels for 12%

profile of v1, /device:TPU:1, one launch (start us, length us, event | category | flops | bytes accessed | tf_op | source)
XLA Modules:
  0.0 512.4 jit_solution(1929031339492570450)
XLA Ops:
  10.5 2.8 gather_fusion.1
  14.2 2.5 collective-permute-start
  16.7 3.3 collective-permute-start.4
  24.7 2.0 collective-permute-done.1
  27.0 3.0 collective-permute-start.2
  30.1 2.8 collective-permute-start.6
  37.8 3.6 collective-permute-start.3
  42.6 5.3 %collective-permute-done.10.refs_7_ = f32[2,64,1024]{2,1,0:T(8,128)S(1)} collective-permute-done((f32[2,64,1024]{2,1,0:T(8,128)S(1)}, f32[2,64,1024]{2,1,0:T(8,128)S(1)}, u32[]{:S(2)}, u32[]{:S(2)}) %collective-permute-start.10) | collective-permute-done | bytes 524320 | tf_op jit(solution)/shard_map/ppermute | solution.py:27
  48.7 9.2 %collective-permute-done.9.refs_6_ = f32[2,64,1024]{2,1,0:T(8,128)} collective-permute-done((f32[2,64,1024]{2,1,0:T(8,128)S(1)}, f32[2,64,1024]{2,1,0:T(8,128)}, u32[]{:S(2)}, u32[]{:S(2)}) %collective-permute-start.9) | collective-permute-done | bytes 524320 | tf_op jit(solution)/shard_map/ppermute | solution.py:27
  57.9 39.0 %shard_map.103 = (bf16[64,2,256,256]{3,2,1,0:T(8,128)(2,1)}, f32[8,64,1024]{2,1,0:T(8,128)}, f32[8,64,1024]{2,1,0:T(8,128)}, f32[2,64,1024]{2,1,0:T(8,128)}, f32...) custom-call(s32[9,64]{1,0:T(8,128)} %stack.22.index, f32[16,8,1024]{2,1,0:T(8,128)} %copy-done.21, ...), custom_call_target="tpu_custom_call" | custom-call | flops 3221225472 | bytes 29360128 | tf_op jit(solution)/shard_map/pallas_call | solution.py:244
  96.9 5.7 %collective-permute-start.14 = (f32[8,64,1024]{2,1,0:T(8,128)}, f32[8,64,1024]{2,1,0:T(8,128)}, u32[]{:S(2)}, u32[]{:S(2)}) collective-permute-start(f32[8,64,1024]{2,1,0:T(8,128)} %get-tuple-element.30), channel_id=1, source_target_pairs={{0,1},{1,0},{2,3},{3,2},{4,5},{5,4},{6,7},{7,6},{8,9},{9,8},{10,11... | collective-permute-start | bytes 6291464 | tf_op jit(solution)/shard_map/ppermute | solution.py:31
  103.9 38.0 %shard_map.107 = (f32[64,8192]{1,0:T(8,128)}, f32[64,8192]{1,0:T(8,128)}, f32[64,8192]{1,0:T(8,128)}) custom-call(s32[9,64]{1,0:T(8,128)} %stack.32.index, f32[16,8,1024]{2,1,0:T(8,128)} %copy-done.21, f32[8,8,1024]{2,1,0:T(8,128)} %get-tuple-element.68.refs_1_, f32[8,1]{1,0:T(8,128)} %copy.17.refs_2_, f32[64,16384]{1,0:T(8,128)} %all-gather.2.cloned.1.call-done.refs_3_, ...), custom_call_target="tpu_custom_call" | custom-call | flops 3221225472 | bytes 29360128 | tf_op jit(solution)/shard_map/pallas_call | solution.py:244
  143.2 2.4 collective-permute-start.13
  146.5 1.7 slice_add_fusion.6
  148.6 10.4 %collective-permute-done.11 = f32[2,64,1024]{2,1,0:T(8,128)S(1)} collective-permute-done((f32[2,64,1024]{2,1,0:T(8,128)}, f32[2,64,1024]{2,1,0:T(8,128)S(1)}, u32[]{:S(2)}, u32[]{:S(2)}) %collective-permute-start.11) | collective-permute-done | bytes 524320 | tf_op jit(solution)/shard_map/ppermute | solution.py:27
  159.1 16.0 %collective-permute-done.12 = f32[2,64,1024]{2,1,0:T(8,128)S(1)} collective-permute-done((f32[2,64,1024]{2,1,0:T(8,128)S(1)}, f32[2,64,1024]{2,1,0:T(8,128)S(1)}, u32[]{:S(2)}, u32[]{:S(2)}) %collective-permute-start.12) | collective-permute-done | bytes 524320 | tf_op jit(solution)/shard_map/ppermute | solution.py:27
  175.6 3.9 collective-permute-start.18
  179.5 8.6 %collective-permute-done.17 = f32[2,64,1024]{2,1,0:T(8,128)S(1)} collective-permute-done((f32[2,64,1024]{2,1,0:T(8,128)S(1)}, f32[2,64,1024]{2,1,0:T(8,128)S(1)}, u32[]{:S(2)}, u32[]{:S(2)}) %collective-permute-start.17) | collective-permute-done | bytes 524320 | tf_op jit(solution)/shard_map/ppermute | solution.py:23
  188.1 1.5 fusion.5.refs_1_
  189.7 4.5 gather_fusion
  194.3 4.1 collective-permute-done.19.refs_3_
  198.4 2.2 copy-done.2
  201.7 1.4 collective-permute-start.20
  204.3 2.1 collective-permute-done.21
  206.9 2.1 collective-permute-done.22
  209.8 3.6 collective-permute-done.23
  213.5 2.4 collective-permute-start.24
  215.8 1.7 collective-permute-done.24
  217.5 3.1 collective-permute-done.25
  220.8 3.9 collective-permute-done.26
  226.1 2.4 collective-permute-start.35
  228.5 2.5 collective-permute-done.27
  231.0 4.0 collective-permute-done.35
  236.2 1.9 collective-permute-start.29
  238.7 8.1 %collective-permute-start.31 = (f32[2,64,1024]{2,1,0:T(8,128)S(1)}, f32[2,64,1024]{2,1,0:T(8,128)S(1)}, u32[]{:S(2)}, u32[]{:S(2)}) collective-permute-start(f32[2,64,1024]{2,1,0:T(8,128)S(1)} %get-tuple-element.67.refs_1_), channel_id=1, source_target_pairs={{0,1},{1,0},{2,3},{3,2},{4,5},{5,4},{6,7},{7,6},{8,9},{9,8},{10,11... | collective-permute-start | bytes 1572872 | tf_op jit(solution)/shard_map/ppermute | solution.py:31
  246.9 1.6 collective-permute-start.37
  248.5 5.1 collective-permute-done.29.refs_3_
  253.6 4.6 collective-permute-done.30.refs_4_
  258.2 5.9 %collective-permute-start.32 = (f32[2,64,1024]{2,1,0:T(8,128)S(1)}, f32[2,64,1024]{2,1,0:T(8,128)}, u32[]{:S(2)}, u32[]{:S(2)}) collective-permute-start(f32[2,64,1024]{2,1,0:T(8,128)S(1)} %collective-permute-done.28.refs_2_), channel_id=1, source_target_pairs={{0,1},{1,0},{2,3},{3,2},{4,5},{5,4},{6,7},{7,6},{8,9},{9,8},{10,11... | collective-permute-start | bytes 1572872 | tf_op jit(solution)/shard_map/ppermute | solution.py:31
  264.2 8.6 %collective-permute-done.36.refs_10_ = f32[2,64,1024]{2,1,0:T(8,128)S(1)} collective-permute-done((f32[2,64,1024]{2,1,0:T(8,128)S(1)}, f32[2,64,1024]{2,1,0:T(8,128)S(1)}, u32[]{:S(2)}, u32[]{:S(2)}) %collective-permute-start.36) | collective-permute-done | bytes 524320 | tf_op jit(solution)/shard_map/ppermute | solution.py:27
  273.7 3.1 add.463
  278.2 16.9 %shard_map.105 = (f32[8,64,1024]{2,1,0:T(8,128)}, f32[8,64,1024]{2,1,0:T(8,128)}, f32[2,64,1024]{2,1,0:T(8,128)}, f32[2,64,1024]{2,1,0:T(8,128)}, f32[2,64,1024]{2,1,0:T(8,128)}, /*index=5*/f32[2,64,1024]{2,1,0:T(8,128)}) custom-call(s32[9,64]{1,0:T(8,128)} %stack.26.index, bf16[64,2,256,256]{3,2,1,0:T(8,128)(2,1)} %get-tuple-element.32.refs_0_, ...), custom_call_target="tpu_custom_call" | custom-call | flops 3221225472 | bytes 29360128 | tf_op jit(solution)/shard_map/pallas_call | solution.py:244
  296.8 1.9 collective-permute-start.41
  300.0 1.7 slice_add_fusion.2
  301.7 2.2 collective-permute-start.43
  303.9 7.3 %collective-permute-done.39 = f32[2,64,1024]{2,1,0:T(8,128)S(1)} collective-permute-done((f32[2,64,1024]{2,1,0:T(8,128)}, f32[2,64,1024]{2,1,0:T(8,128)S(1)}, u32[]{:S(2)}, u32[]{:S(2)}) %collective-permute-start.39) | collective-permute-done | bytes 524320 | tf_op jit(solution)/shard_map/ppermute | solution.py:27
  312.2 10.1 %collective-permute-done.40 = f32[2,64,1024]{2,1,0:T(8,128)S(1)} collective-permute-done((f32[2,64,1024]{2,1,0:T(8,128)}, f32[2,64,1024]{2,1,0:T(8,128)S(1)}, u32[]{:S(2)}, u32[]{:S(2)}) %collective-permute-start.40) | collective-permute-done | bytes 524320 | tf_op jit(solution)/shard_map/ppermute | solution.py:27
  323.0 5.4 %collective-permute-done.44 = f32[2,64,1024]{2,1,0:T(8,128)S(1)} collective-permute-done((f32[2,64,1024]{2,1,0:T(8,128)S(1)}, f32[2,64,1024]{2,1,0:T(8,128)S(1)}, u32[]{:S(2)}, u32[]{:S(2)}) %collective-permute-start.44) | collective-permute-done | bytes 524320 | tf_op jit(solution)/shard_map/ppermute | solution.py:23
  328.5 8.1 %collective-permute-done.45 = f32[2,64,1024]{2,1,0:T(8,128)S(1)} collective-permute-done((f32[2,64,1024]{2,1,0:T(8,128)S(1)}, f32[2,64,1024]{2,1,0:T(8,128)S(1)}, u32[]{:S(2)}, u32[]{:S(2)}) %collective-permute-start.45) | collective-permute-done | bytes 524320 | tf_op jit(solution)/shard_map/ppermute | solution.py:23
  337.9 1.5 collective-permute-start.47
  339.4 5.8 %collective-permute-done.47.refs_3_ = f32[64,1024]{1,0:T(8,128)S(1)} collective-permute-done((f32[64,1024]{1,0:T(8,128)S(1)}, f32[64,1024]{1,0:T(8,128)S(1)}, u32[]{:S(2)}, u32[]{:S(2)}) %collective-permute-start.47) | collective-permute-done | bytes 262176 | tf_op jit(solution)/shard_map/ppermute | solution.py:35
  346.3 1.6 collective-permute-start.48
  348.7 1.4 collective-permute-start.49
  351.3 1.5 collective-permute-start.50
  353.9 1.9 collective-permute-start.51
  355.8 4.3 gram_sums.1
  360.2 1.9 collective-permute-start.52
  362.0 2.3 collective-permute-done.52
  364.3 2.8 collective-permute-done.53
  367.1 1.7 collective-permute-start.54
  368.9 1.8 add.464
  371.2 128.6 %all-reduce.2.cloned.1.call-done.gram = f32[160,128]{1,0:T(8,128)} async-done(((f32[160,128]{1,0:T(8,128)}), f32[160,128]{1,0:T(8,128)}) %all-reduce.2.cloned.1.call-update) | async-done | bytes 81936 | tf_op jit(solution)/shard_map/psum | solution.py:488
  499.8 2.2 copy-done.5
  502.9 1.8 shard_map.106
  (178 shorter events, 41.0 us)
Async XLA Ops:
  8.0 181.7 %copy-start = (f32[1024]{0:T(1024)S(1)}, f32[1024]{0:T(1024)}, u32[]{:S(2)}) copy-start(f32[1024]{0:T(1024)} %param.10) | copy-start | bytes 12292
  8.0 49.8 %all-gather.2.cloned.1.call-start = ((), (), s32[]{:S(2)}) async-start(), calls=%async_computation.2 | async-start | bytes 4456448 | tf_op jit(solution)/shard_map/all_gather | solution.py:485
  8.8 360.1 %reduce-scatter.5.cloned.1.call-start = ((), (), s32[]{:S(2)}) async-start(), calls=%async_computation.5 | async-start | bytes 2359296 | tf_op jit(solution)/shard_map/reduce_scatter | solution.py:498
  14.2 7.9 %collective-permute-start = (f32[1,8,1024]{2,1,0:T(8,128)S(1)}, f32[1,8,1024]{2,1,0:T(8,128)S(1)}, u32[]{:S(2)}, u32[]{:S(2)}) collective-permute-start(f32[1,8,1024]{2,1,0:T(8,128)S(1)} %get-tuple-element.52), channel_id=1, source_target_pairs={{0,2},{1,3},{2,0},{3,1},{4,6},{5,7},{6,4},{7,5},{8,10},{9,11},{10,... | collective-permute-start | bytes 98312 | tf_op jit(solution)/shard_map/ppermute | solution.py:52
  16.7 5.4 %collective-permute-start.4 = (f32[1,8,1024]{2,1,0:T(8,128)S(1)}, f32[1,8,1024]{2,1,0:T(8,128)S(1)}, u32[]{:S(2)}, u32[]{:S(2)}) collective-permute-start(f32[1,8,1024]{2,1,0:T(8,128)S(1)} %get-tuple-element.52), channel_id=1, source_target_pairs={{0,16},{16,0},{32,48},{48,32},{64,80},{80,64},{96,112},{112,96},{1... | collective-permute-start | bytes 98312 | tf_op jit(solution)/shard_map/ppermute | solution.py:55
  20.0 14.7 %collective-permute-start.7 = (f32[64,1024]{1,0:T(8,128)}, f32[64,1024]{1,0:T(8,128)S(1)}, u32[]{:S(2)}, u32[]{:S(2)}) collective-permute-start(f32[64,1024]{1,0:T(8,128)} %first.5), channel_id=1, source_target_pairs={{0,16},{16,0},{32,48},{48,32},{64,80},{80,64},{96,112},{112,96},{1... | collective-permute-start | bytes 786440 | tf_op jit(solution)/shard_map/ppermute | solution.py:39
  22.1 4.6 collective-permute-start.1
  23.5 3.5 collective-permute-start.5
  27.0 10.0 %collective-permute-start.2 = (f32[4,8,1024]{2,1,0:T(8,128)S(1)}, f32[4,8,1024]{2,1,0:T(8,128)S(1)}, u32[]{:S(2)}, u32[]{:S(2)}) collective-permute-start(f32[4,8,1024]{2,1,0:T(8,128)S(1)} %get-tuple-element.71), channel_id=1, source_target_pairs={{0,8},{1,9},{2,10},{3,11},{4,12},{5,13},{6,14},{7,15},{8,0},{9,1},... | collective-permute-start | bytes 393224 | tf_op jit(solution)/shard_map/ppermute | solution.py:52
  30.1 6.9 %collective-permute-start.6 = (f32[4,8,1024]{2,1,0:T(8,128)S(1)}, f32[4,8,1024]{2,1,0:T(8,128)S(1)}, u32[]{:S(2)}, u32[]{:S(2)}) collective-permute-start(f32[4,8,1024]{2,1,0:T(8,128)S(1)} %get-tuple-element.70), channel_id=1, source_target_pairs={{0,64},{16,80},{32,96},{48,112},{64,0},{80,16},{96,32},{112,48},{1... | collective-permute-start | bytes 393224 | tf_op jit(solution)/shard_map/ppermute | solution.py:55
  34.8 13.1 %collective-permute-start.10 = (f32[2,64,1024]{2,1,0:T(8,128)S(1)}, f32[2,64,1024]{2,1,0:T(8,128)S(1)}, u32[]{:S(2)}, u32[]{:S(2)}) collective-permute-start(f32[2,64,1024]{2,1,0:T(8,128)S(1)} %pad_maximum_fusion.2.refs_4_), channel_id=1, source_target_pairs={{0,96},{16,112},{32,0},{48,16},{64,32},{80,48},{96,64},{112,80},{1... | collective-permute-start | bytes 1572872 | tf_op jit(solution)/shard_map/ppermute | solution.py:27
  35.7 12.9 %collective-permute-start.8 = (f32[2,64,1024]{2,1,0:T(8,128)S(1)}, f32[2,64,1024]{2,1,0:T(8,128)S(1)}, u32[]{:S(2)}, u32[]{:S(2)}) collective-permute-start(f32[2,64,1024]{2,1,0:T(8,128)S(1)} %pad_maximum_fusion.2.refs_4_), channel_id=1, source_target_pairs={{0,32},{16,48},{32,64},{48,80},{64,96},{80,112},{96,0},{112,16},{1... | collective-permute-start | bytes 1572872 | tf_op jit(solution)/shard_map/ppermute | solution.py:27
  36.4 21.5 %collective-permute-start.9 = (f32[2,64,1024]{2,1,0:T(8,128)S(1)}, f32[2,64,1024]{2,1,0:T(8,128)}, u32[]{:S(2)}, u32[]{:S(2)}) collective-permute-start(f32[2,64,1024]{2,1,0:T(8,128)S(1)} %pad_maximum_fusion.2.refs_4_), channel_id=1, source_target_pairs={{0,64},{16,80},{32,96},{48,112},{64,0},{80,16},{96,32},{112,48},{1... | collective-permute-start | bytes 1572872 | tf_op jit(solution)/shard_map/ppermute | solution.py:27
  37.8 4.8 collective-permute-start.3
  96.9 49.6 %collective-permute-start.14 = (f32[8,64,1024]{2,1,0:T(8,128)}, f32[8,64,1024]{2,1,0:T(8,128)}, u32[]{:S(2)}, u32[]{:S(2)}) collective-permute-start(f32[8,64,1024]{2,1,0:T(8,128)} %get-tuple-element.30), channel_id=1, source_target_pairs={{0,1},{1,0},{2,3},{3,2},{4,5},{5,4},{6,7},{7,6},{8,9},{9,8},{10,11... | collective-permute-start | bytes 6291464 | tf_op jit(solution)/shard_map/ppermute | solution.py:31
  141.9 227.0 %reduce-scatter.3.cloned.1.call-start = ((), (), s32[]{:S(2)}) async-start(), calls=%async_computation.4 | async-start | bytes 2359296 | tf_op jit(solution)/shard_map/reduce_scatter | solution.py:500
  141.9 17.1 %collective-permute-start.11 = (f32[2,64,1024]{2,1,0:T(8,128)}, f32[2,64,1024]{2,1,0:T(8,128)S(1)}, u32[]{:S(2)}, u32[]{:S(2)}) collective-permute-start(f32[2,64,1024]{2,1,0:T(8,128)} %get-tuple-element.26), channel_id=1, source_target_pairs={{0,64},{16,80},{32,96},{48,112},{64,0},{80,16},{96,32},{112,48},{1... | collective-permute-start | bytes 1572872 | tf_op jit(solution)/shard_map/ppermute | solution.py:27
  142.9 32.2 %collective-permute-start.12 = (f32[2,64,1024]{2,1,0:T(8,128)S(1)}, f32[2,64,1024]{2,1,0:T(8,128)S(1)}, u32[]{:S(2)}, u32[]{:S(2)}) collective-permute-start(f32[2,64,1024]{2,1,0:T(8,128)S(1)} %copy-done.26), channel_id=1, source_target_pairs={{0,32},{16,48},{32,64},{48,80},{64,96},{80,112},{96,0},{112,16},{1... | collective-permute-start | bytes 1572872 | tf_op jit(solution)/shard_map/ppermute | solution.py:27
  143.2 32.3 %collective-permute-start.13 = (f32[2,64,1024]{2,1,0:T(8,128)S(1)}, f32[2,64,1024]{2,1,0:T(8,128)S(1)}, u32[]{:S(2)}, u32[]{:S(2)}) collective-permute-start(f32[2,64,1024]{2,1,0:T(8,128)S(1)} %copy-done.24), channel_id=1, source_target_pairs={{0,96},{16,112},{32,0},{48,16},{64,32},{80,48},{96,64},{112,80},{1... | collective-permute-start | bytes 1572872 | tf_op jit(solution)/shard_map/ppermute | solution.py:27
  145.6 101.3 %collective-permute-start.55 = (f32[64,8192]{1,0:T(8,128)}, f32[64,8192]{1,0:T(8,128)}, u32[]{:S(2)}, u32[]{:S(2)}) collective-permute-start(f32[64,8192]{1,0:T(8,128)} %get-tuple-element.45), channel_id=1, source_target_pairs={{0,1},{1,0},{2,3},{3,2},{4,5},{5,4},{6,7},{7,6},{8,9},{9,8},{10,11... | collective-permute-start | bytes 6291464 | tf_op jit(solution)/shard_map/ppermute | solution.py:31
  148.2 31.3 %collective-permute-start.15 = (f32[2,64,1024]{2,1,0:T(8,128)S(1)}, f32[2,64,1024]{2,1,0:T(8,128)S(1)}, u32[]{:S(2)}, u32[]{:S(2)}) collective-permute-start(f32[2,64,1024]{2,1,0:T(8,128)S(1)} %get-tuple-element.63), channel_id=1, source_target_pairs={{0,8},{1,9},{2,10},{3,11},{4,12},{5,13},{6,14},{7,15},{8,0},{9,1},... | collective-permute-start | bytes 1572872 | tf_op jit(solution)/shard_map/ppermute | solution.py:23
  159.0 20.5 %collective-permute-start.16 = (f32[2,64,1024]{2,1,0:T(8,128)S(1)}, f32[2,64,1024]{2,1,0:T(8,128)S(1)}, u32[]{:S(2)}, u32[]{:S(2)}) collective-permute-start(f32[2,64,1024]{2,1,0:T(8,128)S(1)} %get-tuple-element.65), channel_id=1, source_target_pairs={{0,4},{1,5},{2,6},{3,7},{4,8},{5,9},{6,10},{7,11},{8,12},{9,13},{1... | collective-permute-start | bytes 1572872 | tf_op jit(solution)/shard_map/ppermute | solution.py:23
  175.1 13.0 %collective-permute-start.17 = (f32[2,64,1024]{2,1,0:T(8,128)S(1)}, f32[2,64,1024]{2,1,0:T(8,128)S(1)}, u32[]{:S(2)}, u32[]{:S(2)}) collective-permute-start(f32[2,64,1024]{2,1,0:T(8,128)S(1)} %get-tuple-element.64), channel_id=1, source_target_pairs={{0,12},{1,13},{2,14},{3,15},{4,0},{5,1},{6,2},{7,3},{8,4},{9,5},{1... | collective-permute-start | bytes 1572872 | tf_op jit(solution)/shard_map/ppermute | solution.py:23
  175.6 18.7 %collective-permute-start.18 = (f32[64,1024]{1,0:T(8,128)S(1)}, f32[64,1024]{1,0:T(8,128)S(1)}, u32[]{:S(2)}, u32[]{:S(2)}) collective-permute-start(f32[64,1024]{1,0:T(8,128)S(1)} %slice_bitcast_fusion.3), channel_id=1, source_target_pairs={{0,16},{16,0},{32,48},{48,32},{64,80},{80,64},{96,112},{112,96},{1... | collective-permute-start | bytes 786440 | tf_op jit(solution)/shard_map/ppermute | solution.py:39
  189.6 8.8 %collective-permute-start.19 = (f32[64,1024]{1,0:T(8,128)S(1)}, f32[64,1024]{1,0:T(8,128)S(1)}, u32[]{:S(2)}, u32[]{:S(2)}) collective-permute-start(f32[64,1024]{1,0:T(8,128)S(1)} %slice_bitcast_fusion.2), channel_id=1, source_target_pairs={{0,2},{1,3},{2,0},{3,1},{4,6},{5,7},{6,4},{7,5},{8,10},{9,11},{10,... | collective-permute-start | bytes 786440 | tf_op jit(solution)/shard_map/ppermute | solution.py:35
  201.7 2.2 collective-permute-start.20
  203.9 2.5 collective-permute-start.21
  206.5 2.5 collective-permute-start.22
  209.0 4.5 collective-permute-start.23
  213.5 4.0 collective-permute-start.24
  217.5 3.1 collective-permute-start.25
  220.6 4.1 collective-permute-start.26
  224.7 48.9 %copy-start.8 = (f32[64,8192]{1,0:T(8,128)S(1)}, f32[64,8192]{1,0:T(8,128)}, u32[]{:S(2)}) copy-start(f32[64,8192]{1,0:T(8,128)} %get-tuple-element.44) | copy-start | bytes 6291460
  225.7 5.3 %collective-permute-start.27 = (f32[64,1024]{1,0:T(8,128)S(1)}, f32[64,1024]{1,0:T(8,128)S(1)}, u32[]{:S(2)}, u32[]{:S(2)}) collective-permute-start(f32[64,1024]{1,0:T(8,128)S(1)} %shard_map.104.refs_5_.second), channel_id=1, source_target_pairs={{0,2},{1,3},{2,0},{3,1},{4,6},{5,7},{6,4},{7,5},{8,10},{9,11},{10,... | collective-permute-start | bytes 786440 | tf_op jit(solution)/shard_map/ppermute | solution.py:35
  226.1 9.0 %collective-permute-start.35 = (f32[64,1024]{1,0:T(8,128)S(1)}, f32[64,1024]{1,0:T(8,128)S(1)}, u32[]{:S(2)}, u32[]{:S(2)}) collective-permute-start(f32[64,1024]{1,0:T(8,128)S(1)} %shard_map.104.refs_5_.second), channel_id=1, source_target_pairs={{0,16},{16,0},{32,48},{48,32},{64,80},{80,64},{96,112},{112,96},{1... | collective-permute-start | bytes 786440 | tf_op jit(solution)/shard_map/ppermute | solution.py:39
  235.2 41.6 %copy-start.10 = (f32[2,64,1024]{2,1,0:T(8,128)}, f32[2,64,1024]{2,1,0:T(8,128)S(1)}, u32[]{:S(2)}) copy-start(f32[2,64,1024]{2,1,0:T(8,128)S(1)} %get-tuple-element.66.refs_9_) | copy-start | bytes 1572868
  235.2 41.6 %copy-start.11 = (f32[2,64,1024]{2,1,0:T(8,128)}, f32[2,64,1024]{2,1,0:T(8,128)S(1)}, u32[]{:S(2)}) copy-start(f32[2,64,1024]{2,1,0:T(8,128)S(1)} %get-tuple-element.67.refs_1_) | copy-start | bytes 1572868
  235.2 11.7 %collective-permute-start.28 = (f32[2,64,1024]{2,1,0:T(8,128)S(1)}, f32[2,64,1024]{2,1,0:T(8,128)S(1)}, u32[]{:S(2)}, u32[]{:S(2)}) collective-permute-start(f32[2,64,1024]{2,1,0:T(8,128)S(1)} %get-tuple-element.67.refs_1_), channel_id=1, source_target_pairs={{0,4},{1,5},{2,6},{3,7},{4,8},{5,9},{6,10},{7,11},{8,12},{9,13},{1... | collective-permute-start | bytes 1572872 | tf_op jit(solution)/shard_map/ppermute | solution.py:23
  236.2 17.3 %collective-permute-start.29 = (f32[2,64,1024]{2,1,0:T(8,128)S(1)}, f32[2,64,1024]{2,1,0:T(8,128)S(1)}, u32[]{:S(2)}, u32[]{:S(2)}) collective-permute-start(f32[2,64,1024]{2,1,0:T(8,128)S(1)} %get-tuple-element.67.refs_1_), channel_id=1, source_target_pairs={{0,8},{1,9},{2,10},{3,11},{4,12},{5,13},{6,14},{7,15},{8,0},{9,1},... | collective-permute-start | bytes 1572872 | tf_op jit(solution)/shard_map/ppermute | solution.py:23
  238.1 20.1 %collective-permute-start.30 = (f32[2,64,1024]{2,1,0:T(8,128)S(1)}, f32[2,64,1024]{2,1,0:T(8,128)S(1)}, u32[]{:S(2)}, u32[]{:S(2)}) collective-permute-start(f32[2,64,1024]{2,1,0:T(8,128)S(1)} %get-tuple-element.67.refs_1_), channel_id=1, source_target_pairs={{0,12},{1,13},{2,14},{3,15},{4,0},{5,1},{6,2},{7,3},{8,4},{9,5},{1... | collective-permute-start | bytes 1572872 | tf_op jit(solution)/shard_map/ppermute | solution.py:23
  238.7 25.3 %collective-permute-start.31 = (f32[2,64,1024]{2,1,0:T(8,128)S(1)}, f32[2,64,1024]{2,1,0:T(8,128)S(1)}, u32[]{:S(2)}, u32[]{:S(2)}) collective-permute-start(f32[2,64,1024]{2,1,0:T(8,128)S(1)} %get-tuple-element.67.refs_1_), channel_id=1, source_target_pairs={{0,1},{1,0},{2,3},{3,2},{4,5},{5,4},{6,7},{7,6},{8,9},{9,8},{10,11... | collective-permute-start | bytes 1572872 | tf_op jit(solution)/shard_map/ppermute | solution.py:31
  246.9 25.9 %collective-permute-start.36 = (f32[2,64,1024]{2,1,0:T(8,128)S(1)}, f32[2,64,1024]{2,1,0:T(8,128)S(1)}, u32[]{:S(2)}, u32[]{:S(2)}) collective-permute-start(f32[2,64,1024]{2,1,0:T(8,128)S(1)} %get-tuple-element.66.refs_9_), channel_id=1, source_target_pairs={{0,32},{16,48},{32,64},{48,80},{64,96},{80,112},{96,0},{112,16},{1... | collective-permute-start | bytes 1572872 | tf_op jit(solution)/shard_map/ppermute | solution.py:27
  246.9 31.2 %collective-permute-start.37 = (f32[2,64,1024]{2,1,0:T(8,128)S(1)}, f32[2,64,1024]{2,1,0:T(8,128)}, u32[]{:S(2)}, u32[]{:S(2)}) collective-permute-start(f32[2,64,1024]{2,1,0:T(8,128)S(1)} %get-tuple-element.66.refs_9_), channel_id=1, source_target_pairs={{0,64},{16,80},{32,96},{48,112},{64,0},{80,16},{96,32},{112,48},{1... | collective-permute-start | bytes 1572872 | tf_op jit(solution)/shard_map/ppermute | solution.py:27
  253.6 24.6 %collective-permute-start.38 = (f32[2,64,1024]{2,1,0:T(8,128)S(1)}, f32[2,64,1024]{2,1,0:T(8,128)}, u32[]{:S(2)}, u32[]{:S(2)}) collective-permute-start(f32[2,64,1024]{2,1,0:T(8,128)S(1)} %get-tuple-element.66.refs_9_), channel_id=1, source_target_pairs={{0,96},{16,112},{32,0},{48,16},{64,32},{80,48},{96,64},{112,80},{1... | collective-permute-start | bytes 1572872 | tf_op jit(solution)/shard_map/ppermute | solution.py:27
  258.2 19.9 %collective-permute-start.32 = (f32[2,64,1024]{2,1,0:T(8,128)S(1)}, f32[2,64,1024]{2,1,0:T(8,128)}, u32[]{:S(2)}, u32[]{:S(2)}) collective-permute-start(f32[2,64,1024]{2,1,0:T(8,128)S(1)} %collective-permute-done.28.refs_2_), channel_id=1, source_target_pairs={{0,1},{1,0},{2,3},{3,2},{4,5},{5,4},{6,7},{7,6},{8,9},{9,8},{10,11... | collective-permute-start | bytes 1572872 | tf_op jit(solution)/shard_map/ppermute | solution.py:31
  264.1 14.1 %collective-permute-start.33 = (f32[2,64,1024]{2,1,0:T(8,128)S(1)}, f32[2,64,1024]{2,1,0:T(8,128)}, u32[]{:S(2)}, u32[]{:S(2)}) collective-permute-start(f32[2,64,1024]{2,1,0:T(8,128)S(1)} %collective-permute-done.29.refs_3_), channel_id=1, source_target_pairs={{0,1},{1,0},{2,3},{3,2},{4,5},{5,4},{6,7},{7,6},{8,9},{9,8},{10,11... | collective-permute-start | bytes 1572872 | tf_op jit(solution)/shard_map/ppermute | solution.py:31
  272.8 5.3 %collective-permute-start.34 = (f32[2,64,1024]{2,1,0:T(8,128)S(1)}, f32[2,64,1024]{2,1,0:T(8,128)}, u32[]{:S(2)}, u32[]{:S(2)}) collective-permute-start(f32[2,64,1024]{2,1,0:T(8,128)S(1)} %collective-permute-done.30.refs_4_), channel_id=1, source_target_pairs={{0,1},{1,0},{2,3},{3,2},{4,5},{5,4},{6,7},{7,6},{8,9},{9,8},{10,11... | collective-permute-start | bytes 1572872 | tf_op jit(solution)/shard_map/ppermute | solution.py:31
  276.9 222.9 %all-reduce.2.cloned.1.call-start = ((), (), s32[]{:S(2)}) async-start(), calls=%async_computation.3 | async-start | bytes 163840 | tf_op jit(solution)/shard_map/psum | solution.py:488
  295.1 4.9 collective-permute-start.42
  296.0 15.3 %collective-permute-start.39 = (f32[2,64,1024]{2,1,0:T(8,128)}, f32[2,64,1024]{2,1,0:T(8,128)S(1)}, u32[]{:S(2)}, u32[]{:S(2)}) collective-permute-start(f32[2,64,1024]{2,1,0:T(8,128)} %get-tuple-element.35), channel_id=1, source_target_pairs={{0,64},{16,80},{32,96},{48,112},{64,0},{80,16},{96,32},{112,48},{1... | collective-permute-start | bytes 1572872 | tf_op jit(solution)/shard_map/ppermute | solution.py:27
  296.0 26.3 %collective-permute-start.40 = (f32[2,64,1024]{2,1,0:T(8,128)}, f32[2,64,1024]{2,1,0:T(8,128)S(1)}, u32[]{:S(2)}, u32[]{:S(2)}) collective-permute-start(f32[2,64,1024]{2,1,0:T(8,128)} %get-tuple-element.36), channel_id=1, source_target_pairs={{0,32},{16,48},{32,64},{48,80},{64,96},{80,112},{96,0},{112,16},{1... | collective-permute-start | bytes 1572872 | tf_op jit(solution)/shard_map/ppermute | solution.py:27
  296.8 25.5 %collective-permute-start.41 = (f32[2,64,1024]{2,1,0:T(8,128)}, f32[2,64,1024]{2,1,0:T(8,128)S(1)}, u32[]{:S(2)}, u32[]{:S(2)}) collective-permute-start(f32[2,64,1024]{2,1,0:T(8,128)} %get-tuple-element.37), channel_id=1, source_target_pairs={{0,96},{16,112},{32,0},{48,16},{64,32},{80,48},{96,64},{112,80},{1... | collective-permute-start | bytes 1572872 | tf_op jit(solution)/shard_map/ppermute | solution.py:27
  301.7 21.3 %collective-permute-start.43 = (f32[2,64,1024]{2,1,0:T(8,128)S(1)}, f32[2,64,1024]{2,1,0:T(8,128)S(1)}, u32[]{:S(2)}, u32[]{:S(2)}) collective-permute-start(f32[2,64,1024]{2,1,0:T(8,128)S(1)} %get-tuple-element.60), channel_id=1, source_target_pairs={{0,8},{1,9},{2,10},{3,11},{4,12},{5,13},{6,14},{7,15},{8,0},{9,1},... | collective-permute-start | bytes 1572872 | tf_op jit(solution)/shard_map/ppermute | solution.py:23
  303.9 24.6 %collective-permute-start.44 = (f32[2,64,1024]{2,1,0:T(8,128)S(1)}, f32[2,64,1024]{2,1,0:T(8,128)S(1)}, u32[]{:S(2)}, u32[]{:S(2)}) collective-permute-start(f32[2,64,1024]{2,1,0:T(8,128)S(1)} %get-tuple-element.62), channel_id=1, source_target_pairs={{0,4},{1,5},{2,6},{3,7},{4,8},{5,9},{6,10},{7,11},{8,12},{9,13},{1... | collective-permute-start | bytes 1572872 | tf_op jit(solution)/shard_map/ppermute | solution.py:23
  311.2 25.4 %collective-permute-start.45 = (f32[2,64,1024]{2,1,0:T(8,128)S(1)}, f32[2,64,1024]{2,1,0:T(8,128)S(1)}, u32[]{:S(2)}, u32[]{:S(2)}) collective-permute-start(f32[2,64,1024]{2,1,0:T(8,128)S(1)} %get-tuple-element.61), channel_id=1, source_target_pairs={{0,12},{1,13},{2,14},{3,15},{4,0},{5,1},{6,2},{7,3},{8,4},{9,5},{1... | collective-permute-start | bytes 1572872 | tf_op jit(solution)/shard_map/ppermute | solution.py:23
  322.5 17.0 %collective-permute-start.46 = (f32[64,1024]{1,0:T(8,128)S(1)}, f32[64,1024]{1,0:T(8,128)S(1)}, u32[]{:S(2)}, u32[]{:S(2)}) collective-permute-start(f32[64,1024]{1,0:T(8,128)S(1)} %slice_bitcast_fusion.1), channel_id=1, source_target_pairs={{0,16},{16,0},{32,48},{48,32},{64,80},{80,64},{96,112},{112,96},{1... | collective-permute-start | bytes 786440 | tf_op jit(solution)/shard_map/ppermute | solution.py:39
  337.9 7.3 %collective-permute-start.47 = (f32[64,1024]{1,0:T(8,128)S(1)}, f32[64,1024]{1,0:T(8,128)S(1)}, u32[]{:S(2)}, u32[]{:S(2)}) collective-permute-start(f32[64,1024]{1,0:T(8,128)S(1)} %slice_bitcast_fusion), channel_id=1, source_target_pairs={{0,2},{1,3},{2,0},{3,1},{4,6},{5,7},{6,4},{7,5},{8,10},{9,11},{10,... | collective-permute-start | bytes 786440 | tf_op jit(solution)/shard_map/ppermute | solution.py:35
  346.3 2.4 collective-permute-start.48
  348.7 2.5 collective-permute-start.49
  351.3 2.6 collective-permute-start.50
  353.9 6.2 %collective-permute-start.51 = (f32[24,128]{1,0:T(8,128)S(1)}, f32[24,128]{1,0:T(8,128)S(1)}, u32[]{:S(2)}, u32[]{:S(2)}) collective-permute-start(f32[24,128]{1,0:T(8,128)S(1)} %add.457), channel_id=1, source_target_pairs={{0,8},{1,9},{2,10},{3,11},{4,12},{5,13},{6,14},{7,15},{8,0},{9,1},... | collective-permute-start | bytes 36872 | tf_op jit(solution)/shard_map/ppermute | solution.py:45
  360.2 4.1 collective-permute-start.52
  364.3 2.8 collective-permute-start.53
  367.1 4.0 collective-permute-start.54
  (23 other events, 387.3 us)
Sparse Core Ops, SparseCore 0:
  10.5 43.2 all-gather.1
  142.0 79.4 reduce-scatter.4
  277.0 58.2 reduce-scatter.2
Sparse Core Ops, SparseCore 1:
  360.2 139.5 all-reduce.1

commit v2 on v0

--- a/solution.py
+++ b/solution.py
@@ -15,6 +15,8 @@
 ROOT_THREE = math.sqrt(3.0)
 SUPPORT = 3.0
 EPSILON = 1e-06
+KERNEL_UNIT = 27.0 / 20.0
+SLOPE_UNIT = 27.0
 F32 = jnp.float32
 BF16 = jnp.bfloat16
 
@@ -42,7 +44,8 @@
 def sum_everywhere(v):
     for axis, size, bits in (("col", 16, (1, 2, 4, 8)), ("row", 8, (1, 2, 4))):
         for bit in bits:
-            v = v + lax.ppermute(v, axis, [(i, i ^ bit) for i in range(size)])
+            other = lax.ppermute(v, axis, [(i, i ^ bit) for i in range(size)])
+            v = v + other
     return v
 
 
@@ -114,15 +117,15 @@
             (((0,), (0,)), ((), ())),
             preferred_element_type=F32,
         )
-        shifted = jnp.maximum(dist_sq, 0.0) + EPSILON
+        shifted = jnp.maximum(dist_sq, 0.0) + EPSILON / (SUPPORT * SUPPORT)
         radius = shifted * lax.rsqrt(shifted)
-        decaying = jnp.exp2(radius * (-ROOT_THREE / math.log(2.0)))
-        tapered = jnp.maximum(1.0 - radius * (1.0 / SUPPORT), 0.0)
+        decaying = jnp.exp2(radius * (-ROOT_THREE * SUPPORT / math.log(2.0)))
+        tapered = jnp.maximum(1.0 - radius, 0.0)
         common = decaying * (tapered * tapered * tapered)
-        weight = tapered * (3.0 + (12.0 / SUPPORT) * radius)
-        growing = (1.0 / 3.0) + (ROOT_THREE / 3.0) * radius
+        weight = tapered * (1.0 + 4.0 * radius)
+        growing = 1.0 / KERNEL_UNIT + (ROOT_THREE * SUPPORT / KERNEL_UNIT) * radius
         kernel_tile = common * weight * growing
-        slope_tile = shifted * common * (weight + (60.0 / (SUPPORT * SUPPORT)) * growing)
+        slope_tile = shifted * common * (weight + growing)
         for out, tile in ((kern, kernel_tile), (slope, slope_tile)):
             high, low = split_two(tile)
             out[g, 0] = high.astype(BF16)
@@ -181,7 +184,7 @@
             else:
                 pieces = [array.at[:, pl.ds(k * 1024, 1024)] for k in range(array.shape[1] // 1024)]
             for piece in pieces:
-                value = piece[...]
+                value = piece[...] * (SLOPE_UNIT if flat else KERNEL_UNIT)
                 high = value.astype(BF16)
                 held[slot, 0:64] = high
                 held[slot, 64:128] = (value - high.astype(F32)).astype(BF16)
@@ -368,8 +371,16 @@
 
 
 def last_rest_kernel(
-    total, sums, next_sums, gram, image, earlier, first, second, out, coefficients, held
+    total, sums, next_sums, gram, image, earlier, first, second, out, coefficients, held, here, moved
 ):
+    blocks = here.shape[1] // 8
+
+    def fetch(k):
+        at = pl.ds(k * 8, 8)
+        return pltpu.make_async_copy(earlier.at[:, at], here.at[:, at], moved.at[k])
+
+    for k in range(blocks):
+        fetch(k).start()
     count = 17
     means = sums[...] * (1.0 / total)
     along = means[0:count]
@@ -413,21 +424,29 @@
         [along[16:17], jnp.sqrt(norm_sq), alpha, beta, jnp.zeros((4, 128), F32)], axis=0
     )
 
-    @row_blocks_of(out.shape[0])
-    def _(at):
-        out[at] = combine(held[at], image[at], vectors_at(earlier, [first, second], at))
+    @pl.loop(0, blocks)
+    def _(k):
+        fetch(k).wait()
+        at = pl.ds(pl.multiple_of(k * 8, 8), 8)
+        out[at] = combine(held[at], image[at], vectors_at(here, [first, second], at))
 
 
 def rest_call(kernel, total, smalls, image, earlier, extra, with_coefficients):
     rows, lanes = image.shape
     out_shape = [jax.ShapeDtypeStruct((rows, lanes), F32)]
+    near = pl.BlockSpec(memory_space=pltpu.VMEM)
+    scratch = [pltpu.VMEM((128, 128), F32)]
     if with_coefficients:
         out_shape.append(jax.ShapeDtypeStruct((8, 128), F32))
+        scratch += [pltpu.VMEM(earlier.shape, F32), pltpu.SemaphoreType.DMA((rows // 8,))]
     return pl.pallas_call(
         functools.partial(kernel, float(total)),
         out_shape=tuple(out_shape),
-        scratch_shapes=[pltpu.VMEM((128, 128), F32)],
-        compiler_params=pltpu.CompilerParams(vmem_limit_bytes=2 << 20),
+        in_specs=[near] * (len(smalls) + 1)
+        + [pl.BlockSpec(memory_space=pltpu.HBM) if with_coefficients else near]
+        + [near] * len(extra),
+        scratch_shapes=scratch,
+        compiler_params=pltpu.CompilerParams(vmem_limit_bytes=8 << 20),
         cost_estimate=pl.CostEstimate(
             flops=rows * lanes * 40, bytes_accessed=rows * lanes * 4 * 20, transcendentals=0
         ),
@@ -487,7 +506,7 @@
         col_xor * 1024 + col_sub * BLOCK,
         row_points,
         col_points,
-        inv_scale[:, None],
+        inv_scale[:, None] * (1.0 / SUPPORT),
     )
 
     noise = noise_here[None]

time: 476 us -> 479 us (level)
  no operation moved by 1% of the time
where the time goes in v2:
time: 479 us; the launch traced here: 478 us
  waiting for transfers between devices  255 us (53%)
  starting transfers between devices  85.9 us (18%)
  Pallas kernels  85.6 us (18%)
  local copies, waits for them, and re-layouts  18.1 us (4%)
  other arithmetic  17.3 us (4%)
  between operations  15.7 us (3%)
    psum x1, waiting for transfers between devices, on_device(): gram = lax.psum(gram, ('row', 'col'))  128 us
    pallas_call x3, Pallas kernels, products(): pl.pallas_call(functools.partial(product_kernel, len(row_in), len(col_in)...  51.9 us
    ppermute x12, waiting for transfers between devices, shift_x(): return lax.ppermute(v, 'row', [(i, (i + 2 * s) % 8) for i in range(8)])  48.8 us
    ppermute x9, waiting for transfers between devices, shift_y(): return lax.ppermute(v, 'col', [(i, (i + 4 * s) % 16) for i in range(16)])  29.7 us
    ppermute x14, waiting for transfers between devices, sum_everywhere(): other = lax.ppermute(v, axis, [(i, i ^ bit) for i in range(size)])  26.1 us
    pallas_call x1, Pallas kernels, make_tiles(): pl.pallas_call(tile_kernel, out_shape=(out, out), grid_spec=pltpu.Prefetc...  24.1 us
    ppermute x7, starting transfers between devices, flip_core(): return lax.ppermute(v, 'col', [(i, i ^ 1) for i in range(16)])  20 us
    ppermute x14, starting transfers between devices, sum_everywhere(): other = lax.ppermute(v, axis, [(i, i ^ bit) for i in range(size)])  17.1 us
  transfers between devices with their start and end apart: 60, of which 33 were waited for; matrix products, arithmetic and copies ran while one was open for 6% of the time, Pallas kernels for 14%

profile of v2, /device:TPU:1, one launch (start us, length us, event | category | flops | bytes accessed | tf_op | source)
XLA Modules:
  0.0 478.1 jit_solution(10945149853819248646)
XLA Ops:
  10.5 2.8 gather_fusion.1
  14.2 2.5 collective-permute-start
  16.7 3.3 collective-permute-start.4
  25.9 2.4 collective-permute-done.1
  28.3 2.9 collective-permute-start.2
  31.2 2.7 collective-permute-start.6
  38.5 4.0 collective-permute-start.3
  43.7 24.1 %make_tiles.1 = (bf16[64,2,256,256]{3,2,1,0:T(8,128)(2,1)}, bf16[64,2,256,256]{3,2,1,0:T(8,128)(2,1)}) custom-call(s32[64]{0:T(128)S(1)} %get-tuple-element.82.row_at, s32[64]{0:T(128)S(1)} %get-tuple-element.83.col_at, f32[16,8,1024]{2,1,0:T(8,128)S(1)} %constant_dynamic-update-slice_fusion.row_points, f32[8,8,1024]{2,1,0:T(8,128)S(1)} %get-tuple-element.75.col_points, ...), custom_call_target="tpu_custom_call" | custom-call | flops 125829120 | bytes 33554432 | tf_op jit(solution)/shard_map/make_tiles/pallas_call | solution.py:140
  67.8 4.3 gram_sums.1
  73.2 17.3 %kernel_products.2 = (f32[8,64,1024]{2,1,0:T(8,128)}, f32[8,64,1024]{2,1,0:T(8,128)}, f32[2,64,1024]{2,1,0:T(8,128)}, f32[2,64,1024]{2,1,0:T(8,128)}, f32[2,64,1024]{2,1,0:T(8,128)}, /*index=5*/f32[2,64,1024]{2,1,0:T(8,128)}) custom-call(s32[7,64]{1,0:T(8,128)} %stack.22.index, bf16[64,2,256,256]{3,2,1,0:T(8,128)(2,1)} %get-tuple-element.33.tiles, ...), custom_call_target="tpu_custom_call" | custom-call | flops 3221225472 | bytes 29360128 | tf_op jit(solution)/shard_map/kernel_products/pallas_call | solution.py:243
  91.8 17.2 %slope_products.1 = (f32[64,8192]{1,0:T(8,128)}, f32[64,8192]{1,0:T(8,128)}, f32[64,8192]{1,0:T(8,128)}) custom-call(s32[7,64]{1,0:T(8,128)} %stack.32.index, bf16[64,2,256,256]{3,2,1,0:T(8,128)(2,1)} %get-tuple-element.53.tiles, f32[64,16384]{1,0:T(8,128)} %all-gather.2.cloned.1.call-done.refs_0_, f32[2,64,1024]{2,1,0:T(8,128)} %copy-done.9, ...), custom_call_target="tpu_custom_call" | custom-call | flops 3221225472 | bytes 29360128 | tf_op jit(solution)/shard_map/slope_products/pallas_call | solution.py:243
  109.1 2.9 collective-permute-start.11
  112.3 2.4 collective-permute-start.13
  115.6 1.7 slice_add_fusion.6
  117.4 1.6 collective-permute-start.15
  119.0 6.7 %collective-permute-done.11 = f32[2,64,1024]{2,1,0:T(8,128)S(1)} collective-permute-done((f32[2,64,1024]{2,1,0:T(8,128)}, f32[2,64,1024]{2,1,0:T(8,128)S(1)}, u32[]{:S(2)}, u32[]{:S(2)}) %collective-permute-start.11) | collective-permute-done | bytes 524320 | tf_op jit(solution)/shard_map/ppermute | solution.py:29
  126.3 15.8 %collective-permute-done.12 = f32[2,64,1024]{2,1,0:T(8,128)S(1)} collective-permute-done((f32[2,64,1024]{2,1,0:T(8,128)}, f32[2,64,1024]{2,1,0:T(8,128)S(1)}, u32[]{:S(2)}, u32[]{:S(2)}) %collective-permute-start.12) | collective-permute-done | bytes 524320 | tf_op jit(solution)/shard_map/ppermute | solution.py:29
  142.1 2.6 collective-permute-start.17
  144.9 2.0 collective-permute-start.18
  146.9 8.7 %collective-permute-done.17 = f32[2,64,1024]{2,1,0:T(8,128)S(1)} collective-permute-done((f32[2,64,1024]{2,1,0:T(8,128)S(1)}, f32[2,64,1024]{2,1,0:T(8,128)S(1)}, u32[]{:S(2)}, u32[]{:S(2)}) %collective-permute-start.17) | collective-permute-done | bytes 524320 | tf_op jit(solution)/shard_map/ppermute | solution.py:25
  155.6 1.5 fusion.5.refs_1_
  157.2 4.5 gather_fusion
  161.7 4.0 collective-permute-done.19.refs_3_
  165.7 2.2 copy-done.3
  169.0 1.6 collective-permute-start.20
  172.2 1.8 collective-permute-done.21
  174.3 2.2 collective-permute-done.22
  176.5 2.1 collective-permute-start.23
  178.6 2.4 collective-permute-done.23
  181.1 2.5 collective-permute-start.24
  183.5 1.6 collective-permute-done.24
  185.1 2.9 collective-permute-done.25
  189.2 3.1 collective-permute-done.26
  193.5 2.7 collective-permute-start.35
  196.2 2.4 collective-permute-done.27
  198.5 4.1 collective-permute-done.35
  204.1 2.1 collective-permute-start.29
  206.8 8.3 %collective-permute-start.31 = (f32[2,64,1024]{2,1,0:T(8,128)S(1)}, f32[2,64,1024]{2,1,0:T(8,128)S(1)}, u32[]{:S(2)}, u32[]{:S(2)}) collective-permute-start(f32[2,64,1024]{2,1,0:T(8,128)S(1)} %get-tuple-element.74.refs_0_), channel_id=1, source_target_pairs={{0,1},{1,0},{2,3},{3,2},{4,5},{5,4},{6,7},{7,6},{8,9},{9,8},{10,11... | collective-permute-start | bytes 1572872 | tf_op jit(solution)/shard_map/ppermute | solution.py:33
  216.1 5.4 %collective-permute-done.29.refs_2_ = f32[2,64,1024]{2,1,0:T(8,128)S(1)} collective-permute-done((f32[2,64,1024]{2,1,0:T(8,128)S(1)}, f32[2,64,1024]{2,1,0:T(8,128)S(1)}, u32[]{:S(2)}, u32[]{:S(2)}) %collective-permute-start.29) | collective-permute-done | bytes 524320 | tf_op jit(solution)/shard_map/ppermute | solution.py:25
  221.7 3.7 collective-permute-done.30.refs_3_
  225.4 8.0 %collective-permute-start.32 = (f32[2,64,1024]{2,1,0:T(8,128)S(1)}, f32[2,64,1024]{2,1,0:T(8,128)}, u32[]{:S(2)}, u32[]{:S(2)}) collective-permute-start(f32[2,64,1024]{2,1,0:T(8,128)S(1)} %collective-permute-done.28.refs_1_), channel_id=1, source_target_pairs={{0,1},{1,0},{2,3},{3,2},{4,5},{5,4},{6,7},{7,6},{8,9},{9,8},{10,11... | collective-permute-start | bytes 1572872 | tf_op jit(solution)/shard_map/ppermute | solution.py:33
  233.8 7.2 %collective-permute-done.36.refs_9_ = f32[2,64,1024]{2,1,0:T(8,128)S(1)} collective-permute-done((f32[2,64,1024]{2,1,0:T(8,128)S(1)}, f32[2,64,1024]{2,1,0:T(8,128)S(1)}, u32[]{:S(2)}, u32[]{:S(2)}) %collective-permute-start.36) | collective-permute-done | bytes 524320 | tf_op jit(solution)/shard_map/ppermute | solution.py:29
  241.9 3.1 add.432
  246.3 17.3 %kernel_products.3 = (f32[8,64,1024]{2,1,0:T(8,128)}, f32[8,64,1024]{2,1,0:T(8,128)}, f32[2,64,1024]{2,1,0:T(8,128)}, f32[2,64,1024]{2,1,0:T(8,128)}, f32[2,64,1024]{2,1,0:T(8,128)}, /*index=5*/f32[2,64,1024]{2,1,0:T(8,128)}) custom-call(s32[7,64]{1,0:T(8,128)} %stack.26.index, bf16[64,2,256,256]{3,2,1,0:T(8,128)(2,1)} %get-tuple-element.33.tiles, ...), custom_call_target="tpu_custom_call" | custom-call | flops 3221225472 | bytes 29360128 | tf_op jit(solution)/shard_map/kernel_products/pallas_call | solution.py:243
  265.0 2.7 collective-permute-start.41
  268.6 1.7 slice_add_fusion.2
  270.3 1.7 collective-permute-start.43
  272.0 7.8 %collective-permute-done.39 = f32[2,64,1024]{2,1,0:T(8,128)S(1)} collective-permute-done((f32[2,64,1024]{2,1,0:T(8,128)}, f32[2,64,1024]{2,1,0:T(8,128)S(1)}, u32[]{:S(2)}, u32[]{:S(2)}) %collective-permute-start.39) | collective-permute-done | bytes 524320 | tf_op jit(solution)/shard_map/ppermute | solution.py:29
  280.2 11.3 %collective-permute-done.40 = f32[2,64,1024]{2,1,0:T(8,128)S(1)} collective-permute-done((f32[2,64,1024]{2,1,0:T(8,128)}, f32[2,64,1024]{2,1,0:T(8,128)S(1)}, u32[]{:S(2)}, u32[]{:S(2)}) %collective-permute-start.40) | collective-permute-done | bytes 524320 | tf_op jit(solution)/shard_map/ppermute | solution.py:29
  292.3 4.7 collective-permute-done.44
  297.1 7.2 %collective-permute-done.45 = f32[2,64,1024]{2,1,0:T(8,128)S(1)} collective-permute-done((f32[2,64,1024]{2,1,0:T(8,128)S(1)}, f32[2,64,1024]{2,1,0:T(8,128)S(1)}, u32[]{:S(2)}, u32[]{:S(2)}) %collective-permute-start.45) | collective-permute-done | bytes 524320 | tf_op jit(solution)/shard_map/ppermute | solution.py:25
  305.6 2.1 collective-permute-start.47
  307.7 6.2 %collective-permute-done.47.refs_3_ = f32[64,1024]{1,0:T(8,128)S(1)} collective-permute-done((f32[64,1024]{1,0:T(8,128)S(1)}, f32[64,1024]{1,0:T(8,128)S(1)}, u32[]{:S(2)}, u32[]{:S(2)}) %collective-permute-start.47) | collective-permute-done | bytes 262176 | tf_op jit(solution)/shard_map/ppermute | solution.py:37
  316.9 1.5 collective-permute-start.49
  322.0 1.5 collective-permute-start.51
  323.6 2.5 collective-permute-done.51
  326.1 2.0 collective-permute-start.52
  328.1 2.0 collective-permute-done.52
  330.2 2.5 collective-permute-done.53
  332.7 1.4 collective-permute-start.54
  334.1 1.8 add.433
  336.8 128.3 %all-reduce.2.cloned.1.call-done.gram = f32[160,128]{1,0:T(8,128)} async-done(((f32[160,128]{1,0:T(8,128)}), f32[160,128]{1,0:T(8,128)}) %all-reduce.2.cloned.1.call-update) | async-done | bytes 81936 | tf_op jit(solution)/shard_map/psum | solution.py:519
  465.1 2.2 copy-done.6
  468.1 2.2 shard_map.104
  (190 shorter events, 44.3 us)
Async XLA Ops:
  8.0 149.2 %copy-start = (f32[1024]{0:T(1024)S(1)}, f32[1024]{0:T(1024)}, u32[]{:S(2)}) copy-start(f32[1024]{0:T(1024)} %param.10) | copy-start | bytes 12292
  8.0 64.1 %all-gather.2.cloned.1.call-start = ((), (), s32[]{:S(2)}) async-start(), calls=%async_computation.2 | async-start | bytes 4456448 | tf_op jit(solution)/shard_map/all_gather | solution.py:513
  8.8 325.4 %reduce-scatter.5.cloned.1.call-start = ((), (), s32[]{:S(2)}) async-start(), calls=%async_computation.5 | async-start | bytes 2359296 | tf_op jit(solution)/shard_map/reduce_scatter | solution.py:527
  14.2 9.1 %collective-permute-start = (f32[1,8,1024]{2,1,0:T(8,128)S(1)}, f32[1,8,1024]{2,1,0:T(8,128)S(1)}, u32[]{:S(2)}, u32[]{:S(2)}) collective-permute-start(f32[1,8,1024]{2,1,0:T(8,128)S(1)} %get-tuple-element.66), channel_id=1, source_target_pairs={{0,2},{1,3},{2,0},{3,1},{4,6},{5,7},{6,4},{7,5},{8,10},{9,11},{10,... | collective-permute-start | bytes 98312 | tf_op jit(solution)/shard_map/ppermute | solution.py:55
  16.7 6.6 %collective-permute-start.4 = (f32[1,8,1024]{2,1,0:T(8,128)S(1)}, f32[1,8,1024]{2,1,0:T(8,128)S(1)}, u32[]{:S(2)}, u32[]{:S(2)}) collective-permute-start(f32[1,8,1024]{2,1,0:T(8,128)S(1)} %get-tuple-element.66), channel_id=1, source_target_pairs={{0,16},{16,0},{32,48},{48,32},{64,80},{80,64},{96,112},{112,96},{1... | collective-permute-start | bytes 98312 | tf_op jit(solution)/shard_map/ppermute | solution.py:58
  20.0 14.6 %collective-permute-start.7 = (f32[64,1024]{1,0:T(8,128)}, f32[64,1024]{1,0:T(8,128)S(1)}, u32[]{:S(2)}, u32[]{:S(2)}) collective-permute-start(f32[64,1024]{1,0:T(8,128)} %first.4), channel_id=1, source_target_pairs={{0,16},{16,0},{32,48},{48,32},{64,80},{80,64},{96,112},{112,96},{1... | collective-permute-start | bytes 786440 | tf_op jit(solution)/shard_map/ppermute | solution.py:41
  23.3 5.0 %collective-permute-start.1 = (f32[2,8,1024]{2,1,0:T(8,128)S(1)}, f32[2,8,1024]{2,1,0:T(8,128)S(1)}, u32[]{:S(2)}, u32[]{:S(2)}) collective-permute-start(f32[2,8,1024]{2,1,0:T(8,128)S(1)} %get-tuple-element.80), channel_id=1, source_target_pairs={{0,4},{1,5},{2,6},{3,7},{4,0},{5,1},{6,2},{7,3},{8,12},{9,13},{10,... | collective-permute-start | bytes 196616 | tf_op jit(solution)/shard_map/ppermute | solution.py:55
  24.7 3.6 collective-permute-start.5
  28.3 9.2 %collective-permute-start.2 = (f32[4,8,1024]{2,1,0:T(8,128)S(1)}, f32[4,8,1024]{2,1,0:T(8,128)S(1)}, u32[]{:S(2)}, u32[]{:S(2)}) collective-permute-start(f32[4,8,1024]{2,1,0:T(8,128)S(1)} %get-tuple-element.78), channel_id=1, source_target_pairs={{0,8},{1,9},{2,10},{3,11},{4,12},{5,13},{6,14},{7,15},{8,0},{9,1},... | collective-permute-start | bytes 393224 | tf_op jit(solution)/shard_map/ppermute | solution.py:55
  31.2 6.3 %collective-permute-start.6 = (f32[4,8,1024]{2,1,0:T(8,128)S(1)}, f32[4,8,1024]{2,1,0:T(8,128)}, u32[]{:S(2)}, u32[]{:S(2)}) collective-permute-start(f32[4,8,1024]{2,1,0:T(8,128)S(1)} %get-tuple-element.77), channel_id=1, source_target_pairs={{0,64},{16,80},{32,96},{48,112},{64,0},{80,16},{96,32},{112,48},{1... | collective-permute-start | bytes 393224 | tf_op jit(solution)/shard_map/ppermute | solution.py:58
  34.7 37.4 %collective-permute-start.10 = (f32[2,64,1024]{2,1,0:T(8,128)S(1)}, f32[2,64,1024]{2,1,0:T(8,128)S(1)}, u32[]{:S(2)}, u32[]{:S(2)}) collective-permute-start(f32[2,64,1024]{2,1,0:T(8,128)S(1)} %pad_maximum_fusion.2.refs_1_), channel_id=1, source_target_pairs={{0,96},{16,112},{32,0},{48,16},{64,32},{80,48},{96,64},{112,80},{1... | collective-permute-start | bytes 1572872 | tf_op jit(solution)/shard_map/ppermute | solution.py:29
  35.7 36.4 %collective-permute-start.8 = (f32[2,64,1024]{2,1,0:T(8,128)S(1)}, f32[2,64,1024]{2,1,0:T(8,128)S(1)}, u32[]{:S(2)}, u32[]{:S(2)}) collective-permute-start(f32[2,64,1024]{2,1,0:T(8,128)S(1)} %pad_maximum_fusion.2.refs_1_), channel_id=1, source_target_pairs={{0,32},{16,48},{32,64},{48,80},{64,96},{80,112},{96,0},{112,16},{1... | collective-permute-start | bytes 1572872 | tf_op jit(solution)/shard_map/ppermute | solution.py:29
  36.2 35.9 %collective-permute-start.9 = (f32[2,64,1024]{2,1,0:T(8,128)S(1)}, f32[2,64,1024]{2,1,0:T(8,128)S(1)}, u32[]{:S(2)}, u32[]{:S(2)}) collective-permute-start(f32[2,64,1024]{2,1,0:T(8,128)S(1)} %pad_maximum_fusion.2.refs_1_), channel_id=1, source_target_pairs={{0,64},{16,80},{32,96},{48,112},{64,0},{80,16},{96,32},{112,48},{1... | collective-permute-start | bytes 1572872 | tf_op jit(solution)/shard_map/ppermute | solution.py:29
  38.5 5.2 %collective-permute-start.3 = (f32[8,8,1024]{2,1,0:T(8,128)S(1)}, f32[8,8,1024]{2,1,0:T(8,128)S(1)}, u32[]{:S(2)}, u32[]{:S(2)}) collective-permute-start(f32[8,8,1024]{2,1,0:T(8,128)S(1)} %get-tuple-element.76), channel_id=1, source_target_pairs={{0,1},{1,0},{2,3},{3,2},{4,5},{5,4},{6,7},{7,6},{8,9},{9,8},{10,11... | collective-permute-start | bytes 786440 | tf_op jit(solution)/shard_map/ppermute | solution.py:55
  90.5 25.1 %collective-permute-start.14 = (f32[8,64,1024]{2,1,0:T(8,128)}, f32[8,64,1024]{2,1,0:T(8,128)}, u32[]{:S(2)}, u32[]{:S(2)}) collective-permute-start(f32[8,64,1024]{2,1,0:T(8,128)} %get-tuple-element.39), channel_id=1, source_target_pairs={{0,1},{1,0},{2,3},{3,2},{4,5},{5,4},{6,7},{7,6},{8,9},{9,8},{10,11... | collective-permute-start | bytes 6291464 | tf_op jit(solution)/shard_map/ppermute | solution.py:33
  109.1 225.1 %reduce-scatter.3.cloned.1.call-start = ((), (), s32[]{:S(2)}) async-start(), calls=%async_computation.4 | async-start | bytes 2359296 | tf_op jit(solution)/shard_map/reduce_scatter | solution.py:529
  109.1 16.6 %collective-permute-start.11 = (f32[2,64,1024]{2,1,0:T(8,128)}, f32[2,64,1024]{2,1,0:T(8,128)S(1)}, u32[]{:S(2)}, u32[]{:S(2)}) collective-permute-start(f32[2,64,1024]{2,1,0:T(8,128)} %get-tuple-element.35), channel_id=1, source_target_pairs={{0,64},{16,80},{32,96},{48,112},{64,0},{80,16},{96,32},{112,48},{1... | collective-permute-start | bytes 1572872 | tf_op jit(solution)/shard_map/ppermute | solution.py:29
  112.0 30.1 %collective-permute-start.12 = (f32[2,64,1024]{2,1,0:T(8,128)}, f32[2,64,1024]{2,1,0:T(8,128)S(1)}, u32[]{:S(2)}, u32[]{:S(2)}) collective-permute-start(f32[2,64,1024]{2,1,0:T(8,128)} %get-tuple-element.36), channel_id=1, source_target_pairs={{0,32},{16,48},{32,64},{48,80},{64,96},{80,112},{96,0},{112,16},{1... | collective-permute-start | bytes 1572872 | tf_op jit(solution)/shard_map/ppermute | solution.py:29
  112.3 32.4 %collective-permute-start.13 = (f32[2,64,1024]{2,1,0:T(8,128)S(1)}, f32[2,64,1024]{2,1,0:T(8,128)S(1)}, u32[]{:S(2)}, u32[]{:S(2)}) collective-permute-start(f32[2,64,1024]{2,1,0:T(8,128)S(1)} %copy-done.30), channel_id=1, source_target_pairs={{0,96},{16,112},{32,0},{48,16},{64,32},{80,48},{96,64},{112,80},{1... | collective-permute-start | bytes 1572872 | tf_op jit(solution)/shard_map/ppermute | solution.py:29
  114.7 100.4 %collective-permute-start.55 = (f32[64,8192]{1,0:T(8,128)}, f32[64,8192]{1,0:T(8,128)}, u32[]{:S(2)}, u32[]{:S(2)}) collective-permute-start(f32[64,8192]{1,0:T(8,128)} %get-tuple-element.55), channel_id=1, source_target_pairs={{0,1},{1,0},{2,3},{3,2},{4,5},{5,4},{6,7},{7,6},{8,9},{9,8},{10,11... | collective-permute-start | bytes 6291464 | tf_op jit(solution)/shard_map/ppermute | solution.py:33
  117.4 29.5 %collective-permute-start.15 = (f32[2,64,1024]{2,1,0:T(8,128)S(1)}, f32[2,64,1024]{2,1,0:T(8,128)S(1)}, u32[]{:S(2)}, u32[]{:S(2)}) collective-permute-start(f32[2,64,1024]{2,1,0:T(8,128)S(1)} %get-tuple-element.70), channel_id=1, source_target_pairs={{0,8},{1,9},{2,10},{3,11},{4,12},{5,13},{6,14},{7,15},{8,0},{9,1},... | collective-permute-start | bytes 1572872 | tf_op jit(solution)/shard_map/ppermute | solution.py:25
  125.7 21.2 %collective-permute-start.16 = (f32[2,64,1024]{2,1,0:T(8,128)S(1)}, f32[2,64,1024]{2,1,0:T(8,128)S(1)}, u32[]{:S(2)}, u32[]{:S(2)}) collective-permute-start(f32[2,64,1024]{2,1,0:T(8,128)S(1)} %get-tuple-element.72), channel_id=1, source_target_pairs={{0,4},{1,5},{2,6},{3,7},{4,8},{5,9},{6,10},{7,11},{8,12},{9,13},{1... | collective-permute-start | bytes 1572872 | tf_op jit(solution)/shard_map/ppermute | solution.py:25
  142.1 13.5 %collective-permute-start.17 = (f32[2,64,1024]{2,1,0:T(8,128)S(1)}, f32[2,64,1024]{2,1,0:T(8,128)S(1)}, u32[]{:S(2)}, u32[]{:S(2)}) collective-permute-start(f32[2,64,1024]{2,1,0:T(8,128)S(1)} %get-tuple-element.71), channel_id=1, source_target_pairs={{0,12},{1,13},{2,14},{3,15},{4,0},{5,1},{6,2},{7,3},{8,4},{9,5},{1... | collective-permute-start | bytes 1572872 | tf_op jit(solution)/shard_map/ppermute | solution.py:25
  144.9 16.8 %collective-permute-start.18 = (f32[64,1024]{1,0:T(8,128)S(1)}, f32[64,1024]{1,0:T(8,128)S(1)}, u32[]{:S(2)}, u32[]{:S(2)}) collective-permute-start(f32[64,1024]{1,0:T(8,128)S(1)} %slice_bitcast_fusion.3), channel_id=1, source_target_pairs={{0,16},{16,0},{32,48},{48,32},{64,80},{80,64},{96,112},{112,96},{1... | collective-permute-start | bytes 786440 | tf_op jit(solution)/shard_map/ppermute | solution.py:41
  157.1 8.7 %collective-permute-start.19 = (f32[64,1024]{1,0:T(8,128)S(1)}, f32[64,1024]{1,0:T(8,128)S(1)}, u32[]{:S(2)}, u32[]{:S(2)}) collective-permute-start(f32[64,1024]{1,0:T(8,128)S(1)} %slice_bitcast_fusion.2), channel_id=1, source_target_pairs={{0,2},{1,3},{2,0},{3,1},{4,6},{5,7},{6,4},{7,5},{8,10},{9,11},{10,... | collective-permute-start | bytes 786440 | tf_op jit(solution)/shard_map/ppermute | solution.py:37
  169.0 2.4 collective-permute-start.20
  171.4 2.5 collective-permute-start.21
  174.0 2.5 collective-permute-start.22
  176.5 4.5 collective-permute-start.23
  181.1 4.0 collective-permute-start.24
  185.1 3.0 collective-permute-start.25
  188.1 4.1 collective-permute-start.26
  192.2 49.6 %copy-start.10 = (f32[64,8192]{1,0:T(8,128)S(1)}, f32[64,8192]{1,0:T(8,128)}, u32[]{:S(2)}) copy-start(f32[64,8192]{1,0:T(8,128)} %get-tuple-element.54) | copy-start | bytes 6291460
  193.2 5.3 %collective-permute-start.27 = (f32[64,1024]{1,0:T(8,128)S(1)}, f32[64,1024]{1,0:T(8,128)S(1)}, u32[]{:S(2)}, u32[]{:S(2)}) collective-permute-start(f32[64,1024]{1,0:T(8,128)S(1)} %shard_map.103.refs_5_.second), channel_id=1, source_target_pairs={{0,2},{1,3},{2,0},{3,1},{4,6},{5,7},{6,4},{7,5},{8,10},{9,11},{10,... | collective-permute-start | bytes 786440 | tf_op jit(solution)/shard_map/ppermute | solution.py:37
  193.5 9.2 %collective-permute-start.35 = (f32[64,1024]{1,0:T(8,128)S(1)}, f32[64,1024]{1,0:T(8,128)S(1)}, u32[]{:S(2)}, u32[]{:S(2)}) collective-permute-start(f32[64,1024]{1,0:T(8,128)S(1)} %shard_map.103.refs_5_.second), channel_id=1, source_target_pairs={{0,16},{16,0},{32,48},{48,32},{64,80},{80,64},{96,112},{112,96},{1... | collective-permute-start | bytes 786440 | tf_op jit(solution)/shard_map/ppermute | solution.py:41
  202.8 42.2 %copy-start.11 = (f32[2,64,1024]{2,1,0:T(8,128)}, f32[2,64,1024]{2,1,0:T(8,128)S(1)}, u32[]{:S(2)}) copy-start(f32[2,64,1024]{2,1,0:T(8,128)S(1)} %get-tuple-element.73.refs_8_) | copy-start | bytes 1572868
  202.8 42.2 %copy-start.12 = (f32[2,64,1024]{2,1,0:T(8,128)}, f32[2,64,1024]{2,1,0:T(8,128)S(1)}, u32[]{:S(2)}) copy-start(f32[2,64,1024]{2,1,0:T(8,128)S(1)} %get-tuple-element.74.refs_0_) | copy-start | bytes 1572868
  202.8 12.4 %collective-permute-start.28 = (f32[2,64,1024]{2,1,0:T(8,128)S(1)}, f32[2,64,1024]{2,1,0:T(8,128)S(1)}, u32[]{:S(2)}, u32[]{:S(2)}) collective-permute-start(f32[2,64,1024]{2,1,0:T(8,128)S(1)} %get-tuple-element.74.refs_0_), channel_id=1, source_target_pairs={{0,4},{1,5},{2,6},{3,7},{4,8},{5,9},{6,10},{7,11},{8,12},{9,13},{1... | collective-permute-start | bytes 1572872 | tf_op jit(solution)/shard_map/ppermute | solution.py:25
  204.1 17.4 %collective-permute-start.29 = (f32[2,64,1024]{2,1,0:T(8,128)S(1)}, f32[2,64,1024]{2,1,0:T(8,128)S(1)}, u32[]{:S(2)}, u32[]{:S(2)}) collective-permute-start(f32[2,64,1024]{2,1,0:T(8,128)S(1)} %get-tuple-element.74.refs_0_), channel_id=1, source_target_pairs={{0,8},{1,9},{2,10},{3,11},{4,12},{5,13},{6,14},{7,15},{8,0},{9,1},... | collective-permute-start | bytes 1572872 | tf_op jit(solution)/shard_map/ppermute | solution.py:25
  206.1 19.3 %collective-permute-start.30 = (f32[2,64,1024]{2,1,0:T(8,128)S(1)}, f32[2,64,1024]{2,1,0:T(8,128)S(1)}, u32[]{:S(2)}, u32[]{:S(2)}) collective-permute-start(f32[2,64,1024]{2,1,0:T(8,128)S(1)} %get-tuple-element.74.refs_0_), channel_id=1, source_target_pairs={{0,12},{1,13},{2,14},{3,15},{4,0},{5,1},{6,2},{7,3},{8,4},{9,5},{1... | collective-permute-start | bytes 1572872 | tf_op jit(solution)/shard_map/ppermute | solution.py:25
  206.8 26.7 %collective-permute-start.31 = (f32[2,64,1024]{2,1,0:T(8,128)S(1)}, f32[2,64,1024]{2,1,0:T(8,128)S(1)}, u32[]{:S(2)}, u32[]{:S(2)}) collective-permute-start(f32[2,64,1024]{2,1,0:T(8,128)S(1)} %get-tuple-element.74.refs_0_), channel_id=1, source_target_pairs={{0,1},{1,0},{2,3},{3,2},{4,5},{5,4},{6,7},{7,6},{8,9},{9,8},{10,11... | collective-permute-start | bytes 1572872 | tf_op jit(solution)/shard_map/ppermute | solution.py:33
  215.1 25.9 %collective-permute-start.36 = (f32[2,64,1024]{2,1,0:T(8,128)S(1)}, f32[2,64,1024]{2,1,0:T(8,128)S(1)}, u32[]{:S(2)}, u32[]{:S(2)}) collective-permute-start(f32[2,64,1024]{2,1,0:T(8,128)S(1)} %get-tuple-element.73.refs_8_), channel_id=1, source_target_pairs={{0,32},{16,48},{32,64},{48,80},{64,96},{80,112},{96,0},{112,16},{1... | collective-permute-start | bytes 1572872 | tf_op jit(solution)/shard_map/ppermute | solution.py:29
  215.2 31.1 %collective-permute-start.37 = (f32[2,64,1024]{2,1,0:T(8,128)S(1)}, f32[2,64,1024]{2,1,0:T(8,128)}, u32[]{:S(2)}, u32[]{:S(2)}) collective-permute-start(f32[2,64,1024]{2,1,0:T(8,128)S(1)} %get-tuple-element.73.refs_8_), channel_id=1, source_target_pairs={{0,64},{16,80},{32,96},{48,112},{64,0},{80,16},{96,32},{112,48},{1... | collective-permute-start | bytes 1572872 | tf_op jit(solution)/shard_map/ppermute | solution.py:29
  221.5 24.8 %collective-permute-start.38 = (f32[2,64,1024]{2,1,0:T(8,128)S(1)}, f32[2,64,1024]{2,1,0:T(8,128)}, u32[]{:S(2)}, u32[]{:S(2)}) collective-permute-start(f32[2,64,1024]{2,1,0:T(8,128)S(1)} %get-tuple-element.73.refs_8_), channel_id=1, source_target_pairs={{0,96},{16,112},{32,0},{48,16},{64,32},{80,48},{96,64},{112,80},{1... | collective-permute-start | bytes 1572872 | tf_op jit(solution)/shard_map/ppermute | solution.py:29
  225.4 20.9 %collective-permute-start.32 = (f32[2,64,1024]{2,1,0:T(8,128)S(1)}, f32[2,64,1024]{2,1,0:T(8,128)}, u32[]{:S(2)}, u32[]{:S(2)}) collective-permute-start(f32[2,64,1024]{2,1,0:T(8,128)S(1)} %collective-permute-done.28.refs_1_), channel_id=1, source_target_pairs={{0,1},{1,0},{2,3},{3,2},{4,5},{5,4},{6,7},{7,6},{8,9},{9,8},{10,11... | collective-permute-start | bytes 1572872 | tf_op jit(solution)/shard_map/ppermute | solution.py:33
  233.5 12.9 %collective-permute-start.33 = (f32[2,64,1024]{2,1,0:T(8,128)S(1)}, f32[2,64,1024]{2,1,0:T(8,128)}, u32[]{:S(2)}, u32[]{:S(2)}) collective-permute-start(f32[2,64,1024]{2,1,0:T(8,128)S(1)} %collective-permute-done.29.refs_2_), channel_id=1, source_target_pairs={{0,1},{1,0},{2,3},{3,2},{4,5},{5,4},{6,7},{7,6},{8,9},{9,8},{10,11... | collective-permute-start | bytes 1572872 | tf_op jit(solution)/shard_map/ppermute | solution.py:33
  241.0 5.4 %collective-permute-start.34 = (f32[2,64,1024]{2,1,0:T(8,128)S(1)}, f32[2,64,1024]{2,1,0:T(8,128)}, u32[]{:S(2)}, u32[]{:S(2)}) collective-permute-start(f32[2,64,1024]{2,1,0:T(8,128)S(1)} %collective-permute-done.30.refs_3_), channel_id=1, source_target_pairs={{0,1},{1,0},{2,3},{3,2},{4,5},{5,4},{6,7},{7,6},{8,9},{9,8},{10,11... | collective-permute-start | bytes 1572872 | tf_op jit(solution)/shard_map/ppermute | solution.py:33
  245.1 220.0 %all-reduce.2.cloned.1.call-start = ((), (), s32[]{:S(2)}) async-start(), calls=%async_computation.3 | async-start | bytes 163840 | tf_op jit(solution)/shard_map/psum | solution.py:519
  263.7 4.9 %collective-permute-start.42 = (f32[8,64,1024]{2,1,0:T(8,128)}, f32[8,64,1024]{2,1,0:T(8,128)S(1)}, u32[]{:S(2)}, u32[]{:S(2)}) collective-permute-start(f32[8,64,1024]{2,1,0:T(8,128)} %get-tuple-element.47), channel_id=1, source_target_pairs={{0,1},{1,0},{2,3},{3,2},{4,5},{5,4},{6,7},{7,6},{8,9},{9,8},{10,11... | collective-permute-start | bytes 6291464 | tf_op jit(solution)/shard_map/ppermute | solution.py:33
  264.6 15.3 %collective-permute-start.39 = (f32[2,64,1024]{2,1,0:T(8,128)}, f32[2,64,1024]{2,1,0:T(8,128)S(1)}, u32[]{:S(2)}, u32[]{:S(2)}) collective-permute-start(f32[2,64,1024]{2,1,0:T(8,128)} %get-tuple-element.43), channel_id=1, source_target_pairs={{0,64},{16,80},{32,96},{48,112},{64,0},{80,16},{96,32},{112,48},{1... | collective-permute-start | bytes 1572872 | tf_op jit(solution)/shard_map/ppermute | solution.py:29
  265.0 26.5 %collective-permute-start.40 = (f32[2,64,1024]{2,1,0:T(8,128)}, f32[2,64,1024]{2,1,0:T(8,128)S(1)}, u32[]{:S(2)}, u32[]{:S(2)}) collective-permute-start(f32[2,64,1024]{2,1,0:T(8,128)} %get-tuple-element.44), channel_id=1, source_target_pairs={{0,32},{16,48},{32,64},{48,80},{64,96},{80,112},{96,0},{112,16},{1... | collective-permute-start | bytes 1572872 | tf_op jit(solution)/shard_map/ppermute | solution.py:29
  265.0 26.5 %collective-permute-start.41 = (f32[2,64,1024]{2,1,0:T(8,128)}, f32[2,64,1024]{2,1,0:T(8,128)S(1)}, u32[]{:S(2)}, u32[]{:S(2)}) collective-permute-start(f32[2,64,1024]{2,1,0:T(8,128)} %get-tuple-element.45), channel_id=1, source_target_pairs={{0,96},{16,112},{32,0},{48,16},{64,32},{80,48},{96,64},{112,80},{1... | collective-permute-start | bytes 1572872 | tf_op jit(solution)/shard_map/ppermute | solution.py:29
  270.3 22.0 %collective-permute-start.43 = (f32[2,64,1024]{2,1,0:T(8,128)S(1)}, f32[2,64,1024]{2,1,0:T(8,128)S(1)}, u32[]{:S(2)}, u32[]{:S(2)}) collective-permute-start(f32[2,64,1024]{2,1,0:T(8,128)S(1)} %get-tuple-element.67), channel_id=1, source_target_pairs={{0,8},{1,9},{2,10},{3,11},{4,12},{5,13},{6,14},{7,15},{8,0},{9,1},... | collective-permute-start | bytes 1572872 | tf_op jit(solution)/shard_map/ppermute | solution.py:25
  272.0 25.1 %collective-permute-start.44 = (f32[2,64,1024]{2,1,0:T(8,128)S(1)}, f32[2,64,1024]{2,1,0:T(8,128)S(1)}, u32[]{:S(2)}, u32[]{:S(2)}) collective-permute-start(f32[2,64,1024]{2,1,0:T(8,128)S(1)} %get-tuple-element.69), channel_id=1, source_target_pairs={{0,4},{1,5},{2,6},{3,7},{4,8},{5,9},{6,10},{7,11},{8,12},{9,13},{1... | collective-permute-start | bytes 1572872 | tf_op jit(solution)/shard_map/ppermute | solution.py:25
  279.8 24.5 %collective-permute-start.45 = (f32[2,64,1024]{2,1,0:T(8,128)S(1)}, f32[2,64,1024]{2,1,0:T(8,128)S(1)}, u32[]{:S(2)}, u32[]{:S(2)}) collective-permute-start(f32[2,64,1024]{2,1,0:T(8,128)S(1)} %get-tuple-element.68), channel_id=1, source_target_pairs={{0,12},{1,13},{2,14},{3,15},{4,0},{5,1},{6,2},{7,3},{8,4},{9,5},{1... | collective-permute-start | bytes 1572872 | tf_op jit(solution)/shard_map/ppermute | solution.py:25
  291.7 16.0 %collective-permute-start.46 = (f32[64,1024]{1,0:T(8,128)S(1)}, f32[64,1024]{1,0:T(8,128)S(1)}, u32[]{:S(2)}, u32[]{:S(2)}) collective-permute-start(f32[64,1024]{1,0:T(8,128)S(1)} %slice_bitcast_fusion.1), channel_id=1, source_target_pairs={{0,16},{16,0},{32,48},{48,32},{64,80},{80,64},{96,112},{112,96},{1... | collective-permute-start | bytes 786440 | tf_op jit(solution)/shard_map/ppermute | solution.py:41
  305.6 8.3 %collective-permute-start.47 = (f32[64,1024]{1,0:T(8,128)S(1)}, f32[64,1024]{1,0:T(8,128)S(1)}, u32[]{:S(2)}, u32[]{:S(2)}) collective-permute-start(f32[64,1024]{1,0:T(8,128)S(1)} %slice_bitcast_fusion), channel_id=1, source_target_pairs={{0,2},{1,3},{2,0},{3,1},{4,6},{5,7},{6,4},{7,5},{8,10},{9,11},{10,... | collective-permute-start | bytes 786440 | tf_op jit(solution)/shard_map/ppermute | solution.py:37
  315.0 1.9 collective-permute-start.48
  316.9 2.5 collective-permute-start.49
  319.5 2.5 collective-permute-start.50
  322.0 4.0 collective-permute-start.51
  326.1 4.0 collective-permute-start.52
  330.2 2.5 collective-permute-start.53
  332.7 4.0 collective-permute-start.54
  (28 other events, 401.9 us)
Sparse Core Ops, SparseCore 0:
  10.5 44.2 all-gather.1
  109.2 81.2 reduce-scatter.4
  245.2 58.0 reduce-scatter.2
Sparse Core Ops, SparseCore 1:
  323.7 141.3 all-reduce.1

commit v3 on v0

--- a/solution.py
+++ b/solution.py
@@ -410,8 +410,8 @@
     beta = jnp.sqrt(jnp.maximum(rest_sq, 0.0) + EPSILON)
     held[...] = turned(jnp.concatenate([scale, next_along, beside], axis=0) / beta)
     coefficients[...] = jnp.concatenate(
-        [along[16:17], jnp.sqrt(norm_sq), alpha, beta, jnp.zeros((4, 128), F32)], axis=0
-    )
+        [along[16:17], jnp.sqrt(norm_sq), alpha, beta], axis=0
+    )[:, :64]
 
     @row_blocks_of(out.shape[0])
     def _(at):
@@ -422,7 +422,7 @@
     rows, lanes = image.shape
     out_shape = [jax.ShapeDtypeStruct((rows, lanes), F32)]
     if with_coefficients:
-        out_shape.append(jax.ShapeDtypeStruct((8, 128), F32))
+        out_shape.append(jax.ShapeDtypeStruct((4, 64), F32))
     return pl.pallas_call(
         functools.partial(kernel, float(total)),
         out_shape=tuple(out_shape),
@@ -482,6 +482,14 @@
 
     row_points, col_points = gather_points(arranged)
     row_xor, col_xor = row_owner ^ col_at, col_owner ^ row_at
+    slope_to = core_rel * 8 + (row_owner >> 1)
+    row_points, slope_table, next_table = lax.optimization_barrier(
+        (
+            row_points,
+            table(row_owner, col_from, slope_to, col_owner),
+            table(row_from, col_from, row_to, col_to),
+        )
+    )
     kern, slope = make_tiles(
         ((row_xor & 1) * 8 + (row_xor >> 1)) * 1024 + row_sub * BLOCK,
         col_xor * 1024 + col_sub * BLOCK,
@@ -501,9 +509,8 @@
     col_in = gather_row_group(current)
     parts = products(first_table, kern, row_in, col_in, False)
     pieces = reduce_parts(parts)
-    slope_to = core_rel * 8 + (row_owner >> 1)
     row_keep, row_send, col_part = products(
-        table(row_owner, col_from, slope_to, col_owner), slope, row_in, col_in, True
+        slope_table, slope, row_in, col_in, True
     )
     col_sum = lax.psum_scatter(col_part, "row", scatter_dimension=1, tiled=True)
     row_part = row_keep + flip_core(row_send)
@@ -523,7 +530,7 @@
 
     row_in = gather_col_group(rest)
     col_in = gather_row_group(rest)
-    parts = products(table(row_from, col_from, row_to, col_to), kern, row_in, col_in, False)
+    parts = products(next_table, kern, row_in, col_in, False)
     pieces = reduce_parts(parts)
     image, next_sums = image_dots(basis_vectors, noise, pieces, [current, rest])
     next_sums = sum_everywhere(next_sums)
@@ -536,7 +543,7 @@
         [current, rest],
         True,
     )
-    return (lanczos_next, rows[:4, :64], gradient_product)
+    return (lanczos_next, rows, gradient_product)
 
 
 def solution(mesh):

time: 476 us -> 474 us (level)
  waiting for transfers between devices: 256 us -> 263 us
  starting transfers between devices: 84.3 us -> 77.4 us
where the time goes in v3:
time: 474 us
  waiting for transfers between devices  263 us (55%)
  Pallas kernels  84.5 us (18%)
  starting transfers between devices  77.4 us (16%)
  local copies, waits for them, and re-layouts  16.9 us (4%)
  other arithmetic  16.1 us (3%)
  between operations  15.7 us (3%)
    psum x1, waiting for transfers between devices, on_device(): gram = lax.psum(gram, ('row', 'col'))  127 us
    ppermute x12, waiting for transfers between devices, shift_x(): return lax.ppermute(v, 'row', [(i, (i + 2 * s) % 8) for i in range(8)])  52.5 us
    pallas_call x3, Pallas kernels, products(): pl.pallas_call(functools.partial(product_kernel, len(row_in), len(col_in)...  50.4 us
    ppermute x9, waiting for transfers between devices, shift_y(): return lax.ppermute(v, 'col', [(i, (i + 4 * s) % 16) for i in range(16)])  31.4 us
    ppermute x14, waiting for transfers between devices, sum_everywhere(): v = v + lax.ppermute(v, axis, [(i, i ^ bit) for i in range(size)])  30.1 us
    pallas_call x1, Pallas kernels, make_tiles(): pl.pallas_call(tile_kernel, out_shape=(out, out), grid_spec=pltpu.Prefetc...  24.8 us
    ppermute x7, starting transfers between devices, flip_core(): return lax.ppermute(v, 'col', [(i, i ^ 1) for i in range(16)])  15.9 us
    ppermute x14, starting transfers between devices, sum_everywhere(): v = v + lax.ppermute(v, axis, [(i, i ^ bit) for i in range(size)])  14 us
  transfers between devices with their start and end apart: 60, of which 33 were waited for; matrix products, arithmetic and copies ran while one was open for 6% of the time, Pallas kernels for 14%

profile of v3, /device:TPU:1, one launch (start us, length us, event | category | flops | bytes accessed | tf_op | source)
XLA Modules:
  0.0 473.9 jit_solution(6200547234289826906)
XLA Ops:
  10.5 2.8 gather_fusion.1
  14.2 2.5 collective-permute-start
  16.7 3.3 collective-permute-start.4
  24.8 2.0 collective-permute-done.1
  27.1 3.1 collective-permute-start.2
  30.1 2.8 collective-permute-start.6
  38.0 3.6 collective-permute-start.3
  42.9 24.8 %make_tiles.1 = (bf16[64,2,256,256]{3,2,1,0:T(8,128)(2,1)}, bf16[64,2,256,256]{3,2,1,0:T(8,128)(2,1)}) custom-call(s32[64]{0:T(128)S(1)} %get-tuple-element.93.row_at, s32[64]{0:T(128)S(1)} %get-tuple-element.94.col_at, f32[16,8,1024]{2,1,0:T(8,128)S(1)} %constant_dynamic-update-slice_fusion.row_points, f32[8,8,1024]{2,1,0:T(8,128)S(1)} %get-tuple-element.79.col_points, ...), custom_call_target="tpu_custom_call" | custom-call | flops 125829120 | bytes 33554432 | tf_op jit(solution)/shard_map/make_tiles/pallas_call | solution.py:137
  67.7 4.3 gram_sums.1
  73.2 16.8 %kernel_products.2 = (f32[8,64,1024]{2,1,0:T(8,128)}, f32[8,64,1024]{2,1,0:T(8,128)}, f32[2,64,1024]{2,1,0:T(8,128)}, f32[2,64,1024]{2,1,0:T(8,128)}, f32[2,64,1024]{2,1,0:T(8,128)}, /*index=5*/f32[2,64,1024]{2,1,0:T(8,128)}) custom-call(s32[7,64]{1,0:T(8,128)} %stack.24.index, bf16[64,2,256,256]{3,2,1,0:T(8,128)(2,1)} %get-tuple-element.37.tiles, ...), custom_call_target="tpu_custom_call" | custom-call | flops 3221225472 | bytes 29360128 | tf_op jit(solution)/shard_map/kernel_products/pallas_call | solution.py:240
  90.4 16.8 %slope_products.1 = (f32[64,8192]{1,0:T(8,128)}, f32[64,8192]{1,0:T(8,128)}, f32[64,8192]{1,0:T(8,128)}) custom-call(s32[7,64]{1,0:T(8,128)} %stack.22.index, bf16[64,2,256,256]{3,2,1,0:T(8,128)(2,1)} %get-tuple-element.59.tiles, f32[64,16384]{1,0:T(8,128)} %all-gather.2.cloned.1.call-done.refs_0_, f32[2,64,1024]{2,1,0:T(8,128)} %copy-done.9, ...), custom_call_target="tpu_custom_call" | custom-call | flops 3221225472 | bytes 29360128 | tf_op jit(solution)/shard_map/slope_products/pallas_call | solution.py:240
  107.3 2.2 collective-permute-start.11
  109.8 2.4 collective-permute-start.13
  113.2 1.7 slice_add_fusion.6
  114.9 1.9 collective-permute-start.15
  116.8 7.1 %collective-permute-done.11 = f32[2,64,1024]{2,1,0:T(8,128)S(1)} collective-permute-done((f32[2,64,1024]{2,1,0:T(8,128)}, f32[2,64,1024]{2,1,0:T(8,128)S(1)}, u32[]{:S(2)}, u32[]{:S(2)}) %collective-permute-start.11) | collective-permute-done | bytes 524320 | tf_op jit(solution)/shard_map/ppermute | solution.py:27
  124.0 16.3 %collective-permute-done.12 = f32[2,64,1024]{2,1,0:T(8,128)S(1)} collective-permute-done((f32[2,64,1024]{2,1,0:T(8,128)S(1)}, f32[2,64,1024]{2,1,0:T(8,128)S(1)}, u32[]{:S(2)}, u32[]{:S(2)}) %collective-permute-start.12) | collective-permute-done | bytes 524320 | tf_op jit(solution)/shard_map/ppermute | solution.py:27
  140.3 3.4 collective-permute-start.17
  144.9 9.6 %collective-permute-done.17 = f32[2,64,1024]{2,1,0:T(8,128)S(1)} collective-permute-done((f32[2,64,1024]{2,1,0:T(8,128)S(1)}, f32[2,64,1024]{2,1,0:T(8,128)S(1)}, u32[]{:S(2)}, u32[]{:S(2)}) %collective-permute-start.17) | collective-permute-done | bytes 524320 | tf_op jit(solution)/shard_map/ppermute | solution.py:23
  154.5 1.5 fusion.5.refs_1_
  156.1 4.5 gather_fusion
  160.7 4.2 collective-permute-done.19.refs_3_
  164.9 2.2 copy-done.3
  168.2 1.4 collective-permute-start.20
  170.4 2.5 collective-permute-done.21
  173.0 2.5 collective-permute-done.22
  175.5 1.7 collective-permute-start.23
  177.2 2.8 collective-permute-done.23
  181.4 2.7 collective-permute-done.24
  184.0 3.2 collective-permute-done.25
  187.8 3.5 collective-permute-done.26
  192.4 2.0 collective-permute-start.35
  194.4 3.2 collective-permute-done.27
  197.6 3.3 collective-permute-done.35
  201.8 2.5 collective-permute-start.29
  204.9 8.2 %collective-permute-start.31 = (f32[2,64,1024]{2,1,0:T(8,128)S(1)}, f32[2,64,1024]{2,1,0:T(8,128)S(1)}, u32[]{:S(2)}, u32[]{:S(2)}) collective-permute-start(f32[2,64,1024]{2,1,0:T(8,128)S(1)} %get-tuple-element.78.refs_0_), channel_id=1, source_target_pairs={{0,1},{1,0},{2,3},{3,2},{4,5},{5,4},{6,7},{7,6},{8,9},{9,8},{10,11... | collective-permute-start | bytes 1572872 | tf_op jit(solution)/shard_map/ppermute | solution.py:31
  214.1 5.5 %collective-permute-done.29.refs_2_ = f32[2,64,1024]{2,1,0:T(8,128)S(1)} collective-permute-done((f32[2,64,1024]{2,1,0:T(8,128)S(1)}, f32[2,64,1024]{2,1,0:T(8,128)S(1)}, u32[]{:S(2)}, u32[]{:S(2)}) %collective-permute-start.29) | collective-permute-done | bytes 524320 | tf_op jit(solution)/shard_map/ppermute | solution.py:23
  220.1 4.1 collective-permute-done.30.refs_3_
  224.1 4.5 collective-permute-start.32
  228.8 10.2 %collective-permute-done.36.refs_9_ = f32[2,64,1024]{2,1,0:T(8,128)S(1)} collective-permute-done((f32[2,64,1024]{2,1,0:T(8,128)S(1)}, f32[2,64,1024]{2,1,0:T(8,128)S(1)}, u32[]{:S(2)}, u32[]{:S(2)}) %collective-permute-start.36) | collective-permute-done | bytes 524320 | tf_op jit(solution)/shard_map/ppermute | solution.py:27
  239.8 3.1 add.432
  243.1 16.8 %kernel_products.3 = (f32[8,64,1024]{2,1,0:T(8,128)}, f32[8,64,1024]{2,1,0:T(8,128)}, f32[2,64,1024]{2,1,0:T(8,128)}, f32[2,64,1024]{2,1,0:T(8,128)}, f32[2,64,1024]{2,1,0:T(8,128)}, /*index=5*/f32[2,64,1024]{2,1,0:T(8,128)}) custom-call(s32[7,64]{1,0:T(8,128)} %stack.23.index, bf16[64,2,256,256]{3,2,1,0:T(8,128)(2,1)} %get-tuple-element.37.tiles, ...), custom_call_target="tpu_custom_call" | custom-call | flops 3221225472 | bytes 29360128 | tf_op jit(solution)/shard_map/kernel_products/pallas_call | solution.py:240
  260.8 2.7 collective-permute-start.41
  264.8 1.7 slice_add_fusion.2
  266.5 1.6 collective-permute-start.43
  268.1 7.7 %collective-permute-done.39 = f32[2,64,1024]{2,1,0:T(8,128)S(1)} collective-permute-done((f32[2,64,1024]{2,1,0:T(8,128)}, f32[2,64,1024]{2,1,0:T(8,128)S(1)}, u32[]{:S(2)}, u32[]{:S(2)}) %collective-permute-start.39) | collective-permute-done | bytes 524320 | tf_op jit(solution)/shard_map/ppermute | solution.py:27
  275.9 11.1 %collective-permute-done.40 = f32[2,64,1024]{2,1,0:T(8,128)S(1)} collective-permute-done((f32[2,64,1024]{2,1,0:T(8,128)}, f32[2,64,1024]{2,1,0:T(8,128)S(1)}, u32[]{:S(2)}, u32[]{:S(2)}) %collective-permute-start.40) | collective-permute-done | bytes 524320 | tf_op jit(solution)/shard_map/ppermute | solution.py:27
  287.3 1.9 collective-permute-start.46
  289.2 4.1 collective-permute-done.44
  293.2 8.2 %collective-permute-done.45 = f32[2,64,1024]{2,1,0:T(8,128)S(1)} collective-permute-done((f32[2,64,1024]{2,1,0:T(8,128)S(1)}, f32[2,64,1024]{2,1,0:T(8,128)S(1)}, u32[]{:S(2)}, u32[]{:S(2)}) %collective-permute-start.45) | collective-permute-done | bytes 524320 | tf_op jit(solution)/shard_map/ppermute | solution.py:23
  302.8 2.2 collective-permute-start.47
  304.9 6.1 %collective-permute-done.47.refs_3_ = f32[64,1024]{1,0:T(8,128)S(1)} collective-permute-done((f32[64,1024]{1,0:T(8,128)S(1)}, f32[64,1024]{1,0:T(8,128)S(1)}, u32[]{:S(2)}, u32[]{:S(2)}) %collective-permute-start.47) | collective-permute-done | bytes 262176 | tf_op jit(solution)/shard_map/ppermute | solution.py:35
  314.2 1.5 collective-permute-start.49
  316.7 2.4 collective-permute-start.50
  320.2 1.4 collective-permute-start.51
  321.7 2.6 collective-permute-done.51
  324.3 1.8 collective-permute-start.52
  326.0 2.3 collective-permute-done.52
  328.3 2.5 collective-permute-done.53
  331.5 1.8 add.433
  333.2 1.7 collective-permute-done.54
  334.9 126.9 %all-reduce.2.cloned.1.call-done.gram = f32[160,128]{1,0:T(8,128)} async-done(((f32[160,128]{1,0:T(8,128)}), f32[160,128]{1,0:T(8,128)}) %all-reduce.2.cloned.1.call-update) | async-done | bytes 81936 | tf_op jit(solution)/shard_map/psum | solution.py:508
  461.9 2.2 copy-done.6
  464.9 1.8 shard_map.104
  (178 shorter events, 38.7 us)
Async XLA Ops:
  8.0 148.1 %copy-start = (f32[1024]{0:T(1024)S(1)}, f32[1024]{0:T(1024)}, u32[]{:S(2)}) copy-start(f32[1024]{0:T(1024)} %param.10) | copy-start | bytes 12292
  8.0 64.1 %all-gather.2.cloned.1.call-start = ((), (), s32[]{:S(2)}) async-start(), calls=%async_computation.2 | async-start | bytes 4456448 | tf_op jit(solution)/shard_map/all_gather | solution.py:502
  8.8 322.7 %reduce-scatter.5.cloned.1.call-start = ((), (), s32[]{:S(2)}) async-start(), calls=%async_computation.5 | async-start | bytes 2359296 | tf_op jit(solution)/shard_map/reduce_scatter | solution.py:515
  14.2 7.9 %collective-permute-start = (f32[1,8,1024]{2,1,0:T(8,128)S(1)}, f32[1,8,1024]{2,1,0:T(8,128)S(1)}, u32[]{:S(2)}, u32[]{:S(2)}) collective-permute-start(f32[1,8,1024]{2,1,0:T(8,128)S(1)} %get-tuple-element.70), channel_id=1, source_target_pairs={{0,2},{1,3},{2,0},{3,1},{4,6},{5,7},{6,4},{7,5},{8,10},{9,11},{10,... | collective-permute-start | bytes 98312 | tf_op jit(solution)/shard_map/ppermute | solution.py:52
  16.7 5.4 %collective-permute-start.4 = (f32[1,8,1024]{2,1,0:T(8,128)S(1)}, f32[1,8,1024]{2,1,0:T(8,128)S(1)}, u32[]{:S(2)}, u32[]{:S(2)}) collective-permute-start(f32[1,8,1024]{2,1,0:T(8,128)S(1)} %get-tuple-element.70), channel_id=1, source_target_pairs={{0,16},{16,0},{32,48},{48,32},{64,80},{80,64},{96,112},{112,96},{1... | collective-permute-start | bytes 98312 | tf_op jit(solution)/shard_map/ppermute | solution.py:55
  20.0 14.8 %collective-permute-start.7 = (f32[64,1024]{1,0:T(8,128)}, f32[64,1024]{1,0:T(8,128)S(1)}, u32[]{:S(2)}, u32[]{:S(2)}) collective-permute-start(f32[64,1024]{1,0:T(8,128)} %first.4), channel_id=1, source_target_pairs={{0,16},{16,0},{32,48},{48,32},{64,80},{80,64},{96,112},{112,96},{1... | collective-permute-start | bytes 786440 | tf_op jit(solution)/shard_map/ppermute | solution.py:39
  22.2 4.6 collective-permute-start.1
  23.5 3.5 collective-permute-start.5
  27.1 10.0 %collective-permute-start.2 = (f32[4,8,1024]{2,1,0:T(8,128)S(1)}, f32[4,8,1024]{2,1,0:T(8,128)S(1)}, u32[]{:S(2)}, u32[]{:S(2)}) collective-permute-start(f32[4,8,1024]{2,1,0:T(8,128)S(1)} %get-tuple-element.82), channel_id=1, source_target_pairs={{0,8},{1,9},{2,10},{3,11},{4,12},{5,13},{6,14},{7,15},{8,0},{9,1},... | collective-permute-start | bytes 393224 | tf_op jit(solution)/shard_map/ppermute | solution.py:52
  30.1 6.9 %collective-permute-start.6 = (f32[4,8,1024]{2,1,0:T(8,128)S(1)}, f32[4,8,1024]{2,1,0:T(8,128)}, u32[]{:S(2)}, u32[]{:S(2)}) collective-permute-start(f32[4,8,1024]{2,1,0:T(8,128)S(1)} %get-tuple-element.81), channel_id=1, source_target_pairs={{0,64},{16,80},{32,96},{48,112},{64,0},{80,16},{96,32},{112,48},{1... | collective-permute-start | bytes 393224 | tf_op jit(solution)/shard_map/ppermute | solution.py:55
  34.9 37.2 %collective-permute-start.10 = (f32[2,64,1024]{2,1,0:T(8,128)S(1)}, f32[2,64,1024]{2,1,0:T(8,128)S(1)}, u32[]{:S(2)}, u32[]{:S(2)}) collective-permute-start(f32[2,64,1024]{2,1,0:T(8,128)S(1)} %pad_maximum_fusion.2.refs_1_), channel_id=1, source_target_pairs={{0,96},{16,112},{32,0},{48,16},{64,32},{80,48},{96,64},{112,80},{1... | collective-permute-start | bytes 1572872 | tf_op jit(solution)/shard_map/ppermute | solution.py:27
  35.8 36.2 %collective-permute-start.8 = (f32[2,64,1024]{2,1,0:T(8,128)S(1)}, f32[2,64,1024]{2,1,0:T(8,128)S(1)}, u32[]{:S(2)}, u32[]{:S(2)}) collective-permute-start(f32[2,64,1024]{2,1,0:T(8,128)S(1)} %pad_maximum_fusion.2.refs_1_), channel_id=1, source_target_pairs={{0,32},{16,48},{32,64},{48,80},{64,96},{80,112},{96,0},{112,16},{1... | collective-permute-start | bytes 1572872 | tf_op jit(solution)/shard_map/ppermute | solution.py:27
  36.4 35.6 %collective-permute-start.9 = (f32[2,64,1024]{2,1,0:T(8,128)S(1)}, f32[2,64,1024]{2,1,0:T(8,128)S(1)}, u32[]{:S(2)}, u32[]{:S(2)}) collective-permute-start(f32[2,64,1024]{2,1,0:T(8,128)S(1)} %pad_maximum_fusion.2.refs_1_), channel_id=1, source_target_pairs={{0,64},{16,80},{32,96},{48,112},{64,0},{80,16},{96,32},{112,48},{1... | collective-permute-start | bytes 1572872 | tf_op jit(solution)/shard_map/ppermute | solution.py:27
  38.0 4.8 %collective-permute-start.3 = (f32[8,8,1024]{2,1,0:T(8,128)S(1)}, f32[8,8,1024]{2,1,0:T(8,128)S(1)}, u32[]{:S(2)}, u32[]{:S(2)}) collective-permute-start(f32[8,8,1024]{2,1,0:T(8,128)S(1)} %get-tuple-element.80), channel_id=1, source_target_pairs={{0,1},{1,0},{2,3},{3,2},{4,5},{5,4},{6,7},{7,6},{8,9},{9,8},{10,11... | collective-permute-start | bytes 786440 | tf_op jit(solution)/shard_map/ppermute | solution.py:52
  90.0 23.2 %collective-permute-start.14 = (f32[8,64,1024]{2,1,0:T(8,128)}, f32[8,64,1024]{2,1,0:T(8,128)}, u32[]{:S(2)}, u32[]{:S(2)}) collective-permute-start(f32[8,64,1024]{2,1,0:T(8,128)} %get-tuple-element.43), channel_id=1, source_target_pairs={{0,1},{1,0},{2,3},{3,2},{4,5},{5,4},{6,7},{7,6},{8,9},{9,8},{10,11... | collective-permute-start | bytes 6291464 | tf_op jit(solution)/shard_map/ppermute | solution.py:31
  107.3 224.2 %reduce-scatter.3.cloned.1.call-start = ((), (), s32[]{:S(2)}) async-start(), calls=%async_computation.4 | async-start | bytes 2359296 | tf_op jit(solution)/shard_map/reduce_scatter | solution.py:517
  107.3 16.6 %collective-permute-start.11 = (f32[2,64,1024]{2,1,0:T(8,128)}, f32[2,64,1024]{2,1,0:T(8,128)S(1)}, u32[]{:S(2)}, u32[]{:S(2)}) collective-permute-start(f32[2,64,1024]{2,1,0:T(8,128)} %get-tuple-element.39), channel_id=1, source_target_pairs={{0,64},{16,80},{32,96},{48,112},{64,0},{80,16},{96,32},{112,48},{1... | collective-permute-start | bytes 1572872 | tf_op jit(solution)/shard_map/ppermute | solution.py:27
  109.5 30.8 %collective-permute-start.12 = (f32[2,64,1024]{2,1,0:T(8,128)S(1)}, f32[2,64,1024]{2,1,0:T(8,128)S(1)}, u32[]{:S(2)}, u32[]{:S(2)}) collective-permute-start(f32[2,64,1024]{2,1,0:T(8,128)S(1)} %copy-done.27), channel_id=1, source_target_pairs={{0,32},{16,48},{32,64},{48,80},{64,96},{80,112},{96,0},{112,16},{1... | collective-permute-start | bytes 1572872 | tf_op jit(solution)/shard_map/ppermute | solution.py:27
  109.8 33.9 %collective-permute-start.13 = (f32[2,64,1024]{2,1,0:T(8,128)S(1)}, f32[2,64,1024]{2,1,0:T(8,128)S(1)}, u32[]{:S(2)}, u32[]{:S(2)}) collective-permute-start(f32[2,64,1024]{2,1,0:T(8,128)S(1)} %copy-done.26), channel_id=1, source_target_pairs={{0,96},{16,112},{32,0},{48,16},{64,32},{80,48},{96,64},{112,80},{1... | collective-permute-start | bytes 1572872 | tf_op jit(solution)/shard_map/ppermute | solution.py:27
  112.2 100.8 %collective-permute-start.55 = (f32[64,8192]{1,0:T(8,128)}, f32[64,8192]{1,0:T(8,128)}, u32[]{:S(2)}, u32[]{:S(2)}) collective-permute-start(f32[64,8192]{1,0:T(8,128)} %get-tuple-element.61), channel_id=1, source_target_pairs={{0,1},{1,0},{2,3},{3,2},{4,5},{5,4},{6,7},{7,6},{8,9},{9,8},{10,11... | collective-permute-start | bytes 6291464 | tf_op jit(solution)/shard_map/ppermute | solution.py:31
  114.9 30.0 %collective-permute-start.15 = (f32[2,64,1024]{2,1,0:T(8,128)S(1)}, f32[2,64,1024]{2,1,0:T(8,128)S(1)}, u32[]{:S(2)}, u32[]{:S(2)}) collective-permute-start(f32[2,64,1024]{2,1,0:T(8,128)S(1)} %get-tuple-element.74), channel_id=1, source_target_pairs={{0,8},{1,9},{2,10},{3,11},{4,12},{5,13},{6,14},{7,15},{8,0},{9,1},... | collective-permute-start | bytes 1572872 | tf_op jit(solution)/shard_map/ppermute | solution.py:23
  123.9 21.0 %collective-permute-start.16 = (f32[2,64,1024]{2,1,0:T(8,128)S(1)}, f32[2,64,1024]{2,1,0:T(8,128)S(1)}, u32[]{:S(2)}, u32[]{:S(2)}) collective-permute-start(f32[2,64,1024]{2,1,0:T(8,128)S(1)} %get-tuple-element.76), channel_id=1, source_target_pairs={{0,4},{1,5},{2,6},{3,7},{4,8},{5,9},{6,10},{7,11},{8,12},{9,13},{1... | collective-permute-start | bytes 1572872 | tf_op jit(solution)/shard_map/ppermute | solution.py:23
  140.3 14.2 %collective-permute-start.17 = (f32[2,64,1024]{2,1,0:T(8,128)S(1)}, f32[2,64,1024]{2,1,0:T(8,128)S(1)}, u32[]{:S(2)}, u32[]{:S(2)}) collective-permute-start(f32[2,64,1024]{2,1,0:T(8,128)S(1)} %get-tuple-element.75), channel_id=1, source_target_pairs={{0,12},{1,13},{2,14},{3,15},{4,0},{5,1},{6,2},{7,3},{8,4},{9,5},{1... | collective-permute-start | bytes 1572872 | tf_op jit(solution)/shard_map/ppermute | solution.py:23
  143.9 16.8 %collective-permute-start.18 = (f32[64,1024]{1,0:T(8,128)S(1)}, f32[64,1024]{1,0:T(8,128)S(1)}, u32[]{:S(2)}, u32[]{:S(2)}) collective-permute-start(f32[64,1024]{1,0:T(8,128)S(1)} %slice_bitcast_fusion.3), channel_id=1, source_target_pairs={{0,16},{16,0},{32,48},{48,32},{64,80},{80,64},{96,112},{112,96},{1... | collective-permute-start | bytes 786440 | tf_op jit(solution)/shard_map/ppermute | solution.py:39
  156.0 8.9 %collective-permute-start.19 = (f32[64,1024]{1,0:T(8,128)S(1)}, f32[64,1024]{1,0:T(8,128)S(1)}, u32[]{:S(2)}, u32[]{:S(2)}) collective-permute-start(f32[64,1024]{1,0:T(8,128)S(1)} %slice_bitcast_fusion.2), channel_id=1, source_target_pairs={{0,2},{1,3},{2,0},{3,1},{4,6},{5,7},{6,4},{7,5},{8,10},{9,11},{10,... | collective-permute-start | bytes 786440 | tf_op jit(solution)/shard_map/ppermute | solution.py:35
  168.2 2.3 collective-permute-start.20
  170.4 2.5 collective-permute-start.21
  173.0 2.5 collective-permute-start.22
  175.5 4.5 collective-permute-start.23
  180.0 4.0 collective-permute-start.24
  184.0 3.2 collective-permute-start.25
  187.2 4.1 collective-permute-start.26
  191.3 48.5 %copy-start.10 = (f32[64,8192]{1,0:T(8,128)S(1)}, f32[64,8192]{1,0:T(8,128)}, u32[]{:S(2)}) copy-start(f32[64,8192]{1,0:T(8,128)} %get-tuple-element.60) | copy-start | bytes 6291460
  192.3 5.3 %collective-permute-start.27 = (f32[64,1024]{1,0:T(8,128)S(1)}, f32[64,1024]{1,0:T(8,128)S(1)}, u32[]{:S(2)}, u32[]{:S(2)}) collective-permute-start(f32[64,1024]{1,0:T(8,128)S(1)} %shard_map.103.refs_5_.second), channel_id=1, source_target_pairs={{0,2},{1,3},{2,0},{3,1},{4,6},{5,7},{6,4},{7,5},{8,10},{9,11},{10,... | collective-permute-start | bytes 786440 | tf_op jit(solution)/shard_map/ppermute | solution.py:35
  192.4 8.5 %collective-permute-start.35 = (f32[64,1024]{1,0:T(8,128)S(1)}, f32[64,1024]{1,0:T(8,128)S(1)}, u32[]{:S(2)}, u32[]{:S(2)}) collective-permute-start(f32[64,1024]{1,0:T(8,128)S(1)} %shard_map.103.refs_5_.second), channel_id=1, source_target_pairs={{0,16},{16,0},{32,48},{48,32},{64,80},{80,64},{96,112},{112,96},{1... | collective-permute-start | bytes 786440 | tf_op jit(solution)/shard_map/ppermute | solution.py:39
  201.1 41.8 %copy-start.11 = (f32[2,64,1024]{2,1,0:T(8,128)}, f32[2,64,1024]{2,1,0:T(8,128)S(1)}, u32[]{:S(2)}) copy-start(f32[2,64,1024]{2,1,0:T(8,128)S(1)} %get-tuple-element.77.refs_8_) | copy-start | bytes 1572868
  201.1 41.8 %copy-start.12 = (f32[2,64,1024]{2,1,0:T(8,128)}, f32[2,64,1024]{2,1,0:T(8,128)S(1)}, u32[]{:S(2)}) copy-start(f32[2,64,1024]{2,1,0:T(8,128)S(1)} %get-tuple-element.78.refs_0_) | copy-start | bytes 1572868
  201.1 12.1 %collective-permute-start.28 = (f32[2,64,1024]{2,1,0:T(8,128)S(1)}, f32[2,64,1024]{2,1,0:T(8,128)S(1)}, u32[]{:S(2)}, u32[]{:S(2)}) collective-permute-start(f32[2,64,1024]{2,1,0:T(8,128)S(1)} %get-tuple-element.78.refs_0_), channel_id=1, source_target_pairs={{0,4},{1,5},{2,6},{3,7},{4,8},{5,9},{6,10},{7,11},{8,12},{9,13},{1... | collective-permute-start | bytes 1572872 | tf_op jit(solution)/shard_map/ppermute | solution.py:23
  201.8 17.8 %collective-permute-start.29 = (f32[2,64,1024]{2,1,0:T(8,128)S(1)}, f32[2,64,1024]{2,1,0:T(8,128)S(1)}, u32[]{:S(2)}, u32[]{:S(2)}) collective-permute-start(f32[2,64,1024]{2,1,0:T(8,128)S(1)} %get-tuple-element.78.refs_0_), channel_id=1, source_target_pairs={{0,8},{1,9},{2,10},{3,11},{4,12},{5,13},{6,14},{7,15},{8,0},{9,1},... | collective-permute-start | bytes 1572872 | tf_op jit(solution)/shard_map/ppermute | solution.py:23
  204.3 19.8 %collective-permute-start.30 = (f32[2,64,1024]{2,1,0:T(8,128)S(1)}, f32[2,64,1024]{2,1,0:T(8,128)S(1)}, u32[]{:S(2)}, u32[]{:S(2)}) collective-permute-start(f32[2,64,1024]{2,1,0:T(8,128)S(1)} %get-tuple-element.78.refs_0_), channel_id=1, source_target_pairs={{0,12},{1,13},{2,14},{3,15},{4,0},{5,1},{6,2},{7,3},{8,4},{9,5},{1... | collective-permute-start | bytes 1572872 | tf_op jit(solution)/shard_map/ppermute | solution.py:23
  204.9 23.8 %collective-permute-start.31 = (f32[2,64,1024]{2,1,0:T(8,128)S(1)}, f32[2,64,1024]{2,1,0:T(8,128)S(1)}, u32[]{:S(2)}, u32[]{:S(2)}) collective-permute-start(f32[2,64,1024]{2,1,0:T(8,128)S(1)} %get-tuple-element.78.refs_0_), channel_id=1, source_target_pairs={{0,1},{1,0},{2,3},{3,2},{4,5},{5,4},{6,7},{7,6},{8,9},{9,8},{10,11... | collective-permute-start | bytes 1572872 | tf_op jit(solution)/shard_map/ppermute | solution.py:31
  213.0 25.9 %collective-permute-start.36 = (f32[2,64,1024]{2,1,0:T(8,128)S(1)}, f32[2,64,1024]{2,1,0:T(8,128)S(1)}, u32[]{:S(2)}, u32[]{:S(2)}) collective-permute-start(f32[2,64,1024]{2,1,0:T(8,128)S(1)} %get-tuple-element.77.refs_8_), channel_id=1, source_target_pairs={{0,32},{16,48},{32,64},{48,80},{64,96},{80,112},{96,0},{112,16},{1... | collective-permute-start | bytes 1572872 | tf_op jit(solution)/shard_map/ppermute | solution.py:27
  213.2 29.9 %collective-permute-start.37 = (f32[2,64,1024]{2,1,0:T(8,128)S(1)}, f32[2,64,1024]{2,1,0:T(8,128)}, u32[]{:S(2)}, u32[]{:S(2)}) collective-permute-start(f32[2,64,1024]{2,1,0:T(8,128)S(1)} %get-tuple-element.77.refs_8_), channel_id=1, source_target_pairs={{0,64},{16,80},{32,96},{48,112},{64,0},{80,16},{96,32},{112,48},{1... | collective-permute-start | bytes 1572872 | tf_op jit(solution)/shard_map/ppermute | solution.py:27
  219.6 23.4 %collective-permute-start.38 = (f32[2,64,1024]{2,1,0:T(8,128)S(1)}, f32[2,64,1024]{2,1,0:T(8,128)}, u32[]{:S(2)}, u32[]{:S(2)}) collective-permute-start(f32[2,64,1024]{2,1,0:T(8,128)S(1)} %get-tuple-element.77.refs_8_), channel_id=1, source_target_pairs={{0,96},{16,112},{32,0},{48,16},{64,32},{80,48},{96,64},{112,80},{1... | collective-permute-start | bytes 1572872 | tf_op jit(solution)/shard_map/ppermute | solution.py:27
  224.1 18.9 %collective-permute-start.32 = (f32[2,64,1024]{2,1,0:T(8,128)S(1)}, f32[2,64,1024]{2,1,0:T(8,128)}, u32[]{:S(2)}, u32[]{:S(2)}) collective-permute-start(f32[2,64,1024]{2,1,0:T(8,128)S(1)} %collective-permute-done.28.refs_1_), channel_id=1, source_target_pairs={{0,1},{1,0},{2,3},{3,2},{4,5},{5,4},{6,7},{7,6},{8,9},{9,8},{10,11... | collective-permute-start | bytes 1572872 | tf_op jit(solution)/shard_map/ppermute | solution.py:31
  228.7 14.4 %collective-permute-start.33 = (f32[2,64,1024]{2,1,0:T(8,128)S(1)}, f32[2,64,1024]{2,1,0:T(8,128)}, u32[]{:S(2)}, u32[]{:S(2)}) collective-permute-start(f32[2,64,1024]{2,1,0:T(8,128)S(1)} %collective-permute-done.29.refs_2_), channel_id=1, source_target_pairs={{0,1},{1,0},{2,3},{3,2},{4,5},{5,4},{6,7},{7,6},{8,9},{9,8},{10,11... | collective-permute-start | bytes 1572872 | tf_op jit(solution)/shard_map/ppermute | solution.py:31
  239.0 4.1 collective-permute-start.34
  243.0 218.9 %all-reduce.2.cloned.1.call-start = ((), (), s32[]{:S(2)}) async-start(), calls=%async_computation.3 | async-start | bytes 163840 | tf_op jit(solution)/shard_map/psum | solution.py:508
  259.9 4.9 %collective-permute-start.42 = (f32[8,64,1024]{2,1,0:T(8,128)}, f32[8,64,1024]{2,1,0:T(8,128)S(1)}, u32[]{:S(2)}, u32[]{:S(2)}) collective-permute-start(f32[8,64,1024]{2,1,0:T(8,128)} %get-tuple-element.52), channel_id=1, source_target_pairs={{0,1},{1,0},{2,3},{3,2},{4,5},{5,4},{6,7},{7,6},{8,9},{9,8},{10,11... | collective-permute-start | bytes 6291464 | tf_op jit(solution)/shard_map/ppermute | solution.py:31
  260.8 15.0 %collective-permute-start.39 = (f32[2,64,1024]{2,1,0:T(8,128)}, f32[2,64,1024]{2,1,0:T(8,128)S(1)}, u32[]{:S(2)}, u32[]{:S(2)}) collective-permute-start(f32[2,64,1024]{2,1,0:T(8,128)} %get-tuple-element.48), channel_id=1, source_target_pairs={{0,64},{16,80},{32,96},{48,112},{64,0},{80,16},{96,32},{112,48},{1... | collective-permute-start | bytes 1572872 | tf_op jit(solution)/shard_map/ppermute | solution.py:27
  260.8 26.3 %collective-permute-start.40 = (f32[2,64,1024]{2,1,0:T(8,128)}, f32[2,64,1024]{2,1,0:T(8,128)S(1)}, u32[]{:S(2)}, u32[]{:S(2)}) collective-permute-start(f32[2,64,1024]{2,1,0:T(8,128)} %get-tuple-element.49), channel_id=1, source_target_pairs={{0,32},{16,48},{32,64},{48,80},{64,96},{80,112},{96,0},{112,16},{1... | collective-permute-start | bytes 1572872 | tf_op jit(solution)/shard_map/ppermute | solution.py:27
  260.8 26.3 %collective-permute-start.41 = (f32[2,64,1024]{2,1,0:T(8,128)}, f32[2,64,1024]{2,1,0:T(8,128)S(1)}, u32[]{:S(2)}, u32[]{:S(2)}) collective-permute-start(f32[2,64,1024]{2,1,0:T(8,128)} %get-tuple-element.50), channel_id=1, source_target_pairs={{0,96},{16,112},{32,0},{48,16},{64,32},{80,48},{96,64},{112,80},{1... | collective-permute-start | bytes 1572872 | tf_op jit(solution)/shard_map/ppermute | solution.py:27
  266.5 22.7 %collective-permute-start.43 = (f32[2,64,1024]{2,1,0:T(8,128)S(1)}, f32[2,64,1024]{2,1,0:T(8,128)S(1)}, u32[]{:S(2)}, u32[]{:S(2)}) collective-permute-start(f32[2,64,1024]{2,1,0:T(8,128)S(1)} %get-tuple-element.71), channel_id=1, source_target_pairs={{0,8},{1,9},{2,10},{3,11},{4,12},{5,13},{6,14},{7,15},{8,0},{9,1},... | collective-permute-start | bytes 1572872 | tf_op jit(solution)/shard_map/ppermute | solution.py:23
  268.1 25.2 %collective-permute-start.44 = (f32[2,64,1024]{2,1,0:T(8,128)S(1)}, f32[2,64,1024]{2,1,0:T(8,128)S(1)}, u32[]{:S(2)}, u32[]{:S(2)}) collective-permute-start(f32[2,64,1024]{2,1,0:T(8,128)S(1)} %get-tuple-element.73), channel_id=1, source_target_pairs={{0,4},{1,5},{2,6},{3,7},{4,8},{5,9},{6,10},{7,11},{8,12},{9,13},{1... | collective-permute-start | bytes 1572872 | tf_op jit(solution)/shard_map/ppermute | solution.py:23
  275.8 25.7 %collective-permute-start.45 = (f32[2,64,1024]{2,1,0:T(8,128)S(1)}, f32[2,64,1024]{2,1,0:T(8,128)S(1)}, u32[]{:S(2)}, u32[]{:S(2)}) collective-permute-start(f32[2,64,1024]{2,1,0:T(8,128)S(1)} %get-tuple-element.72), channel_id=1, source_target_pairs={{0,12},{1,13},{2,14},{3,15},{4,0},{5,1},{6,2},{7,3},{8,4},{9,5},{1... | collective-permute-start | bytes 1572872 | tf_op jit(solution)/shard_map/ppermute | solution.py:23
  287.3 17.7 %collective-permute-start.46 = (f32[64,1024]{1,0:T(8,128)S(1)}, f32[64,1024]{1,0:T(8,128)S(1)}, u32[]{:S(2)}, u32[]{:S(2)}) collective-permute-start(f32[64,1024]{1,0:T(8,128)S(1)} %slice_bitcast_fusion.1), channel_id=1, source_target_pairs={{0,16},{16,0},{32,48},{48,32},{64,80},{80,64},{96,112},{112,96},{1... | collective-permute-start | bytes 786440 | tf_op jit(solution)/shard_map/ppermute | solution.py:39
  302.8 8.3 %collective-permute-start.47 = (f32[64,1024]{1,0:T(8,128)S(1)}, f32[64,1024]{1,0:T(8,128)S(1)}, u32[]{:S(2)}, u32[]{:S(2)}) collective-permute-start(f32[64,1024]{1,0:T(8,128)S(1)} %slice_bitcast_fusion), channel_id=1, source_target_pairs={{0,2},{1,3},{2,0},{3,1},{4,6},{5,7},{6,4},{7,5},{8,10},{9,11},{10,... | collective-permute-start | bytes 786440 | tf_op jit(solution)/shard_map/ppermute | solution.py:35
  312.1 2.1 collective-permute-start.48
  314.2 2.5 collective-permute-start.49
  316.7 3.5 collective-permute-start.50
  320.2 4.0 collective-permute-start.51
  324.3 4.0 collective-permute-start.52
  328.3 2.5 collective-permute-start.53
  330.9 4.0 collective-permute-start.54
  (24 other events, 357.6 us)
Sparse Core Ops, SparseCore 0:
  10.5 43.2 all-gather.1
  107.4 81.2 reduce-scatter.4
  243.1 58.5 reduce-scatter.2
Sparse Core Ops, SparseCore 1:
  321.7 140.1 all-reduce.1
